TPU v7x, 32 devices: a whole 2x2x4 slice. The times are simulated.
32 devices in a mesh: seq: 8 (over z, y), head: 4 (over x, core).
Axes of the slice: x: 2, y: 2, z: 4, core: 2. Of those that a mesh axis runs over, the one named last changes fastest.
Arguments:
- x_in: bfloat16 [4096, 4096], P('seq', 'head'), may hold values from -160 to 160
- gate_in: bfloat16 [4096, 4096], P('seq', 'head'), may hold values from -6 to 6
- bc_in: bfloat16 [4096, 256], P('seq'), may hold values from -2.390625 to 2.390625
- step_in: float32 [4096, 64], P('seq', 'head'), may hold values from 0.005 to 0.05
- decay_code: int32 [2, 4096, 64], P(None, 'seq', 'head'), may hold values from 1 to 16384
- decay_rate: float32 [2, 64], P(None, 'head'), may hold values from 1.4648437e-05 to 0.012
- skip_gain: float32 [2, 64], P(None, 'head'), may hold values from 0.25 to 1.5
- norm_gain: float32 [4096], P('head'), may hold values from 0.1 to 1.9
- w_out: bfloat16 [4096, 4096], P('head', 'seq'), may hold values from -0.09375 to 0.09375
- resid_in: bfloat16 [4096, 4096], P('seq', 'head'), may hold values from -25 to 25
- resid_gain: float32 [4096], replicated, may hold values from 0.1 to 1.9
- w_in_x: bfloat16 [4096, 4096], P('seq', 'head'), may hold values from -1 to 1
- w_in_bc: bfloat16 [4096, 256], P('seq'), may hold values from -0.09375 to 0.09375
- w_in_dt: bfloat16 [4096, 64], P('seq', 'head'), may hold values from -0.09375 to 0.09375
- step_time_bias: float32 [64], P('head'), may hold values from -3 to -1
- conv_x: bfloat16 [4, 4096], P(None, 'head'), may hold values from -3 to 3
- conv_bc: bfloat16 [4, 256], replicated, may hold values from -3 to 3
Outputs:
- resid_out: bfloat16 [4096, 4096], P('seq', 'head')
- mixer_out: bfloat16 [4096, 4096], P('seq', 'head')
All inputs are finite; a program needn't handle non-finite values.
Results may differ from a plain program's by a relative error of at most 0.007.
Values may be sent and summed in bfloat16 or wider, within the bound.
No kernel may reach another device: no remote copies, remote signals or barrier semaphores. Data moves between devices by JAX's collectives and lax.ppermute only.
A program may use at most 128 MiB of HBM per device.

v0:
```python
import functools
import jax
import jax.numpy as jnp
from jax import lax
from jax.experimental import pallas as pl
from jax.experimental.pallas import tpu as pltpu
from jax.sharding import PartitionSpec as P

HEAD_CHANNELS = 64
GROUP = 256
HALO = 16
F32 = jnp.float32
BF16 = jnp.bfloat16


def z_shift(value, by):
    n = lax.axis_size("seq")
    pairs = [(i, i + 2 * by) for i in range(n) if 0 <= i + 2 * by < n]
    return lax.ppermute(value, "seq", pairs)


def flip(value, axis, bit):
    n = lax.axis_size(axis)
    return lax.ppermute(value, axis, [(i, i ^ bit) for i in range(n)])


def y_swap(value):
    return flip(value, "seq", 1)


def x_swap(value):
    return flip(value, "head", 2)


def c_swap(value):
    return flip(value, "head", 1)


def z_line(value):
    ups, downs = [value], [value]
    for _ in range(1, 4):
        ups.append(z_shift(ups[-1], 1))
        downs.append(z_shift(downs[-1], -1))
    return downs[:0:-1] + ups


def z_whole(value):
    size = lax.axis_size("seq") // 2
    groups = [[2 * i + y for i in range(size)] for y in range(2)]
    return lax.all_gather(value, "seq", axis_index_groups=groups)


HIGHEST = lax.Precision.HIGHEST
LOW = -1e30


def spread(heads):
    channels = heads * HEAD_CHANNELS
    row = lax.broadcasted_iota(jnp.int32, (heads, channels), 0)
    column = lax.broadcasted_iota(jnp.int32, (heads, channels), 1)
    return (column // HEAD_CHANNELS == row).astype(F32)


def exact_dot(a, b):
    return jnp.dot(a, b, precision=HIGHEST, preferred_element_type=F32)


def running_decay(code, rate):
    decay = -jnp.minimum(code.astype(F32) * rate, 20.0)
    rows = code.shape[0]
    lower = (
        lax.broadcasted_iota(jnp.int32, (rows, rows), 0)
        >= lax.broadcasted_iota(jnp.int32, (rows, rows), 1)
    ).astype(F32)
    return exact_dot(lower, decay)


def state_kernel(x_ref, b_ref, step_ref, code_ref, rate_ref, first_ref, end_ref, payload_ref):
    tokens, channels = x_ref.shape
    heads = channels // HEAD_CHANNELS
    table = spread(heads)
    end = None
    decay = jnp.zeros((1, heads), F32)
    for start in range(0, tokens, GROUP):
        rows = pl.ds(start, GROUP)
        total = running_decay(code_ref[rows, :], rate_ref[...])
        last = total[GROUP - 1 :, :]
        weight = exact_dot(jnp.exp(last - total) * step_ref[rows, :], table)
        v = (x_ref[rows, :].astype(F32) * weight).astype(BF16)
        term = lax.dot_general(
            b_ref[rows, :], v, (((0,), (0,)), ((), ())), preferred_element_type=F32
        )
        if end is None:
            first_ref[...] = term
            end = term
        else:
            end = end * exact_dot(jnp.exp(last), table) + term
        decay = decay + last
    end_ref[...] = end
    put_payload(payload_ref, end, exact_dot(decay, table))


def put_payload(payload_ref, state, wide):
    width, channels = state.shape
    payload_ref[:width, :] = state.astype(BF16)
    high = wide.astype(BF16)
    rest = wide - high.astype(F32)
    middle = rest.astype(BF16)
    low = rest - middle.astype(F32)
    row = lax.broadcasted_iota(jnp.int32, (16, channels), 0)
    tail = jnp.where(
        row == 0,
        high.astype(F32),
        jnp.where(row == 1, middle.astype(F32), jnp.where(row == 2, low, 0.0)),
    )
    payload_ref[width:, :] = tail.astype(BF16)


def get_payload(payload_ref):
    width = payload_ref.shape[0] - 16
    tail = payload_ref[width:, :].astype(F32)
    return payload_ref[:width, :].astype(F32), tail[0:1] + tail[1:2] + tail[2:3]


def pair_kernel(
    y_ref, end_ref, own_ref, far_ref, window_ref, payload_ref, early_ref, early_decay_ref
):
    first = y_ref[0] == 0
    own, own_decay = end_ref[...], get_payload(own_ref)[1]
    far, far_decay = get_payload(far_ref)
    early, early_decay = jnp.where(first, own, far), jnp.where(first, own_decay, far_decay)
    late, late_decay = jnp.where(first, far, own), jnp.where(first, far_decay, own_decay)
    window = jnp.exp(late_decay) * early + late
    window_ref[...] = window
    put_payload(payload_ref, window, early_decay + late_decay)
    early_ref[...] = early
    early_decay_ref[...] = early_decay


def step_kernel(
    window_ref, own_ref, far_ref, before_ref, decay_ref, *outs
):
    window_out, payload_ref, before_out, decay_out = outs
    far, far_decay = get_payload(far_ref)
    own_decay = get_payload(own_ref)[1]
    window = jnp.exp(own_decay) * far + window_ref[...]
    window_out[...] = window
    put_payload(payload_ref, window, own_decay + far_decay)
    before_out[...] = before_ref[...] + jnp.exp(decay_ref[...]) * far
    decay_out[...] = decay_ref[...] + far_decay


def start_kernel(window_ref, own_ref, far_ref, *outs):
    window_out, payload_ref, before_out, decay_out = outs
    far, far_decay = get_payload(far_ref)
    own_decay = get_payload(own_ref)[1]
    window = jnp.exp(own_decay) * far + window_ref[...]
    window_out[...] = window
    put_payload(payload_ref, window, own_decay + far_decay)
    before_out[...] = far
    decay_out[...] = far_decay


def entering(y_ref, early_ref, early_decay_ref, before_ref, decay_ref, far_ref):
    far, _ = get_payload(far_ref)
    before = before_ref[...] + jnp.exp(decay_ref[...]) * far
    late = jnp.exp(early_decay_ref[...]) * before + early_ref[...]
    return jnp.where(y_ref[0] == 0, before, late)


def within_kernel(x_ref, bc_ref, step_ref, code_ref, rate_ref, skip_ref, out_ref):
    rows, channels = x_ref.shape
    heads = channels // HEAD_CHANNELS
    width = bc_ref.shape[1] // 2
    half = rows // 2
    total = running_decay(code_ref[...], rate_ref[...])
    across = total.T
    step = step_ref[...].T
    scores = lax.dot_general(
        bc_ref[:, width:],
        bc_ref[:, :width],
        (((1,), (1,)), ((), ())),
        preferred_element_type=F32,
    )
    skip = exact_dot(skip_ref[...], spread(heads))
    keep = lax.broadcasted_iota(jnp.int32, (half, half), 0) >= lax.broadcasted_iota(
        jnp.int32, (half, half), 1
    )
    lane = lax.broadcasted_iota(jnp.int32, (rows, 2 * HEAD_CHANNELS), 1)
    for pair in range(heads // 2):
        columns = pl.ds(pair * 2 * HEAD_CHANNELS, 2 * HEAD_CHANNELS)
        u = x_ref[:, columns]
        halves = []
        for h in (2 * pair, 2 * pair + 1):
            column = total[:, h : h + 1]
            line = across[h : h + 1, :]
            weight = step[h : h + 1, :]
            top = jnp.exp(jnp.where(keep, column[:half] - line[:, :half], LOW))
            top = (top * scores[:half, :half] * weight[:, :half]).astype(BF16)
            left = jnp.exp(column[half:] - line[:, :half])
            left = (left * scores[half:, :half] * weight[:, :half]).astype(BF16)
            right = jnp.exp(jnp.where(keep, column[half:] - line[:, half:], LOW))
            right = (right * scores[half:, half:] * weight[:, half:]).astype(BF16)
            upper = jnp.dot(top, u[:half], preferred_element_type=F32)
            lower = jnp.dot(
                jnp.concatenate([left, right], axis=1), u, preferred_element_type=F32
            )
            halves.append(jnp.concatenate([upper, lower], axis=0))
        mixed = jnp.where(lane < HEAD_CHANNELS, halves[0], halves[1])
        out_ref[:, columns] = mixed + skip[:, pair * 128 : pair * 128 + 128] * u.astype(F32)


def finish_group(start, state, within_ref, c_ref, code_ref, rate_ref, table):
    rows = pl.ds(start, GROUP)
    total = running_decay(code_ref[rows, :], rate_ref[...])
    c = c_ref[rows, :]
    high = state.astype(BF16)
    low = (state - high.astype(F32)).astype(BF16)
    carried = jnp.dot(
        jnp.concatenate([c, c], axis=1),
        jnp.concatenate([high, low], axis=0),
        preferred_element_type=F32,
    )
    mixed = within_ref[rows, :] + carried * exact_dot(jnp.exp(total), table)
    return mixed, exact_dot(jnp.exp(total[GROUP - 1 :, :]), table)


def gated_kernel(
    y_ref,
    early_ref,
    early_decay_ref,
    before_ref,
    decay_ref,
    far_ref,
    first_ref,
    within_ref,
    c_ref,
    code_ref,
    rate_ref,
    gate_ref,
    gain_ref,
    out_ref,
    square_ref,
):
    tokens, channels = within_ref.shape
    table = spread(channels // HEAD_CHANNELS)
    state = entering(y_ref, early_ref, early_decay_ref, before_ref, decay_ref, far_ref)
    for start in range(0, tokens, GROUP):
        mixed, decay = finish_group(start, state, within_ref, c_ref, code_ref, rate_ref, table)
        state = state * decay + first_ref[...]
        gate = gate_ref[pl.ds(start, GROUP), :].astype(F32)
        gated = mixed * (gate / (1.0 + jnp.exp(-gate)))
        out_ref[pl.ds(start, GROUP), :] = (gated * gain_ref[...]).astype(BF16)
        square_ref[:, pl.ds(start, GROUP)] = jnp.sum(gated * gated, axis=1, keepdims=True).T


def last_kernel(
    y_ref,
    early_ref,
    early_decay_ref,
    before_ref,
    decay_ref,
    far_ref,
    first_ref,
    within_ref,
    c_ref,
    code_ref,
    rate_ref,
    out_ref,
    square_ref,
):
    tokens, channels = within_ref.shape
    table = spread(channels // HEAD_CHANNELS)
    state = entering(y_ref, early_ref, early_decay_ref, before_ref, decay_ref, far_ref)
    for start in range(0, tokens, GROUP):
        mixed, decay = finish_group(start, state, within_ref, c_ref, code_ref, rate_ref, table)
        state = state * decay + first_ref[...]
        out_ref[pl.ds(start, GROUP), :] = mixed
        square_ref[:, pl.ds(start, GROUP)] = jnp.sum(mixed * mixed, axis=1, keepdims=True).T


VMEM_SPEC = pl.BlockSpec(memory_space=pltpu.VMEM)
SMEM_SPEC = pl.BlockSpec(memory_space=pltpu.SMEM)
ANY_SPEC = pl.BlockSpec(memory_space=pl.ANY)


def whole_call(kernel, outs, flops, *args):
    moved = sum(a.size * a.dtype.itemsize for a in args)
    moved += sum(o.size * o.dtype.itemsize for o in outs)
    return pl.pallas_call(
        kernel,
        out_shape=outs,
        in_specs=[SMEM_SPEC if a.shape == (1,) else VMEM_SPEC for a in args],
        out_specs=[VMEM_SPEC] * len(outs),
        cost_estimate=pl.CostEstimate(flops=flops, bytes_accessed=moved, transcendentals=0),
        compiler_params=pltpu.CompilerParams(vmem_limit_bytes=48 * 2**20),
    )(*args)


def shape(dims, kind):
    return jax.ShapeDtypeStruct(dims, kind)


def chunk_states(x, b, step, code, rate):
    width, channels = b.shape[1], x.shape[1]
    return whole_call(
        state_kernel,
        [
            shape((width, channels), F32),
            shape((width, channels), F32),
            shape((width + 16, channels), BF16),
        ],
        4 * x.size * width,
        x,
        b,
        step,
        code,
        rate,
    )


def within_blocks(x, bc, step, code, rate, skip):
    tokens, channels = x.shape
    heads = step.shape[1]
    row = lambda cols: pl.BlockSpec((GROUP, cols), lambda i: (i, 0))
    one = pl.BlockSpec((1, heads), lambda i: (0, 0))
    return pl.pallas_call(
        within_kernel,
        name="within",
        grid=(tokens // GROUP,),
        out_shape=shape((tokens, channels), F32),
        in_specs=[row(channels), row(bc.shape[1]), row(heads), row(heads), one, one],
        out_specs=row(channels),
        cost_estimate=pl.CostEstimate(
            flops=16 * x.size * GROUP, bytes_accessed=8 * x.size, transcendentals=0
        ),
        compiler_params=pltpu.CompilerParams(vmem_limit_bytes=32 * 2**20),
    )(x, bc, step, code, rate, skip)


def conv_kernel(mine_ref, far_ref, scale_ref, taps_ref, bias_ref, x_ref, bc_ref, step_ref, pre_ref):
    rows = mine_ref.shape[0]
    tokens, width = x_ref.shape
    share = bc_ref.shape[1]
    scale = scale_ref[...]
    count = taps_ref.shape[0]

    def convolved(start, size):
        columns = pl.ds(start, size)
        pre = (mine_ref[:, columns] + far_ref[:, columns].astype(F32)) * scale
        pre_ref[:, :size] = pre.astype(BF16).astype(F32)
        total = None
        for tap in range(count):
            first = rows - tokens - count + 1 + tap
            part = pre_ref[pl.ds(first, tokens), :size] * taps_ref[tap : tap + 1, columns]
            total = part if total is None else total + part
        return (total / (1.0 + jnp.exp(-total))).astype(BF16)

    for start in range(0, width, 128):
        x_ref[:, pl.ds(start, 128)] = convolved(start, 128)
    bc_ref[...] = convolved(width, share)
    heads = step_ref.shape[1]
    columns = pl.ds(width + share, heads)
    raw = (mine_ref[:, columns] + far_ref[:, columns].astype(F32)) * scale
    raw = raw[rows - tokens :] + bias_ref[...]
    step_ref[...] = jnp.maximum(raw, 0.0) + jnp.log1p(jnp.exp(-jnp.abs(raw)))


def conv_call(mine, far, scale, taps, bias, tokens, width, share):
    rows = mine.shape[0]
    heads = bias.shape[1]
    return pl.pallas_call(
        conv_kernel,
        name="conv",
        out_shape=[
            shape((tokens, width), BF16),
            shape((tokens, share), BF16),
            shape((tokens, heads), F32),
        ],
        in_specs=[VMEM_SPEC] * 5,
        out_specs=[VMEM_SPEC] * 3,
        scratch_shapes=[pltpu.VMEM((rows, 128), F32)],
        cost_estimate=pl.CostEstimate(
            flops=16 * mine.size, bytes_accessed=8 * mine.size, transcendentals=mine.size
        ),
        compiler_params=pltpu.CompilerParams(vmem_limit_bytes=32 * 2**20),
    )(mine, far, scale, taps, bias)


def fetch(spot, sources, buffer, sem, start):
    reach = len(sources) // 2
    for k in range(len(sources)):

        @pl.when(spot == k - reach)
        def _():
            copy = pltpu.make_async_copy(sources[k], buffer, sem)
            if start:
                copy.start()
            else:
                copy.wait()


def out_kernel(count, where_ref, own_ref, far_ref, *refs):
    sources, outs, (buffers, sems) = refs[:7], refs[7:-2], refs[-2:]
    tokens = own_ref.shape[0]
    own_start = pl.multiple_of(where_ref[0] * tokens, tokens)
    far_start = pl.multiple_of((1 - where_ref[0]) * tokens, tokens)
    fetch(where_ref[1], sources, buffers.at[0], sems.at[0], True)
    for i in range(count):
        if i + 1 < count:
            slot = (i + 1) % 2
            fetch(where_ref[i + 2], sources, buffers.at[slot], sems.at[slot], True)
        fetch(where_ref[i + 1], sources, buffers.at[i % 2], sems.at[i % 2], False)
        weight = buffers[i % 2]
        for ref, start in ((own_ref, own_start), (far_ref, far_start)):
            product = jnp.dot(ref[...], weight, preferred_element_type=F32)
            if len(outs) == 1:
                outs[0][i, pl.ds(start, tokens), :] = product.astype(outs[0].dtype)
            else:
                outs[i][pl.ds(start, tokens), :] = product.astype(outs[i].dtype)


def in_kernel(count, where_ref, hidden_ref, *refs):
    sources, (out_ref, buffers, total, sems) = refs[:7], refs[7:]
    rows = out_ref.shape[0]
    window = pl.ds(pl.multiple_of(where_ref[0], HALO), rows)
    fetch(where_ref[1], sources, buffers.at[0], sems.at[0], True)
    for i in range(count):
        if i + 1 < count:
            slot = (i + 1) % 2
            fetch(where_ref[i + 2], sources, buffers.at[slot], sems.at[slot], True)
        fetch(where_ref[i + 1], sources, buffers.at[i % 2], sems.at[i % 2], False)
        hidden = hidden_ref[i, window, :]
        depth = hidden.shape[1]
        large = jnp.dot(hidden, buffers[i % 2, :depth, :], preferred_element_type=F32)
        packed = buffers[i % 2, depth:, :]
        small = lax.dot_general(
            hidden,
            jnp.concatenate([packed[:, :depth], packed[:, depth:]], axis=0),
            (((1,), (1,)), ((), ())),
            preferred_element_type=F32,
        )[:, : out_ref.shape[1] - large.shape[1]]
        for part, columns in (
            (large, slice(0, large.shape[1])),
            (small, slice(large.shape[1], out_ref.shape[1])),
        ):
            if i == 0:
                total[:, columns] = part
            elif i + 1 < count:
                total[:, columns] += part
            else:
                out_ref[:, columns] = (total[:, columns] + part).astype(out_ref.dtype)


def out_call(where, own, far, sources, outs):
    count = where.shape[0] - 1
    tokens, depth = own.shape
    block = sources[0].shape
    return pl.pallas_call(
        functools.partial(out_kernel, count),
        out_shape=outs,
        in_specs=[SMEM_SPEC, VMEM_SPEC, VMEM_SPEC] + [ANY_SPEC] * len(sources),
        out_specs=[VMEM_SPEC] * len(outs),
        scratch_shapes=[pltpu.VMEM((2,) + block, BF16), pltpu.SemaphoreType.DMA((2,))],
        cost_estimate=pl.CostEstimate(
            flops=4 * count * tokens * depth * block[1],
            bytes_accessed=4 * own.size + 2 * count * sources[0].size,
            transcendentals=0,
        ),
        compiler_params=pltpu.CompilerParams(vmem_limit_bytes=32 * 2**20),
    )(where, own, far, *sources)


def in_call(where, hidden, sources, rows, columns, kind):
    count, _, depth = hidden.shape
    block = sources[0].shape
    return pl.pallas_call(
        functools.partial(in_kernel, count),
        out_shape=shape((rows, columns), kind),
        in_specs=[SMEM_SPEC, VMEM_SPEC] + [ANY_SPEC] * len(sources),
        out_specs=VMEM_SPEC,
        scratch_shapes=[
            pltpu.VMEM((2,) + block, BF16),
            pltpu.VMEM((rows, columns), F32),
            pltpu.SemaphoreType.DMA((2,)),
        ],
        cost_estimate=pl.CostEstimate(
            flops=2 * count * rows * depth * block[1],
            bytes_accessed=2 * hidden.size + 2 * count * sources[0].size,
            transcendentals=0,
        ),
        compiler_params=pltpu.CompilerParams(vmem_limit_bytes=40 * 2**20),
    )(where, hidden, *sources)


def pick(stack, index):
    return lax.dynamic_index_in_dim(stack, index, 0, False)


def exchange_states(end, payload, y):
    full, packed = shape(end.shape, F32), shape(payload.shape, BF16)
    row = shape((1, end.shape[1]), F32)
    flag = y[None].astype(jnp.int32)
    far = y_swap(payload)
    window, payload, early, early_decay = whole_call(
        pair_kernel, [full, packed, full, row], end.size, flag, end, payload, far
    )
    parts = ()
    reach, size = 1, lax.axis_size("seq") // 2
    while 2 * reach < size:
        far = z_shift(payload, reach)
        window, payload, *parts = whole_call(
            step_kernel if parts else start_kernel,
            [full, packed, full, row],
            end.size,
            window,
            payload,
            far,
            *parts,
        )
        reach *= 2
    far = z_shift(payload, reach)
    return (flag, early, early_decay, *parts, far)


def on_device(
    x_in,
    gate_in,
    bc_in,
    step_in,
    decay_code,
    decay_rate,
    skip_gain,
    norm_gain,
    w_out,
    resid_in,
    resid_gain,
    w_in_x,
    w_in_bc,
    w_in_dt,
    step_time_bias,
    conv_x,
    conv_bc,
):
    tokens, width = x_in.shape
    seq_size, head_size = lax.axis_size("seq"), lax.axis_size("head")
    z_size = seq_size // 2
    seq_place, head = lax.axis_index("seq"), lax.axis_index("head")
    z, y = seq_place // 2, seq_place % 2
    x_bit, c_bit = head // 2, head % 2
    inner_count = width * head_size
    pair_tokens = 2 * tokens
    state_width = bc_in.shape[1] // 2
    block = w_out.shape[1]
    half = width // 2
    per_head = z_size // head_size
    first = y == 0
    line = z_size == 4 and per_head == 1

    share = w_in_bc.shape[1] // head_size
    bc_weight = lax.dynamic_slice_in_dim(w_in_bc, head * share, share, 1)
    small = share + w_in_dt.shape[1]
    if line:
        below = jnp.concatenate([bc_weight, w_in_dt], axis=1).T
        below = jnp.concatenate([below, jnp.zeros((-small % 32, block), BF16)], axis=0)
        below = below.reshape(2, below.shape[0] // 2, block)
        below = jnp.concatenate([below[0], below[1]], axis=1)
        out_blocks = z_line(w_out)
        in_blocks = z_line(jnp.concatenate([w_in_x, below], axis=0))
    else:
        w_in = jnp.concatenate([w_in_x, bc_weight, w_in_dt], axis=1)
        out_blocks, in_blocks = z_whole(w_out), z_whole(w_in)

    def parity(array, which):
        if per_head == 1:
            return lax.dynamic_slice_in_dim(array, which * block, block, 1)
        parts = array.reshape(tokens, per_head, 2, block)
        return lax.dynamic_index_in_dim(parts, which, 2, False).reshape(tokens, half)

    resid_own = parity(resid_in, y)
    resid_far = y_swap(parity(resid_in, 1 - y))

    code_one, rate_one = decay_code[0], decay_rate[0][None, :]
    first_one, end_one, payload_one = chunk_states(
        x_in, bc_in[:, :state_width], step_in, code_one, rate_one
    )
    within_one = within_blocks(x_in, bc_in, step_in, code_one, rate_one, skip_gain[0][None, :])
    carried_one = exchange_states(end_one, payload_one, y)
    scaled, square_own = whole_call(
        gated_kernel,
        [shape((tokens, width), BF16), shape((1, tokens), F32)],
        4 * x_in.size * state_width,
        *carried_one,
        first_one,
        within_one,
        bc_in[:, state_width:],
        code_one,
        rate_one,
        gate_in,
        norm_gain[None, :],
    )
    scaled_far = y_swap(scaled)
    square_own = square_own + c_swap(square_own)
    square_own = square_own + x_swap(square_own)
    square_far = y_swap(square_own)
    square_one = jnp.concatenate(
        [jnp.where(first, square_own, square_far), jnp.where(first, square_far, square_own)], axis=1
    )[0]
    resid = jnp.concatenate(
        [jnp.where(first, resid_own, resid_far), jnp.where(first, resid_far, resid_own)], axis=0
    ).astype(F32)

    keep_heads = [2 * (x_bit ^ i) + c_bit for i in range(2)]
    send_heads = [2 * (x_bit ^ i) + (1 - c_bit) for i in range(2)]
    if line:
        where = lambda heads: jnp.stack([y] + [z - h for h in heads]).astype(jnp.int32)
        (sends,) = out_call(
            where(send_heads),
            scaled,
            scaled_far,
            out_blocks,
            [shape((2, pair_tokens, block), BF16)],
        )
        keeps = out_call(
            where(keep_heads),
            scaled,
            scaled_far,
            out_blocks,
            [shape((pair_tokens, block), F32)] * 2,
        )
    else:
        both = jnp.concatenate(
            [jnp.where(first, scaled, scaled_far), jnp.where(first, scaled_far, scaled)], axis=0
        )
        by_head = out_blocks.reshape(head_size, per_head, width, block)
        by_head = by_head.transpose(0, 2, 1, 3).reshape(head_size, width, half)
        product = lambda h: jnp.dot(both, pick(by_head, h), preferred_element_type=F32)
        sends = jnp.stack([product(h) for h in send_heads]).astype(BF16)
        keeps = [product(h) for h in keep_heads]
    received = c_swap(sends)
    crossing = x_swap((keeps[1] + received[1].astype(F32)).astype(BF16))
    partial_share = keeps[0] + received[0].astype(F32) + crossing.astype(F32)
    resid_new = (
        resid + partial_share * lax.rsqrt(square_one / inner_count + 1e-05)[:, None]
    ).astype(BF16)

    resid_back = y_swap(lax.dynamic_slice_in_dim(resid_new, (1 - y) * tokens, tokens, 0))
    resid_mine = lax.dynamic_slice_in_dim(resid_new, y * tokens, tokens, 0)
    both = [jnp.where(first, resid_mine, resid_back), jnp.where(first, resid_back, resid_mine)]
    if per_head == 1:
        resid_out = jnp.concatenate(both, axis=1)
    else:
        both = [a.reshape(tokens, per_head, block) for a in both]
        resid_out = jnp.stack(both, axis=2).reshape(tokens, width)

    gains = resid_gain.reshape(z_size, 2, block)
    gain = lax.dynamic_slice_in_dim(
        lax.dynamic_index_in_dim(gains, y, 1, False), head * per_head, per_head, 0
    ).reshape(half)
    hidden_wide = resid_new.astype(F32)
    hidden = (hidden_wide * gain[None, :]).astype(BF16)
    pair = jnp.stack([hidden, x_swap(hidden)])
    other = c_swap(pair)
    square_two = jnp.sum(hidden_wide * hidden_wide, axis=1)
    square_two = square_two + x_swap(square_two)
    square_two = square_two + c_swap(square_two)
    square_two = square_two + y_swap(square_two)
    all_hidden = jnp.stack([pair[0], other[0], pair[1], other[1]])
    halo_hidden = z_shift(all_hidden[:, pair_tokens - HALO :], 1)
    halo_square = z_shift(square_two[pair_tokens - HALO :], 1)
    all_hidden = jnp.concatenate([halo_hidden, all_hidden], axis=1)
    scale_two = lax.rsqrt(jnp.concatenate([halo_square, square_two]) / inner_count + 1e-05)

    reach = tokens + HALO
    keep_start = jnp.where(first, 0, tokens)
    send_start = tokens - keep_start
    if line:
        spots = [z - (head ^ k) for k in range(4)]
        where = lambda start: jnp.stack([start] + spots).astype(jnp.int32)
        columns = width + small
        theirs = in_call(where(send_start), all_hidden, in_blocks, reach, columns, BF16)
        mine = in_call(where(keep_start), all_hidden, in_blocks, reach, columns, F32)
    else:
        wide = jnp.concatenate([pick(all_hidden, head ^ i) for i in range(head_size)], axis=1)
        total = jnp.dot(
            wide, in_blocks.reshape(z_size * block, w_in.shape[1]), preferred_element_type=F32
        )
        mine = lax.dynamic_slice_in_dim(total, keep_start, reach, 0)
        theirs = lax.dynamic_slice_in_dim(total, send_start, reach, 0).astype(BF16)
    scale_mine = lax.dynamic_slice_in_dim(scale_two, keep_start, reach, 0)
    taps = jnp.concatenate(
        [conv_x, lax.dynamic_slice_in_dim(conv_bc, head * share, share, 1)], axis=1
    ).astype(F32)
    x_two, bc_share, step_two = conv_call(
        mine,
        y_swap(theirs),
        scale_mine[:, None],
        taps,
        step_time_bias[None, :],
        tokens,
        width,
        share,
    )
    bc_pair = jnp.stack([bc_share, x_swap(bc_share)])
    bc_other = c_swap(bc_pair)
    bc_stack = jnp.stack([bc_pair[0], bc_other[0], bc_pair[1], bc_other[1]])
    bc_two = jnp.concatenate([pick(bc_stack, head ^ i) for i in range(head_size)], axis=1)

    code_two, rate_two = decay_code[1], decay_rate[1][None, :]
    first_two, end_two, payload_two = chunk_states(
        x_two, bc_two[:, :state_width], step_two, code_two, rate_two
    )
    within_two = within_blocks(x_two, bc_two, step_two, code_two, rate_two, skip_gain[1][None, :])
    carried_two = exchange_states(end_two, payload_two, y)
    mixed_two, square_last = whole_call(
        last_kernel,
        [shape((tokens, width), F32), shape((1, tokens), F32)],
        4 * x_in.size * state_width,
        *carried_two,
        first_two,
        within_two,
        bc_two[:, state_width:],
        code_two,
        rate_two,
    )
    square_last = lax.psum(square_last[0], "head")
    mixer_out = (mixed_two * lax.rsqrt(square_last / inner_count + 1e-05)[:, None]).astype(BF16)
    return (resid_out, mixer_out)


def solution(mesh):
    in_specs = (
        P("seq", "head"),
        P("seq", "head"),
        P("seq", None),
        P("seq", "head"),
        P(None, "seq", "head"),
        P(None, "head"),
        P(None, "head"),
        P("head"),
        P("head", "seq"),
        P("seq", "head"),
        P(),
        P("seq", "head"),
        P("seq", None),
        P("seq", "head"),
        P("head"),
        P(None, "head"),
        P(),
    )
    out_specs = (P("seq", "head"), P("seq", "head"))

    return jax.shard_map(
        on_device, mesh=mesh, in_specs=in_specs, out_specs=out_specs, check_vma=False
    )
```

profile of v0, /device:TPU:28, one launch (start us, length us, event | category | flops | bytes accessed | tf_op | source)
XLA Modules:
  0.0 369.8 jit_solution(2542876096083757144)
XLA Ops:
  8.0 17.9 %collective-permute-done.5.refs_2_ = bf16[1024,512]{1,0:T(8,128)(2,1)S(1)} collective-permute-done((bf16[1024,512]{1,0:T(8,128)(2,1)}, bf16[1024,512]{1,0:T(8,128)(2,1)S(1)}, u32[]{:S(2)}, u32[]{:S(2)}) %collective-permute-start.5) | collective-permute-done | bytes 1048608 | tf_op jit(solution)/shard_map/ppermute | solution.py:19
  25.9 5.3 %collective-permute-start.6 = (bf16[1024,512]{1,0:T(8,128)(2,1)S(1)}, bf16[1024,512]{1,0:T(8,128)(2,1)}, u32[]{:S(2)}, u32[]{:S(2)}) collective-permute-start(bf16[1024,512]{1,0:T(8,128)(2,1)S(1)} %collective-permute-done.5.refs_2_), channel_id=1, source_target_pairs={{8,0},{12,4},{16,8},{20,12},{24,16},{28,20},{9,1},{13,5},{17,9},{2... | collective-permute-start | bytes 3145736 | tf_op jit(solution)/shard_map/ppermute | solution.py:19
  40.3 7.4 %collective-permute-done.1.far_ref = bf16[144,1024]{1,0:T(8,128)(2,1)} collective-permute-done((bf16[144,1024]{1,0:T(8,128)(2,1)}, bf16[144,1024]{1,0:T(8,128)(2,1)}, u32[]{:S(2)}, u32[]{:S(2)}) %collective-permute-start.1) | collective-permute-done | bytes 294944 | tf_op jit(solution)/shard_map/ppermute | solution.py:24
  50.2 12.9 %collective-permute-done.2.far_ref = bf16[144,1024]{1,0:T(8,128)(2,1)S(1)} collective-permute-done((bf16[144,1024]{1,0:T(8,128)(2,1)S(1)}, bf16[144,1024]{1,0:T(8,128)(2,1)S(1)}, u32[]{:S(2)}, u32[]{:S(2)}) %collective-permute-start.2) | collective-permute-done | bytes 294944 | tf_op jit(solution)/shard_map/ppermute | solution.py:19
  70.1 8.8 %collective-permute-done.3.far_ref = bf16[144,1024]{1,0:T(8,128)(2,1)S(1)} collective-permute-done((bf16[144,1024]{1,0:T(8,128)(2,1)S(1)}, bf16[144,1024]{1,0:T(8,128)(2,1)S(1)}, u32[]{:S(2)}, u32[]{:S(2)}) %collective-permute-start.3) | collective-permute-done | bytes 294944 | tf_op jit(solution)/shard_map/ppermute | solution.py:19
  79.8 5.9 %shard_map.179 = (bf16[512,1024]{1,0:T(8,128)(2,1)}, f32[1,512]{1,0:T(1,128)S(1)}) custom-call(s32[1]{0:T(128)} %bitcast.y_ref, f32[128,1024]{1,0:T(8,128)S(1)} %get-tuple-element.33.early_ref, f32[1,1024]{1,0:T(1,128)S(1)} %get-tuple-element.34.early_decay_ref, f32[128,1024]{1,0:T(8,128)S(1)} %get-tuple-element.37.before_ref, ...), custom_call_target="tpu_custom_call" | custom-call | flops 268435456 | bytes 6240324 | tf_op jit(solution)/shard_map/pallas_call | solution.py:290
  89.9 21.1 %collective-permute-done.4.far_ref = bf16[512,1024]{1,0:T(8,128)(2,1)} collective-permute-done((bf16[512,1024]{1,0:T(8,128)(2,1)}, bf16[512,1024]{1,0:T(8,128)(2,1)}, u32[]{:S(2)}, u32[]{:S(2)}) %collective-permute-start.4) | collective-permute-done | bytes 1048608 | tf_op jit(solution)/shard_map/ppermute | solution.py:24
  115.5 6.7 %shard_map.181 = bf16[2,1024,512]{2,1,0:T(8,128)(2,1)} custom-call(s32[3]{0:T(128)S(1)} %pad_add_fusion.1.where_ref, bf16[512,1024]{1,0:T(8,128)(2,1)} %get-tuple-element.41.own_ref, bf16[512,1024]{1,0:T(8,128)(2,1)} %collective-permute-done.4.far_ref, bf16[1024,512]{1,0:T(8,128)(2,1)} %collective-permute-done.7.refs_0_, ...), custom_call_target="tpu_custom_call" | custom-call | flops 2147483648 | bytes 4194304 | tf_op jit(solution)/shard_map/pallas_call | solution.py:459
  125.8 5.3 %shard_map.180 = (f32[1024,512]{1,0:T(8,128)S(1)}, f32[1024,512]{1,0:T(8,128)S(1)}) custom-call(s32[3]{0:T(128)S(1)} %pad_add_fusion.where_ref, bf16[512,1024]{1,0:T(8,128)(2,1)} %get-tuple-element.41.own_ref, bf16[512,1024]{1,0:T(8,128)(2,1)} %collective-permute-done.4.far_ref, bf16[1024,512]{1,0:T(8,128)(2,1)} %collective-permute-done.7.refs_0_, ...), custom_call_target="tpu_custom_call" | custom-call | flops 2147483648 | bytes 4194304 | tf_op jit(solution)/shard_map/pallas_call | solution.py:459
  137.7 22.4 %collective-permute-done.14 = f32[1,512]{1,0:T(1,128)S(1)} collective-permute-done((f32[1,512]{1,0:T(1,128)S(1)}, f32[1,512]{1,0:T(1,128)S(1)}, u32[]{:S(2)}, u32[]{:S(2)}) %collective-permute-start.14) | collective-permute-done | bytes 2080 | tf_op jit(solution)/shard_map/ppermute | solution.py:24
  172.3 18.6 %collective-permute-done.17 = bf16[1024,512]{1,0:T(8,128)(2,1)} collective-permute-done((bf16[1024,512]{1,0:T(8,128)(2,1)}, bf16[1024,512]{1,0:T(8,128)(2,1)}, u32[]{:S(2)}, u32[]{:S(2)}) %collective-permute-start.17) | collective-permute-done | bytes 1048608 | tf_op jit(solution)/shard_map/ppermute | solution.py:24
  192.7 5.5 %collective-permute-start.21 = (bf16[560,1024]{1,0:T(8,128)(2,1)S(1)}, bf16[560,1024]{1,0:T(8,128)(2,1)}, u32[]{:S(2)}, u32[]{:S(2)}) collective-permute-start(bf16[560,1024]{1,0:T(8,128)(2,1)S(1)} %collective-permute-done.20.refs_2_), channel_id=1, source_target_pairs={{8,0},{12,4},{16,8},{20,12},{24,16},{28,20},{9,1},{13,5},{17,9},{2... | collective-permute-start | bytes 3440648 | tf_op jit(solution)/shard_map/ppermute | solution.py:19
  199.4 19.9 %collective-permute-done.21.refs_1_ = bf16[560,1024]{1,0:T(8,128)(2,1)} collective-permute-done((bf16[560,1024]{1,0:T(8,128)(2,1)S(1)}, bf16[560,1024]{1,0:T(8,128)(2,1)}, u32[]{:S(2)}, u32[]{:S(2)}) %collective-permute-start.21) | collective-permute-done | bytes 1146912 | tf_op jit(solution)/shard_map/ppermute | solution.py:19
  219.4 5.5 %collective-permute-start.22 = (bf16[560,1024]{1,0:T(8,128)(2,1)}, bf16[560,1024]{1,0:T(8,128)(2,1)}, u32[]{:S(2)}, u32[]{:S(2)}) collective-permute-start(bf16[560,1024]{1,0:T(8,128)(2,1)} %collective-permute-done.21.refs_1_), channel_id=1, source_target_pairs={{8,0},{12,4},{16,8},{20,12},{24,16},{28,20},{9,1},{13,5},{17,9},{2... | collective-permute-start | bytes 3440648 | tf_op jit(solution)/shard_map/ppermute | solution.py:19
  230.0 22.0 %collective-permute-done.19 = bf16[4,16,512]{2,1,0:T(8,128)(2,1)S(1)} collective-permute-done((bf16[4,16,512]{2,1,0:T(8,128)(2,1)}, bf16[4,16,512]{2,1,0:T(8,128)(2,1)S(1)}, u32[]{:S(2)}, u32[]{:S(2)}) %collective-permute-start.19) | collective-permute-done | bytes 65568 | tf_op jit(solution)/shard_map/ppermute | solution.py:19
  254.4 7.9 %shard_map.183 = bf16[528,1104]{1,0:T(8,128)(2,1)} custom-call(s32[5]{0:T(128)S(1)} %stack.92.where_ref, bf16[4,1040,512]{2,1,0:T(8,128)(2,1)S(1)} %maximum_maximum_fusion.hidden_ref, bf16[560,1024]{1,0:T(8,128)(2,1)} %collective-permute-done.22.refs_0_, bf16[560,1024]{1,0:T(8,128)(2,1)} %collective-permute-done.21.refs_1_, ...), custom_call_target="tpu_custom_call" | custom-call | flops 2214592512 | bytes 8847360 | tf_op jit(solution)/shard_map/pallas_call | solution.py:477
  269.2 18.0 %collective-permute-done.29 = f32[1024]{0:T(1024)S(1)} collective-permute-done((f32[1024]{0:T(1024)S(1)}, f32[1024]{0:T(1024)S(1)}, u32[]{:S(2)}, u32[]{:S(2)}) %collective-permute-start.29) | collective-permute-done | bytes 4128 | tf_op jit(solution)/shard_map/ppermute | solution.py:24
  293.0 7.9 %shard_map.182.mine_ref = f32[528,1104]{1,0:T(8,128)S(1)} custom-call(s32[5]{0:T(128)S(1)} %stack.86.where_ref, bf16[4,1040,512]{2,1,0:T(8,128)(2,1)} %copy-done.2, bf16[560,1024]{1,0:T(8,128)(2,1)} %collective-permute-done.22.refs_0_, bf16[560,1024]{1,0:T(8,128)(2,1)} %collective-permute-done.21.refs_1_, ...), custom_call_target="tpu_custom_call" | custom-call | flops 2214592512 | bytes 8847360 | tf_op jit(solution)/shard_map/pallas_call | solution.py:477
  304.8 5.0 %collective-permute-done.31 = bf16[512,64]{1,0:T(8,128)(2,1)S(1)} collective-permute-done((bf16[512,64]{1,0:T(8,128)(2,1)S(1)}, bf16[512,64]{1,0:T(8,128)(2,1)S(1)}, u32[]{:S(2)}, u32[]{:S(2)}) %collective-permute-start.31) | collective-permute-done | bytes 65568 | tf_op jit(solution)/shard_map/ppermute | solution.py:24
  316.5 14.3 %collective-permute-done.33.far_ref = bf16[144,1024]{1,0:T(8,128)(2,1)S(1)} collective-permute-done((bf16[144,1024]{1,0:T(8,128)(2,1)S(1)}, bf16[144,1024]{1,0:T(8,128)(2,1)S(1)}, u32[]{:S(2)}, u32[]{:S(2)}) %collective-permute-start.33) | collective-permute-done | bytes 294944 | tf_op jit(solution)/shard_map/ppermute | solution.py:24
  333.8 7.6 %collective-permute-done.34.far_ref = bf16[144,1024]{1,0:T(8,128)(2,1)S(1)} collective-permute-done((bf16[144,1024]{1,0:T(8,128)(2,1)S(1)}, bf16[144,1024]{1,0:T(8,128)(2,1)S(1)}, u32[]{:S(2)}, u32[]{:S(2)}) %collective-permute-start.34) | collective-permute-done | bytes 294944 | tf_op jit(solution)/shard_map/ppermute | solution.py:19
  348.6 9.6 %collective-permute-done.35.far_ref = bf16[144,1024]{1,0:T(8,128)(2,1)S(1)} collective-permute-done((bf16[144,1024]{1,0:T(8,128)(2,1)S(1)}, bf16[144,1024]{1,0:T(8,128)(2,1)S(1)}, u32[]{:S(2)}, u32[]{:S(2)}) %collective-permute-start.35) | collective-permute-done | bytes 294944 | tf_op jit(solution)/shard_map/ppermute | solution.py:19
  358.2 4.7 %shard_map.187 = (f32[512,1024]{1,0:T(8,128)S(1)}, f32[1,512]{1,0:T(1,128)S(1)}) custom-call(s32[1]{0:T(128)} %bitcast.y_ref, f32[128,1024]{1,0:T(8,128)S(1)} %get-tuple-element.50.early_ref, f32[1,1024]{1,0:T(1,128)S(1)} %get-tuple-element.51.early_decay_ref, f32[128,1024]{1,0:T(8,128)S(1)} %get-tuple-element.54.before_ref, ...), custom_call_target="tpu_custom_call" | custom-call | flops 268435456 | bytes 6236228 | tf_op jit(solution)/shard_map/pallas_call | solution.py:290
  362.9 5.6 %psum.7 = f32[512]{0:T(512)S(1)} all-reduce(f32[512]{0:T(512)S(1)} %bitcast.53), channel_id=1, replica_groups=mesh['seq'=8,'head'=4] {'head'}, use_global_device_ids=true, to_apply=%region_1.2 | all-reduce | flops 512 | bytes 4096 | tf_op jit(solution)/shard_map/psum | solution.py:726
  (175 shorter events, 102.6 us)
Async XLA Ops:
  0.6 25.2 %collective-permute-start.5 = (bf16[1024,512]{1,0:T(8,128)(2,1)}, bf16[1024,512]{1,0:T(8,128)(2,1)S(1)}, u32[]{:S(2)}, u32[]{:S(2)}) collective-permute-start(bf16[1024,512]{1,0:T(8,128)(2,1)} %refs_3_.3), channel_id=1, source_target_pairs={{8,0},{12,4},{16,8},{20,12},{24,16},{28,20},{9,1},{13,5},{17,9},{2... | collective-permute-start | bytes 3145736 | tf_op jit(solution)/shard_map/ppermute | solution.py:19
  3.2 27.9 %collective-permute-start.8 = (bf16[1024,512]{1,0:T(8,128)(2,1)}, bf16[1024,512]{1,0:T(8,128)(2,1)S(1)}, u32[]{:S(2)}, u32[]{:S(2)}) collective-permute-start(bf16[1024,512]{1,0:T(8,128)(2,1)} %refs_3_.3), channel_id=1, source_target_pairs={{0,8},{4,12},{8,16},{12,20},{16,24},{20,28},{1,9},{5,13},{9,17},{1... | collective-permute-start | bytes 3145736 | tf_op jit(solution)/shard_map/ppermute | solution.py:19
  25.9 60.3 %collective-permute-start.6 = (bf16[1024,512]{1,0:T(8,128)(2,1)S(1)}, bf16[1024,512]{1,0:T(8,128)(2,1)}, u32[]{:S(2)}, u32[]{:S(2)}) collective-permute-start(bf16[1024,512]{1,0:T(8,128)(2,1)S(1)} %collective-permute-done.5.refs_2_), channel_id=1, source_target_pairs={{8,0},{12,4},{16,8},{20,12},{24,16},{28,20},{9,1},{13,5},{17,9},{2... | collective-permute-start | bytes 3145736 | tf_op jit(solution)/shard_map/ppermute | solution.py:19
  31.2 57.4 %collective-permute-start.9 = (bf16[1024,512]{1,0:T(8,128)(2,1)S(1)}, bf16[1024,512]{1,0:T(8,128)(2,1)}, u32[]{:S(2)}, u32[]{:S(2)}) collective-permute-start(bf16[1024,512]{1,0:T(8,128)(2,1)S(1)} %collective-permute-done.8.refs_4_), channel_id=1, source_target_pairs={{0,8},{4,12},{8,16},{12,20},{16,24},{20,28},{1,9},{5,13},{9,17},{1... | collective-permute-start | bytes 3145736 | tf_op jit(solution)/shard_map/ppermute | solution.py:19
  85.7 25.4 %collective-permute-start.4 = (bf16[512,1024]{1,0:T(8,128)(2,1)}, bf16[512,1024]{1,0:T(8,128)(2,1)}, u32[]{:S(2)}, u32[]{:S(2)}) collective-permute-start(bf16[512,1024]{1,0:T(8,128)(2,1)} %get-tuple-element.41.own_ref), channel_id=1, source_target_pairs={{0,4},{4,0},{8,12},{12,8},{16,20},{20,16},{24,28},{28,24},{1,5},{5... | collective-permute-start | bytes 3145736 | tf_op jit(solution)/shard_map/ppermute | solution.py:24
  86.2 24.9 %collective-permute-start.7 = (bf16[1024,512]{1,0:T(8,128)(2,1)}, bf16[1024,512]{1,0:T(8,128)(2,1)}, u32[]{:S(2)}, u32[]{:S(2)}) collective-permute-start(bf16[1024,512]{1,0:T(8,128)(2,1)} %collective-permute-done.6.refs_1_), channel_id=1, source_target_pairs={{8,0},{12,4},{16,8},{20,12},{24,16},{28,20},{9,1},{13,5},{17,9},{2... | collective-permute-start | bytes 3145736 | tf_op jit(solution)/shard_map/ppermute | solution.py:19
  88.5 27.0 %collective-permute-start.10 = (bf16[1024,512]{1,0:T(8,128)(2,1)}, bf16[1024,512]{1,0:T(8,128)(2,1)}, u32[]{:S(2)}, u32[]{:S(2)}) collective-permute-start(bf16[1024,512]{1,0:T(8,128)(2,1)} %collective-permute-done.9.refs_5_), channel_id=1, source_target_pairs={{0,8},{4,12},{8,16},{12,20},{16,24},{20,28},{1,9},{5,13},{9,17},{1... | collective-permute-start | bytes 3145736 | tf_op jit(solution)/shard_map/ppermute | solution.py:19
  124.2 36.5 %collective-permute-start = (bf16[512,512]{1,0:T(8,128)(2,1)}, bf16[512,512]{1,0:T(8,128)(2,1)}, u32[]{:S(2)}, u32[]{:S(2)}) collective-permute-start(bf16[512,512]{1,0:T(8,128)(2,1)} %constant_dynamic-slice_fusion.4), channel_id=1, source_target_pairs={{0,4},{4,0},{8,12},{12,8},{16,20},{20,16},{24,28},{28,24},{1,5},{5... | collective-permute-start | bytes 1572872 | tf_op jit(solution)/shard_map/ppermute | solution.py:24
  134.5 29.2 %collective-permute-start.12 = (bf16[1024,512]{1,0:T(8,128)(2,1)}, bf16[1024,512]{1,0:T(8,128)(2,1)}, u32[]{:S(2)}, u32[]{:S(2)}) collective-permute-start(bf16[1024,512]{1,0:T(8,128)(2,1)} %fusion.2), channel_id=1, source_target_pairs={{0,2},{1,3},{2,0},{3,1},{4,6},{5,7},{6,4},{7,5},{8,10},{9,11},{10,... | collective-permute-start | bytes 3145736 | tf_op jit(solution)/shard_map/ppermute | solution.py:24
  135.8 24.4 %collective-permute-start.14 = (f32[1,512]{1,0:T(1,128)S(1)}, f32[1,512]{1,0:T(1,128)S(1)}, u32[]{:S(2)}, u32[]{:S(2)}) collective-permute-start(f32[1,512]{1,0:T(1,128)S(1)} %add.120), channel_id=1, source_target_pairs={{0,2},{1,3},{2,0},{3,1},{4,6},{5,7},{6,4},{7,5},{8,10},{9,11},{10,... | collective-permute-start | bytes 6152 | tf_op jit(solution)/shard_map/ppermute | solution.py:24
  167.3 23.6 %collective-permute-start.17 = (bf16[1024,512]{1,0:T(8,128)(2,1)}, bf16[1024,512]{1,0:T(8,128)(2,1)}, u32[]{:S(2)}, u32[]{:S(2)}) collective-permute-start(bf16[1024,512]{1,0:T(8,128)(2,1)} %fusion), channel_id=1, source_target_pairs={{0,2},{1,3},{2,0},{3,1},{4,6},{5,7},{6,4},{7,5},{8,10},{9,11},{10,... | collective-permute-start | bytes 3145736 | tf_op jit(solution)/shard_map/ppermute | solution.py:24
  168.2 24.5 %collective-permute-start.20 = (bf16[560,1024]{1,0:T(8,128)(2,1)S(1)}, bf16[560,1024]{1,0:T(8,128)(2,1)S(1)}, u32[]{:S(2)}, u32[]{:S(2)}) collective-permute-start(bf16[560,1024]{1,0:T(8,128)(2,1)S(1)} %maximum_maximum_fusion.1.refs_3_), channel_id=1, source_target_pairs={{8,0},{12,4},{16,8},{20,12},{24,16},{28,20},{9,1},{13,5},{17,9},{2... | collective-permute-start | bytes 3440648 | tf_op jit(solution)/shard_map/ppermute | solution.py:19
  169.6 28.6 %collective-permute-start.23 = (bf16[560,1024]{1,0:T(8,128)(2,1)S(1)}, bf16[560,1024]{1,0:T(8,128)(2,1)S(1)}, u32[]{:S(2)}, u32[]{:S(2)}) collective-permute-start(bf16[560,1024]{1,0:T(8,128)(2,1)S(1)} %maximum_maximum_fusion.1.refs_3_), channel_id=1, source_target_pairs={{0,8},{4,12},{8,16},{12,20},{16,24},{20,28},{1,9},{5,13},{9,17},{1... | collective-permute-start | bytes 3440648 | tf_op jit(solution)/shard_map/ppermute | solution.py:19
  192.3 33.8 %collective-permute-start.18 = (bf16[2,1024,512]{2,1,0:T(8,128)(2,1)S(1)}, bf16[2,1024,512]{2,1,0:T(8,128)(2,1)S(1)}, u32[]{:S(2)}, u32[]{:S(2)}) collective-permute-start(bf16[2,1024,512]{2,1,0:T(8,128)(2,1)S(1)} %pad_maximum_fusion), channel_id=1, source_target_pairs={{0,1},{1,0},{2,3},{3,2},{4,5},{5,4},{6,7},{7,6},{8,9},{9,8},{10,11... | collective-permute-start | bytes 6291464 | tf_op jit(solution)/shard_map/ppermute | solution.py:24
  192.7 26.7 %collective-permute-start.21 = (bf16[560,1024]{1,0:T(8,128)(2,1)S(1)}, bf16[560,1024]{1,0:T(8,128)(2,1)}, u32[]{:S(2)}, u32[]{:S(2)}) collective-permute-start(bf16[560,1024]{1,0:T(8,128)(2,1)S(1)} %collective-permute-done.20.refs_2_), channel_id=1, source_target_pairs={{8,0},{12,4},{16,8},{20,12},{24,16},{28,20},{9,1},{13,5},{17,9},{2... | collective-permute-start | bytes 3440648 | tf_op jit(solution)/shard_map/ppermute | solution.py:19
  198.1 26.7 %collective-permute-start.24 = (bf16[560,1024]{1,0:T(8,128)(2,1)S(1)}, bf16[560,1024]{1,0:T(8,128)(2,1)}, u32[]{:S(2)}, u32[]{:S(2)}) collective-permute-start(bf16[560,1024]{1,0:T(8,128)(2,1)S(1)} %collective-permute-done.23.refs_4_), channel_id=1, source_target_pairs={{0,8},{4,12},{8,16},{12,20},{16,24},{20,28},{1,9},{5,13},{9,17},{1... | collective-permute-start | bytes 3440648 | tf_op jit(solution)/shard_map/ppermute | solution.py:19
  219.4 35.0 %collective-permute-start.22 = (bf16[560,1024]{1,0:T(8,128)(2,1)}, bf16[560,1024]{1,0:T(8,128)(2,1)}, u32[]{:S(2)}, u32[]{:S(2)}) collective-permute-start(bf16[560,1024]{1,0:T(8,128)(2,1)} %collective-permute-done.21.refs_1_), channel_id=1, source_target_pairs={{8,0},{12,4},{16,8},{20,12},{24,16},{28,20},{9,1},{13,5},{17,9},{2... | collective-permute-start | bytes 3440648 | tf_op jit(solution)/shard_map/ppermute | solution.py:19
  224.8 29.6 %collective-permute-start.25 = (bf16[560,1024]{1,0:T(8,128)(2,1)}, bf16[560,1024]{1,0:T(8,128)(2,1)}, u32[]{:S(2)}, u32[]{:S(2)}) collective-permute-start(bf16[560,1024]{1,0:T(8,128)(2,1)} %collective-permute-done.24.refs_5_), channel_id=1, source_target_pairs={{0,8},{4,12},{8,16},{12,20},{16,24},{20,28},{1,9},{5,13},{9,17},{1... | collective-permute-start | bytes 3440648 | tf_op jit(solution)/shard_map/ppermute | solution.py:19
  228.6 23.4 %collective-permute-start.19 = (bf16[4,16,512]{2,1,0:T(8,128)(2,1)}, bf16[4,16,512]{2,1,0:T(8,128)(2,1)S(1)}, u32[]{:S(2)}, u32[]{:S(2)}) collective-permute-start(bf16[4,16,512]{2,1,0:T(8,128)(2,1)} %pad_maximum_fusion.7), channel_id=1, source_target_pairs={{0,8},{4,12},{8,16},{12,20},{16,24},{20,28},{1,9},{5,13},{9,17},{1... | collective-permute-start | bytes 196616 | tf_op jit(solution)/shard_map/ppermute | solution.py:19
  262.4 38.5 %collective-permute-start.26 = (bf16[528,1104]{1,0:T(8,128)(2,1)}, bf16[528,1104]{1,0:T(8,128)(2,1)}, u32[]{:S(2)}, u32[]{:S(2)}) collective-permute-start(bf16[528,1104]{1,0:T(8,128)(2,1)} %shard_map.183), channel_id=1, source_target_pairs={{0,4},{4,0},{8,12},{12,8},{16,20},{20,16},{24,28},{28,24},{1,5},{5... | collective-permute-start | bytes 3497480 | tf_op jit(solution)/shard_map/ppermute | solution.py:24
  268.0 19.2 %collective-permute-start.29 = (f32[1024]{0:T(1024)S(1)}, f32[1024]{0:T(1024)S(1)}, u32[]{:S(2)}, u32[]{:S(2)}) collective-permute-start(f32[1024]{0:T(1024)S(1)} %add.129), channel_id=1, source_target_pairs={{0,4},{4,0},{8,12},{12,8},{16,20},{20,16},{24,28},{28,24},{1,5},{5... | collective-permute-start | bytes 12296 | tf_op jit(solution)/shard_map/ppermute | solution.py:24
  310.1 22.2 %collective-permute-start.16 = (bf16[512,512]{1,0:T(8,128)(2,1)S(1)}, bf16[512,512]{1,0:T(8,128)(2,1)S(1)}, u32[]{:S(2)}, u32[]{:S(2)}) collective-permute-start(bf16[512,512]{1,0:T(8,128)(2,1)S(1)} %constant_dynamic-slice_fusion.3), channel_id=1, source_target_pairs={{0,4},{4,0},{8,12},{12,8},{16,20},{20,16},{24,28},{28,24},{1,5},{5... | collective-permute-start | bytes 1572872 | tf_op jit(solution)/shard_map/ppermute | solution.py:24
  315.6 15.2 %collective-permute-start.33 = (bf16[144,1024]{1,0:T(8,128)(2,1)S(1)}, bf16[144,1024]{1,0:T(8,128)(2,1)S(1)}, u32[]{:S(2)}, u32[]{:S(2)}) collective-permute-start(bf16[144,1024]{1,0:T(8,128)(2,1)S(1)} %get-tuple-element.49.own_ref), channel_id=1, source_target_pairs={{0,4},{4,0},{8,12},{12,8},{16,20},{20,16},{24,28},{28,24},{1,5},{5... | collective-permute-start | bytes 884744 | tf_op jit(solution)/shard_map/ppermute | solution.py:24
  342.3 16.0 %collective-permute-start.35 = (bf16[144,1024]{1,0:T(8,128)(2,1)S(1)}, bf16[144,1024]{1,0:T(8,128)(2,1)S(1)}, u32[]{:S(2)}, u32[]{:S(2)}) collective-permute-start(bf16[144,1024]{1,0:T(8,128)(2,1)S(1)} %get-tuple-element.56), channel_id=1, source_target_pairs={{0,16},{4,20},{8,24},{12,28},{1,17},{5,21},{9,25},{13,29},{2,18},{... | collective-permute-start | bytes 884744 | tf_op jit(solution)/shard_map/ppermute | solution.py:19
  (42 other events, 639.5 us)
where the time goes:
time: 372 us; the launch traced here: 370 us
  waiting for transfers between devices  222 us (60%)
  Pallas kernels  60.4 us (16%)
  starting transfers between devices  47.9 us (13%)
  other arithmetic  18.2 us (5%)
  local copies, waits for them, and re-layouts  14.1 us (4%)
  blocking collectives  5.65 us (2%)
    ppermute x18, waiting for transfers between devices, flip(): return lax.ppermute(value, axis, [(i, i ^ bit) for i in range(n)])  115 us
    ppermute x18, waiting for transfers between devices, z_shift(): return lax.ppermute(value, 'seq', pairs)  107 us
    ppermute x18, starting transfers between devices, z_shift(): return lax.ppermute(value, 'seq', pairs)  38.2 us
    pallas_call x8, Pallas kernels, whole_call(): pl.pallas_call(kernel, out_shape=outs, in_specs=[SMEM_SPEC if a.shape ==...  22 us
    pallas_call x2, Pallas kernels, in_call(): pl.pallas_call(functools.partial(in_kernel, count), out_shape=shape((rows...  15.8 us
    pallas_call x2, Pallas kernels, out_call(): pl.pallas_call(functools.partial(out_kernel, count), out_shape=outs, in_s...  12 us
    ppermute x18, starting transfers between devices, flip(): return lax.ppermute(value, axis, [(i, i ^ bit) for i in range(n)])  9.73 us
    unnamed x64, local copies, waits for them, and re-layouts  8.16 us
  transfers between devices with their start and end apart: 36, of which 22 were waited for; matrix products, arithmetic and copies ran while one was open for 6% of the time, Pallas kernels for 10%

commit v1 on v0

--- a/solution.py
+++ b/solution.py
@@ -9,6 +9,7 @@
 HEAD_CHANNELS = 64
 GROUP = 256
 HALO = 16
+ROWS = 256
 F32 = jnp.float32
 BF16 = jnp.bfloat16
 
@@ -281,7 +282,7 @@
 
 VMEM_SPEC = pl.BlockSpec(memory_space=pltpu.VMEM)
 SMEM_SPEC = pl.BlockSpec(memory_space=pltpu.SMEM)
-ANY_SPEC = pl.BlockSpec(memory_space=pl.ANY)
+HBM_SPEC = pl.BlockSpec(memory_space=pltpu.HBM)
 
 
 def whole_call(kernel, outs, flops, *args):
@@ -411,45 +412,52 @@
             slot = (i + 1) % 2
             fetch(where_ref[i + 2], sources, buffers.at[slot], sems.at[slot], True)
         fetch(where_ref[i + 1], sources, buffers.at[i % 2], sems.at[i % 2], False)
-        weight = buffers[i % 2]
         for ref, start in ((own_ref, own_start), (far_ref, far_start)):
-            product = jnp.dot(ref[...], weight, preferred_element_type=F32)
-            if len(outs) == 1:
-                outs[0][i, pl.ds(start, tokens), :] = product.astype(outs[0].dtype)
-            else:
-                outs[i][pl.ds(start, tokens), :] = product.astype(outs[i].dtype)
+
+            @pl.loop(0, tokens, step=ROWS)
+            def _(row):
+                row = pl.multiple_of(row, ROWS)
+                product = jnp.dot(
+                    ref[pl.ds(row, ROWS), :], buffers[i % 2], preferred_element_type=F32
+                )
+                if len(outs) == 1:
+                    outs[0][i, pl.ds(start + row, ROWS), :] = product.astype(outs[0].dtype)
+                else:
+                    outs[i][pl.ds(start + row, ROWS), :] = product.astype(outs[i].dtype)
 
 
 def in_kernel(count, where_ref, hidden_ref, *refs):
     sources, (out_ref, buffers, total, sems) = refs[:7], refs[7:]
     rows = out_ref.shape[0]
-    window = pl.ds(pl.multiple_of(where_ref[0], HALO), rows)
     fetch(where_ref[1], sources, buffers.at[0], sems.at[0], True)
     for i in range(count):
         if i + 1 < count:
             slot = (i + 1) % 2
             fetch(where_ref[i + 2], sources, buffers.at[slot], sems.at[slot], True)
         fetch(where_ref[i + 1], sources, buffers.at[i % 2], sems.at[i % 2], False)
-        hidden = hidden_ref[i, window, :]
-        depth = hidden.shape[1]
-        large = jnp.dot(hidden, buffers[i % 2, :depth, :], preferred_element_type=F32)
+        depth, wide = hidden_ref.shape[2], buffers.shape[2]
         packed = buffers[i % 2, depth:, :]
-        small = lax.dot_general(
-            hidden,
-            jnp.concatenate([packed[:, :depth], packed[:, depth:]], axis=0),
-            (((1,), (1,)), ((), ())),
-            preferred_element_type=F32,
-        )[:, : out_ref.shape[1] - large.shape[1]]
-        for part, columns in (
-            (large, slice(0, large.shape[1])),
-            (small, slice(large.shape[1], out_ref.shape[1])),
-        ):
-            if i == 0:
-                total[:, columns] = part
-            elif i + 1 < count:
-                total[:, columns] += part
-            else:
-                out_ref[:, columns] = (total[:, columns] + part).astype(out_ref.dtype)
+        below = jnp.concatenate([packed[:, :depth], packed[:, depth:]], axis=0)
+
+        @pl.loop(0, rows, step=rows // 3)
+        def _(row):
+            here = pl.ds(pl.multiple_of(row, HALO), rows // 3)
+            there = pl.ds(pl.multiple_of(where_ref[0] + row, HALO), rows // 3)
+            hidden = hidden_ref[i, there, :]
+            large = jnp.dot(hidden, buffers[i % 2, :depth, :], preferred_element_type=F32)
+            small = lax.dot_general(
+                hidden, below, (((1,), (1,)), ((), ())), preferred_element_type=F32
+            )[:, : out_ref.shape[1] - wide]
+            for part, columns in (
+                (large, slice(0, wide)),
+                (small, slice(wide, out_ref.shape[1])),
+            ):
+                if i == 0:
+                    total[here, columns] = part
+                elif i + 1 < count:
+                    total[here, columns] += part
+                else:
+                    out_ref[here, columns] = (total[here, columns] + part).astype(out_ref.dtype)
 
 
 def out_call(where, own, far, sources, outs):
@@ -459,7 +467,7 @@
     return pl.pallas_call(
         functools.partial(out_kernel, count),
         out_shape=outs,
-        in_specs=[SMEM_SPEC, VMEM_SPEC, VMEM_SPEC] + [ANY_SPEC] * len(sources),
+        in_specs=[SMEM_SPEC, VMEM_SPEC, VMEM_SPEC] + [HBM_SPEC] * len(sources),
         out_specs=[VMEM_SPEC] * len(outs),
         scratch_shapes=[pltpu.VMEM((2,) + block, BF16), pltpu.SemaphoreType.DMA((2,))],
         cost_estimate=pl.CostEstimate(
@@ -477,7 +485,7 @@
     return pl.pallas_call(
         functools.partial(in_kernel, count),
         out_shape=shape((rows, columns), kind),
-        in_specs=[SMEM_SPEC, VMEM_SPEC] + [ANY_SPEC] * len(sources),
+        in_specs=[SMEM_SPEC, VMEM_SPEC] + [HBM_SPEC] * len(sources),
         out_specs=VMEM_SPEC,
         scratch_shapes=[
             pltpu.VMEM((2,) + block, BF16),

time: 372 us -> 376 us (1.011)
  Pallas kernels: 60.4 us -> 65 us
where the time goes in v1:
time: 376 us; the launch traced here: 374 us
  waiting for transfers between devices  222 us (59%)
  Pallas kernels  65 us (17%)
  starting transfers between devices  47.6 us (13%)
  other arithmetic  18.2 us (5%)
  local copies, waits for them, and re-layouts  14.1 us (4%)
  blocking collectives  5.64 us (2%)
    ppermute x18, waiting for transfers between devices, flip(): return lax.ppermute(value, axis, [(i, i ^ bit) for i in range(n)])  115 us
    ppermute x18, waiting for transfers between devices, z_shift(): return lax.ppermute(value, 'seq', pairs)  108 us
    ppermute x18, starting transfers between devices, z_shift(): return lax.ppermute(value, 'seq', pairs)  37.9 us
    pallas_call x8, Pallas kernels, whole_call(): pl.pallas_call(kernel, out_shape=outs, in_specs=[SMEM_SPEC if a.shape ==...  22 us
    pallas_call x2, Pallas kernels, in_call(): pl.pallas_call(functools.partial(in_kernel, count), out_shape=shape((rows...  18.4 us
    pallas_call x2, Pallas kernels, out_call(): pl.pallas_call(functools.partial(out_kernel, count), out_shape=outs, in_s...  14 us
    ppermute x18, starting transfers between devices, flip(): return lax.ppermute(value, axis, [(i, i ^ bit) for i in range(n)])  9.73 us
    unnamed x64, local copies, waits for them, and re-layouts  8.16 us
  transfers between devices with their start and end apart: 36, of which 22 were waited for; matrix products, arithmetic and copies ran while one was open for 6% of the time, Pallas kernels for 10%

profile of v1, /device:TPU:28, one launch (start us, length us, event | category | flops | bytes accessed | tf_op | source)
XLA Modules:
  0.0 374.3 jit_solution(15766707540072139070)
XLA Ops:
  8.0 17.9 %collective-permute-done.5.refs_2_ = bf16[1024,512]{1,0:T(8,128)(2,1)S(1)} collective-permute-done((bf16[1024,512]{1,0:T(8,128)(2,1)}, bf16[1024,512]{1,0:T(8,128)(2,1)S(1)}, u32[]{:S(2)}, u32[]{:S(2)}) %collective-permute-start.5) | collective-permute-done | bytes 1048608 | tf_op jit(solution)/shard_map/ppermute | solution.py:20
  25.9 5.3 %collective-permute-start.6 = (bf16[1024,512]{1,0:T(8,128)(2,1)S(1)}, bf16[1024,512]{1,0:T(8,128)(2,1)}, u32[]{:S(2)}, u32[]{:S(2)}) collective-permute-start(bf16[1024,512]{1,0:T(8,128)(2,1)S(1)} %collective-permute-done.5.refs_2_), channel_id=1, source_target_pairs={{8,0},{12,4},{16,8},{20,12},{24,16},{28,20},{9,1},{13,5},{17,9},{2... | collective-permute-start | bytes 3145736 | tf_op jit(solution)/shard_map/ppermute | solution.py:20
  40.3 7.4 %collective-permute-done.1.far_ref = bf16[144,1024]{1,0:T(8,128)(2,1)} collective-permute-done((bf16[144,1024]{1,0:T(8,128)(2,1)}, bf16[144,1024]{1,0:T(8,128)(2,1)}, u32[]{:S(2)}, u32[]{:S(2)}) %collective-permute-start.1) | collective-permute-done | bytes 294944 | tf_op jit(solution)/shard_map/ppermute | solution.py:25
  50.2 12.9 %collective-permute-done.2.far_ref = bf16[144,1024]{1,0:T(8,128)(2,1)S(1)} collective-permute-done((bf16[144,1024]{1,0:T(8,128)(2,1)S(1)}, bf16[144,1024]{1,0:T(8,128)(2,1)S(1)}, u32[]{:S(2)}, u32[]{:S(2)}) %collective-permute-start.2) | collective-permute-done | bytes 294944 | tf_op jit(solution)/shard_map/ppermute | solution.py:20
  70.1 8.8 %collective-permute-done.3.far_ref = bf16[144,1024]{1,0:T(8,128)(2,1)S(1)} collective-permute-done((bf16[144,1024]{1,0:T(8,128)(2,1)S(1)}, bf16[144,1024]{1,0:T(8,128)(2,1)S(1)}, u32[]{:S(2)}, u32[]{:S(2)}) %collective-permute-start.3) | collective-permute-done | bytes 294944 | tf_op jit(solution)/shard_map/ppermute | solution.py:20
  79.8 5.9 %shard_map.179 = (bf16[512,1024]{1,0:T(8,128)(2,1)}, f32[1,512]{1,0:T(1,128)S(1)}) custom-call(s32[1]{0:T(128)} %bitcast.y_ref, f32[128,1024]{1,0:T(8,128)S(1)} %get-tuple-element.33.early_ref, f32[1,1024]{1,0:T(1,128)S(1)} %get-tuple-element.34.early_decay_ref, f32[128,1024]{1,0:T(8,128)S(1)} %get-tuple-element.37.before_ref, ...), custom_call_target="tpu_custom_call" | custom-call | flops 268435456 | bytes 6240324 | tf_op jit(solution)/shard_map/pallas_call | solution.py:291
  89.9 21.1 %collective-permute-done.4.far_ref = bf16[512,1024]{1,0:T(8,128)(2,1)} collective-permute-done((bf16[512,1024]{1,0:T(8,128)(2,1)}, bf16[512,1024]{1,0:T(8,128)(2,1)}, u32[]{:S(2)}, u32[]{:S(2)}) %collective-permute-start.4) | collective-permute-done | bytes 1048608 | tf_op jit(solution)/shard_map/ppermute | solution.py:25
  115.5 7.7 %shard_map.181 = bf16[2,1024,512]{2,1,0:T(8,128)(2,1)} custom-call(s32[3]{0:T(128)S(1)} %pad_add_fusion.1.where_ref, bf16[512,1024]{1,0:T(8,128)(2,1)} %get-tuple-element.41.own_ref, bf16[512,1024]{1,0:T(8,128)(2,1)} %collective-permute-done.4.far_ref, bf16[1024,512]{1,0:T(8,128)(2,1)} %collective-permute-done.7.refs_0_, ...), custom_call_target="tpu_custom_call" | custom-call | flops 2147483648 | bytes 4194304 | tf_op jit(solution)/shard_map/pallas_call | solution.py:467
  126.8 6.3 %shard_map.180 = (f32[1024,512]{1,0:T(8,128)S(1)}, f32[1024,512]{1,0:T(8,128)S(1)}) custom-call(s32[3]{0:T(128)S(1)} %pad_add_fusion.where_ref, bf16[512,1024]{1,0:T(8,128)(2,1)} %get-tuple-element.41.own_ref, bf16[512,1024]{1,0:T(8,128)(2,1)} %collective-permute-done.4.far_ref, bf16[1024,512]{1,0:T(8,128)(2,1)} %collective-permute-done.7.refs_0_, ...), custom_call_target="tpu_custom_call" | custom-call | flops 2147483648 | bytes 4194304 | tf_op jit(solution)/shard_map/pallas_call | solution.py:467
  139.7 22.4 %collective-permute-done.14 = f32[1,512]{1,0:T(1,128)S(1)} collective-permute-done((f32[1,512]{1,0:T(1,128)S(1)}, f32[1,512]{1,0:T(1,128)S(1)}, u32[]{:S(2)}, u32[]{:S(2)}) %collective-permute-start.14) | collective-permute-done | bytes 2080 | tf_op jit(solution)/shard_map/ppermute | solution.py:25
  174.3 18.6 %collective-permute-done.17 = bf16[1024,512]{1,0:T(8,128)(2,1)} collective-permute-done((bf16[1024,512]{1,0:T(8,128)(2,1)}, bf16[1024,512]{1,0:T(8,128)(2,1)}, u32[]{:S(2)}, u32[]{:S(2)}) %collective-permute-start.17) | collective-permute-done | bytes 1048608 | tf_op jit(solution)/shard_map/ppermute | solution.py:25
  194.7 5.5 %collective-permute-start.21 = (bf16[560,1024]{1,0:T(8,128)(2,1)S(1)}, bf16[560,1024]{1,0:T(8,128)(2,1)}, u32[]{:S(2)}, u32[]{:S(2)}) collective-permute-start(bf16[560,1024]{1,0:T(8,128)(2,1)S(1)} %collective-permute-done.20.refs_2_), channel_id=1, source_target_pairs={{8,0},{12,4},{16,8},{20,12},{24,16},{28,20},{9,1},{13,5},{17,9},{2... | collective-permute-start | bytes 3440648 | tf_op jit(solution)/shard_map/ppermute | solution.py:20
  201.4 19.9 %collective-permute-done.21.refs_1_ = bf16[560,1024]{1,0:T(8,128)(2,1)} collective-permute-done((bf16[560,1024]{1,0:T(8,128)(2,1)S(1)}, bf16[560,1024]{1,0:T(8,128)(2,1)}, u32[]{:S(2)}, u32[]{:S(2)}) %collective-permute-start.21) | collective-permute-done | bytes 1146912 | tf_op jit(solution)/shard_map/ppermute | solution.py:20
  221.3 5.5 %collective-permute-start.22 = (bf16[560,1024]{1,0:T(8,128)(2,1)}, bf16[560,1024]{1,0:T(8,128)(2,1)}, u32[]{:S(2)}, u32[]{:S(2)}) collective-permute-start(bf16[560,1024]{1,0:T(8,128)(2,1)} %collective-permute-done.21.refs_1_), channel_id=1, source_target_pairs={{8,0},{12,4},{16,8},{20,12},{24,16},{28,20},{9,1},{13,5},{17,9},{2... | collective-permute-start | bytes 3440648 | tf_op jit(solution)/shard_map/ppermute | solution.py:20
  232.0 22.0 %collective-permute-done.19 = bf16[4,16,512]{2,1,0:T(8,128)(2,1)S(1)} collective-permute-done((bf16[4,16,512]{2,1,0:T(8,128)(2,1)}, bf16[4,16,512]{2,1,0:T(8,128)(2,1)S(1)}, u32[]{:S(2)}, u32[]{:S(2)}) %collective-permute-start.19) | collective-permute-done | bytes 65568 | tf_op jit(solution)/shard_map/ppermute | solution.py:20
  256.4 9.2 %shard_map.183 = bf16[528,1104]{1,0:T(8,128)(2,1)} custom-call(s32[5]{0:T(128)S(1)} %stack.92.where_ref, bf16[4,1040,512]{2,1,0:T(8,128)(2,1)S(1)} %maximum_maximum_fusion.hidden_ref, bf16[560,1024]{1,0:T(8,128)(2,1)} %collective-permute-done.22.refs_0_, bf16[560,1024]{1,0:T(8,128)(2,1)} %collective-permute-done.21.refs_1_, ...), custom_call_target="tpu_custom_call" | custom-call | flops 2214592512 | bytes 8847360 | tf_op jit(solution)/shard_map/pallas_call | solution.py:485
  272.5 17.9 %collective-permute-done.29 = f32[1024]{0:T(1024)S(1)} collective-permute-done((f32[1024]{0:T(1024)S(1)}, f32[1024]{0:T(1024)S(1)}, u32[]{:S(2)}, u32[]{:S(2)}) %collective-permute-start.29) | collective-permute-done | bytes 4128 | tf_op jit(solution)/shard_map/ppermute | solution.py:25
  296.2 9.2 %shard_map.182.mine_ref = f32[528,1104]{1,0:T(8,128)S(1)} custom-call(s32[5]{0:T(128)S(1)} %stack.86.where_ref, bf16[4,1040,512]{2,1,0:T(8,128)(2,1)} %copy-done.2, bf16[560,1024]{1,0:T(8,128)(2,1)} %collective-permute-done.22.refs_0_, bf16[560,1024]{1,0:T(8,128)(2,1)} %collective-permute-done.21.refs_1_, ...), custom_call_target="tpu_custom_call" | custom-call | flops 2214592512 | bytes 8847360 | tf_op jit(solution)/shard_map/pallas_call | solution.py:485
  309.3 5.0 %collective-permute-done.31 = bf16[512,64]{1,0:T(8,128)(2,1)S(1)} collective-permute-done((bf16[512,64]{1,0:T(8,128)(2,1)S(1)}, bf16[512,64]{1,0:T(8,128)(2,1)S(1)}, u32[]{:S(2)}, u32[]{:S(2)}) %collective-permute-start.31) | collective-permute-done | bytes 65568 | tf_op jit(solution)/shard_map/ppermute | solution.py:25
  321.0 14.3 %collective-permute-done.33.far_ref = bf16[144,1024]{1,0:T(8,128)(2,1)S(1)} collective-permute-done((bf16[144,1024]{1,0:T(8,128)(2,1)S(1)}, bf16[144,1024]{1,0:T(8,128)(2,1)S(1)}, u32[]{:S(2)}, u32[]{:S(2)}) %collective-permute-start.33) | collective-permute-done | bytes 294944 | tf_op jit(solution)/shard_map/ppermute | solution.py:25
  338.4 7.6 %collective-permute-done.34.far_ref = bf16[144,1024]{1,0:T(8,128)(2,1)S(1)} collective-permute-done((bf16[144,1024]{1,0:T(8,128)(2,1)S(1)}, bf16[144,1024]{1,0:T(8,128)(2,1)S(1)}, u32[]{:S(2)}, u32[]{:S(2)}) %collective-permute-start.34) | collective-permute-done | bytes 294944 | tf_op jit(solution)/shard_map/ppermute | solution.py:20
  352.9 9.8 %collective-permute-done.35.far_ref = bf16[144,1024]{1,0:T(8,128)(2,1)S(1)} collective-permute-done((bf16[144,1024]{1,0:T(8,128)(2,1)S(1)}, bf16[144,1024]{1,0:T(8,128)(2,1)S(1)}, u32[]{:S(2)}, u32[]{:S(2)}) %collective-permute-start.35) | collective-permute-done | bytes 294944 | tf_op jit(solution)/shard_map/ppermute | solution.py:20
  362.8 4.7 %shard_map.187 = (f32[512,1024]{1,0:T(8,128)S(1)}, f32[1,512]{1,0:T(1,128)S(1)}) custom-call(s32[1]{0:T(128)} %bitcast.y_ref, f32[128,1024]{1,0:T(8,128)S(1)} %get-tuple-element.50.early_ref, f32[1,1024]{1,0:T(1,128)S(1)} %get-tuple-element.51.early_decay_ref, f32[128,1024]{1,0:T(8,128)S(1)} %get-tuple-element.54.before_ref, ...), custom_call_target="tpu_custom_call" | custom-call | flops 268435456 | bytes 6236228 | tf_op jit(solution)/shard_map/pallas_call | solution.py:291
  367.5 5.6 %psum.7 = f32[512]{0:T(512)S(1)} all-reduce(f32[512]{0:T(512)S(1)} %bitcast.53), channel_id=1, replica_groups=mesh['seq'=8,'head'=4] {'head'}, use_global_device_ids=true, to_apply=%region_1.2 | all-reduce | flops 512 | bytes 4096 | tf_op jit(solution)/shard_map/psum | solution.py:734
  (175 shorter events, 102.4 us)
Async XLA Ops:
  0.6 25.2 %collective-permute-start.5 = (bf16[1024,512]{1,0:T(8,128)(2,1)}, bf16[1024,512]{1,0:T(8,128)(2,1)S(1)}, u32[]{:S(2)}, u32[]{:S(2)}) collective-permute-start(bf16[1024,512]{1,0:T(8,128)(2,1)} %refs_3_.3), channel_id=1, source_target_pairs={{8,0},{12,4},{16,8},{20,12},{24,16},{28,20},{9,1},{13,5},{17,9},{2... | collective-permute-start | bytes 3145736 | tf_op jit(solution)/shard_map/ppermute | solution.py:20
  3.2 27.9 %collective-permute-start.8 = (bf16[1024,512]{1,0:T(8,128)(2,1)}, bf16[1024,512]{1,0:T(8,128)(2,1)S(1)}, u32[]{:S(2)}, u32[]{:S(2)}) collective-permute-start(bf16[1024,512]{1,0:T(8,128)(2,1)} %refs_3_.3), channel_id=1, source_target_pairs={{0,8},{4,12},{8,16},{12,20},{16,24},{20,28},{1,9},{5,13},{9,17},{1... | collective-permute-start | bytes 3145736 | tf_op jit(solution)/shard_map/ppermute | solution.py:20
  25.9 60.3 %collective-permute-start.6 = (bf16[1024,512]{1,0:T(8,128)(2,1)S(1)}, bf16[1024,512]{1,0:T(8,128)(2,1)}, u32[]{:S(2)}, u32[]{:S(2)}) collective-permute-start(bf16[1024,512]{1,0:T(8,128)(2,1)S(1)} %collective-permute-done.5.refs_2_), channel_id=1, source_target_pairs={{8,0},{12,4},{16,8},{20,12},{24,16},{28,20},{9,1},{13,5},{17,9},{2... | collective-permute-start | bytes 3145736 | tf_op jit(solution)/shard_map/ppermute | solution.py:20
  31.2 57.4 %collective-permute-start.9 = (bf16[1024,512]{1,0:T(8,128)(2,1)S(1)}, bf16[1024,512]{1,0:T(8,128)(2,1)}, u32[]{:S(2)}, u32[]{:S(2)}) collective-permute-start(bf16[1024,512]{1,0:T(8,128)(2,1)S(1)} %collective-permute-done.8.refs_4_), channel_id=1, source_target_pairs={{0,8},{4,12},{8,16},{12,20},{16,24},{20,28},{1,9},{5,13},{9,17},{1... | collective-permute-start | bytes 3145736 | tf_op jit(solution)/shard_map/ppermute | solution.py:20
  85.7 25.4 %collective-permute-start.4 = (bf16[512,1024]{1,0:T(8,128)(2,1)}, bf16[512,1024]{1,0:T(8,128)(2,1)}, u32[]{:S(2)}, u32[]{:S(2)}) collective-permute-start(bf16[512,1024]{1,0:T(8,128)(2,1)} %get-tuple-element.41.own_ref), channel_id=1, source_target_pairs={{0,4},{4,0},{8,12},{12,8},{16,20},{20,16},{24,28},{28,24},{1,5},{5... | collective-permute-start | bytes 3145736 | tf_op jit(solution)/shard_map/ppermute | solution.py:25
  86.2 24.9 %collective-permute-start.7 = (bf16[1024,512]{1,0:T(8,128)(2,1)}, bf16[1024,512]{1,0:T(8,128)(2,1)}, u32[]{:S(2)}, u32[]{:S(2)}) collective-permute-start(bf16[1024,512]{1,0:T(8,128)(2,1)} %collective-permute-done.6.refs_1_), channel_id=1, source_target_pairs={{8,0},{12,4},{16,8},{20,12},{24,16},{28,20},{9,1},{13,5},{17,9},{2... | collective-permute-start | bytes 3145736 | tf_op jit(solution)/shard_map/ppermute | solution.py:20
  88.5 27.0 %collective-permute-start.10 = (bf16[1024,512]{1,0:T(8,128)(2,1)}, bf16[1024,512]{1,0:T(8,128)(2,1)}, u32[]{:S(2)}, u32[]{:S(2)}) collective-permute-start(bf16[1024,512]{1,0:T(8,128)(2,1)} %collective-permute-done.9.refs_5_), channel_id=1, source_target_pairs={{0,8},{4,12},{8,16},{12,20},{16,24},{20,28},{1,9},{5,13},{9,17},{1... | collective-permute-start | bytes 3145736 | tf_op jit(solution)/shard_map/ppermute | solution.py:20
  125.2 37.5 %collective-permute-start = (bf16[512,512]{1,0:T(8,128)(2,1)}, bf16[512,512]{1,0:T(8,128)(2,1)}, u32[]{:S(2)}, u32[]{:S(2)}) collective-permute-start(bf16[512,512]{1,0:T(8,128)(2,1)} %constant_dynamic-slice_fusion.4), channel_id=1, source_target_pairs={{0,4},{4,0},{8,12},{12,8},{16,20},{20,16},{24,28},{28,24},{1,5},{5... | collective-permute-start | bytes 1572872 | tf_op jit(solution)/shard_map/ppermute | solution.py:25
  136.5 29.2 %collective-permute-start.12 = (bf16[1024,512]{1,0:T(8,128)(2,1)}, bf16[1024,512]{1,0:T(8,128)(2,1)}, u32[]{:S(2)}, u32[]{:S(2)}) collective-permute-start(bf16[1024,512]{1,0:T(8,128)(2,1)} %fusion.2), channel_id=1, source_target_pairs={{0,2},{1,3},{2,0},{3,1},{4,6},{5,7},{6,4},{7,5},{8,10},{9,11},{10,... | collective-permute-start | bytes 3145736 | tf_op jit(solution)/shard_map/ppermute | solution.py:25
  137.7 24.4 %collective-permute-start.14 = (f32[1,512]{1,0:T(1,128)S(1)}, f32[1,512]{1,0:T(1,128)S(1)}, u32[]{:S(2)}, u32[]{:S(2)}) collective-permute-start(f32[1,512]{1,0:T(1,128)S(1)} %add.120), channel_id=1, source_target_pairs={{0,2},{1,3},{2,0},{3,1},{4,6},{5,7},{6,4},{7,5},{8,10},{9,11},{10,... | collective-permute-start | bytes 6152 | tf_op jit(solution)/shard_map/ppermute | solution.py:25
  169.3 23.6 %collective-permute-start.17 = (bf16[1024,512]{1,0:T(8,128)(2,1)}, bf16[1024,512]{1,0:T(8,128)(2,1)}, u32[]{:S(2)}, u32[]{:S(2)}) collective-permute-start(bf16[1024,512]{1,0:T(8,128)(2,1)} %fusion), channel_id=1, source_target_pairs={{0,2},{1,3},{2,0},{3,1},{4,6},{5,7},{6,4},{7,5},{8,10},{9,11},{10,... | collective-permute-start | bytes 3145736 | tf_op jit(solution)/shard_map/ppermute | solution.py:25
  170.2 24.5 %collective-permute-start.20 = (bf16[560,1024]{1,0:T(8,128)(2,1)S(1)}, bf16[560,1024]{1,0:T(8,128)(2,1)S(1)}, u32[]{:S(2)}, u32[]{:S(2)}) collective-permute-start(bf16[560,1024]{1,0:T(8,128)(2,1)S(1)} %maximum_maximum_fusion.1.refs_3_), channel_id=1, source_target_pairs={{8,0},{12,4},{16,8},{20,12},{24,16},{28,20},{9,1},{13,5},{17,9},{2... | collective-permute-start | bytes 3440648 | tf_op jit(solution)/shard_map/ppermute | solution.py:20
  171.6 28.6 %collective-permute-start.23 = (bf16[560,1024]{1,0:T(8,128)(2,1)S(1)}, bf16[560,1024]{1,0:T(8,128)(2,1)S(1)}, u32[]{:S(2)}, u32[]{:S(2)}) collective-permute-start(bf16[560,1024]{1,0:T(8,128)(2,1)S(1)} %maximum_maximum_fusion.1.refs_3_), channel_id=1, source_target_pairs={{0,8},{4,12},{8,16},{12,20},{16,24},{20,28},{1,9},{5,13},{9,17},{1... | collective-permute-start | bytes 3440648 | tf_op jit(solution)/shard_map/ppermute | solution.py:20
  194.3 33.8 %collective-permute-start.18 = (bf16[2,1024,512]{2,1,0:T(8,128)(2,1)S(1)}, bf16[2,1024,512]{2,1,0:T(8,128)(2,1)S(1)}, u32[]{:S(2)}, u32[]{:S(2)}) collective-permute-start(bf16[2,1024,512]{2,1,0:T(8,128)(2,1)S(1)} %pad_maximum_fusion), channel_id=1, source_target_pairs={{0,1},{1,0},{2,3},{3,2},{4,5},{5,4},{6,7},{7,6},{8,9},{9,8},{10,11... | collective-permute-start | bytes 6291464 | tf_op jit(solution)/shard_map/ppermute | solution.py:25
  194.7 26.7 %collective-permute-start.21 = (bf16[560,1024]{1,0:T(8,128)(2,1)S(1)}, bf16[560,1024]{1,0:T(8,128)(2,1)}, u32[]{:S(2)}, u32[]{:S(2)}) collective-permute-start(bf16[560,1024]{1,0:T(8,128)(2,1)S(1)} %collective-permute-done.20.refs_2_), channel_id=1, source_target_pairs={{8,0},{12,4},{16,8},{20,12},{24,16},{28,20},{9,1},{13,5},{17,9},{2... | collective-permute-start | bytes 3440648 | tf_op jit(solution)/shard_map/ppermute | solution.py:20
  200.1 26.7 %collective-permute-start.24 = (bf16[560,1024]{1,0:T(8,128)(2,1)S(1)}, bf16[560,1024]{1,0:T(8,128)(2,1)}, u32[]{:S(2)}, u32[]{:S(2)}) collective-permute-start(bf16[560,1024]{1,0:T(8,128)(2,1)S(1)} %collective-permute-done.23.refs_4_), channel_id=1, source_target_pairs={{0,8},{4,12},{8,16},{12,20},{16,24},{20,28},{1,9},{5,13},{9,17},{1... | collective-permute-start | bytes 3440648 | tf_op jit(solution)/shard_map/ppermute | solution.py:20
  221.3 35.0 %collective-permute-start.22 = (bf16[560,1024]{1,0:T(8,128)(2,1)}, bf16[560,1024]{1,0:T(8,128)(2,1)}, u32[]{:S(2)}, u32[]{:S(2)}) collective-permute-start(bf16[560,1024]{1,0:T(8,128)(2,1)} %collective-permute-done.21.refs_1_), channel_id=1, source_target_pairs={{8,0},{12,4},{16,8},{20,12},{24,16},{28,20},{9,1},{13,5},{17,9},{2... | collective-permute-start | bytes 3440648 | tf_op jit(solution)/shard_map/ppermute | solution.py:20
  226.8 29.6 %collective-permute-start.25 = (bf16[560,1024]{1,0:T(8,128)(2,1)}, bf16[560,1024]{1,0:T(8,128)(2,1)}, u32[]{:S(2)}, u32[]{:S(2)}) collective-permute-start(bf16[560,1024]{1,0:T(8,128)(2,1)} %collective-permute-done.24.refs_5_), channel_id=1, source_target_pairs={{0,8},{4,12},{8,16},{12,20},{16,24},{20,28},{1,9},{5,13},{9,17},{1... | collective-permute-start | bytes 3440648 | tf_op jit(solution)/shard_map/ppermute | solution.py:20
  230.6 23.4 %collective-permute-start.19 = (bf16[4,16,512]{2,1,0:T(8,128)(2,1)}, bf16[4,16,512]{2,1,0:T(8,128)(2,1)S(1)}, u32[]{:S(2)}, u32[]{:S(2)}) collective-permute-start(bf16[4,16,512]{2,1,0:T(8,128)(2,1)} %pad_maximum_fusion.7), channel_id=1, source_target_pairs={{0,8},{4,12},{8,16},{12,20},{16,24},{20,28},{1,9},{5,13},{9,17},{1... | collective-permute-start | bytes 196616 | tf_op jit(solution)/shard_map/ppermute | solution.py:20
  265.6 39.8 %collective-permute-start.26 = (bf16[528,1104]{1,0:T(8,128)(2,1)}, bf16[528,1104]{1,0:T(8,128)(2,1)}, u32[]{:S(2)}, u32[]{:S(2)}) collective-permute-start(bf16[528,1104]{1,0:T(8,128)(2,1)} %shard_map.183), channel_id=1, source_target_pairs={{0,4},{4,0},{8,12},{12,8},{16,20},{20,16},{24,28},{28,24},{1,5},{5... | collective-permute-start | bytes 3497480 | tf_op jit(solution)/shard_map/ppermute | solution.py:25
  271.2 19.3 %collective-permute-start.29 = (f32[1024]{0:T(1024)S(1)}, f32[1024]{0:T(1024)S(1)}, u32[]{:S(2)}, u32[]{:S(2)}) collective-permute-start(f32[1024]{0:T(1024)S(1)} %add.129), channel_id=1, source_target_pairs={{0,4},{4,0},{8,12},{12,8},{16,20},{20,16},{24,28},{28,24},{1,5},{5... | collective-permute-start | bytes 12296 | tf_op jit(solution)/shard_map/ppermute | solution.py:25
  314.7 22.2 %collective-permute-start.16 = (bf16[512,512]{1,0:T(8,128)(2,1)S(1)}, bf16[512,512]{1,0:T(8,128)(2,1)S(1)}, u32[]{:S(2)}, u32[]{:S(2)}) collective-permute-start(bf16[512,512]{1,0:T(8,128)(2,1)S(1)} %constant_dynamic-slice_fusion.3), channel_id=1, source_target_pairs={{0,4},{4,0},{8,12},{12,8},{16,20},{20,16},{24,28},{28,24},{1,5},{5... | collective-permute-start | bytes 1572872 | tf_op jit(solution)/shard_map/ppermute | solution.py:25
  320.1 15.2 %collective-permute-start.33 = (bf16[144,1024]{1,0:T(8,128)(2,1)S(1)}, bf16[144,1024]{1,0:T(8,128)(2,1)S(1)}, u32[]{:S(2)}, u32[]{:S(2)}) collective-permute-start(bf16[144,1024]{1,0:T(8,128)(2,1)S(1)} %get-tuple-element.49.own_ref), channel_id=1, source_target_pairs={{0,4},{4,0},{8,12},{12,8},{16,20},{20,16},{24,28},{28,24},{1,5},{5... | collective-permute-start | bytes 884744 | tf_op jit(solution)/shard_map/ppermute | solution.py:25
  346.8 15.9 %collective-permute-start.35 = (bf16[144,1024]{1,0:T(8,128)(2,1)S(1)}, bf16[144,1024]{1,0:T(8,128)(2,1)S(1)}, u32[]{:S(2)}, u32[]{:S(2)}) collective-permute-start(bf16[144,1024]{1,0:T(8,128)(2,1)S(1)} %get-tuple-element.56), channel_id=1, source_target_pairs={{0,16},{4,20},{8,24},{12,28},{1,17},{5,21},{9,25},{13,29},{2,18},{... | collective-permute-start | bytes 884744 | tf_op jit(solution)/shard_map/ppermute | solution.py:20
  (42 other events, 647.6 us)

commit v2 on v1

--- a/solution.py
+++ b/solution.py
@@ -294,7 +294,7 @@
         in_specs=[SMEM_SPEC if a.shape == (1,) else VMEM_SPEC for a in args],
         out_specs=[VMEM_SPEC] * len(outs),
         cost_estimate=pl.CostEstimate(flops=flops, bytes_accessed=moved, transcendentals=0),
-        compiler_params=pltpu.CompilerParams(vmem_limit_bytes=48 * 2**20),
+        compiler_params=pltpu.CompilerParams(vmem_limit_bytes=16 * 2**20),
     )(*args)
 
 
@@ -335,57 +335,61 @@
         cost_estimate=pl.CostEstimate(
             flops=16 * x.size * GROUP, bytes_accessed=8 * x.size, transcendentals=0
         ),
-        compiler_params=pltpu.CompilerParams(vmem_limit_bytes=32 * 2**20),
+        compiler_params=pltpu.CompilerParams(vmem_limit_bytes=12 * 2**20),
     )(x, bc, step, code, rate, skip)
 
 
-def conv_kernel(mine_ref, far_ref, scale_ref, taps_ref, bias_ref, x_ref, bc_ref, step_ref, pre_ref):
-    rows = mine_ref.shape[0]
+def convolved(mine_ref, far_ref, scale, taps_ref, pre_ref, start, size, tokens):
+    rows, count = mine_ref.shape[0], taps_ref.shape[0]
+    columns = pl.ds(start, size)
+    pre = (mine_ref[:, columns] + far_ref[:, columns].astype(F32)) * scale
+    pre_ref[:, :size] = pre.astype(BF16).astype(F32)
+    total = None
+    for tap in range(count):
+        first = rows - tokens - count + 1 + tap
+        part = pre_ref[pl.ds(first, tokens), :size] * taps_ref[tap : tap + 1, columns]
+        total = part if total is None else total + part
+    return (total / (1.0 + jnp.exp(-total))).astype(BF16)
+
+
+def conv_kernel(mine_ref, far_ref, scale_ref, taps_ref, *refs):
+    if len(refs) == 2:
+        x_ref, pre_ref = refs
+    else:
+        bias_ref, x_ref, bc_ref, step_ref, late_ref, pre_ref = refs
     tokens, width = x_ref.shape
-    share = bc_ref.shape[1]
     scale = scale_ref[...]
-    count = taps_ref.shape[0]
-
-    def convolved(start, size):
-        columns = pl.ds(start, size)
-        pre = (mine_ref[:, columns] + far_ref[:, columns].astype(F32)) * scale
-        pre_ref[:, :size] = pre.astype(BF16).astype(F32)
-        total = None
-        for tap in range(count):
-            first = rows - tokens - count + 1 + tap
-            part = pre_ref[pl.ds(first, tokens), :size] * taps_ref[tap : tap + 1, columns]
-            total = part if total is None else total + part
-        return (total / (1.0 + jnp.exp(-total))).astype(BF16)
-
-    for start in range(0, width, 128):
-        x_ref[:, pl.ds(start, 128)] = convolved(start, 128)
-    bc_ref[...] = convolved(width, share)
-    heads = step_ref.shape[1]
-    columns = pl.ds(width + share, heads)
-    raw = (mine_ref[:, columns] + far_ref[:, columns].astype(F32)) * scale
-    raw = raw[rows - tokens :] + bias_ref[...]
-    step_ref[...] = jnp.maximum(raw, 0.0) + jnp.log1p(jnp.exp(-jnp.abs(raw)))
-
-
-def conv_call(mine, far, scale, taps, bias, tokens, width, share):
-    rows = mine.shape[0]
-    heads = bias.shape[1]
+
+    @pl.loop(0, width, step=128)
+    def _(start):
+        start = pl.multiple_of(start, 128)
+        x_ref[:, pl.ds(start, 128)] = convolved(
+            mine_ref, far_ref, scale, taps_ref, pre_ref, start, 128, tokens
+        )
+
+    if len(refs) > 2:
+        share, heads = bc_ref.shape[1], step_ref.shape[1]
+        bc_ref[...] = convolved(mine_ref, far_ref, scale, taps_ref, pre_ref, width, share, tokens)
+        columns = pl.ds(width + share, 2 * heads)
+        raw = (mine_ref[:, columns] + far_ref[:, columns].astype(F32)) * scale
+        raw = raw[mine_ref.shape[0] - tokens :] + bias_ref[...]
+        steps = jnp.maximum(raw, 0.0) + jnp.log1p(jnp.exp(-jnp.abs(raw)))
+        step_ref[...] = steps[:, :heads]
+        late_ref[...] = steps[:, heads:]
+
+
+def conv_call(outs, mine, *args):
     return pl.pallas_call(
         conv_kernel,
-        name="conv",
-        out_shape=[
-            shape((tokens, width), BF16),
-            shape((tokens, share), BF16),
-            shape((tokens, heads), F32),
-        ],
-        in_specs=[VMEM_SPEC] * 5,
-        out_specs=[VMEM_SPEC] * 3,
-        scratch_shapes=[pltpu.VMEM((rows, 128), F32)],
+        out_shape=outs,
+        in_specs=[VMEM_SPEC] * (1 + len(args)),
+        out_specs=[VMEM_SPEC] * len(outs),
+        scratch_shapes=[pltpu.VMEM((mine.shape[0], 128), F32)],
         cost_estimate=pl.CostEstimate(
             flops=16 * mine.size, bytes_accessed=8 * mine.size, transcendentals=mine.size
         ),
-        compiler_params=pltpu.CompilerParams(vmem_limit_bytes=32 * 2**20),
-    )(mine, far, scale, taps, bias)
+        compiler_params=pltpu.CompilerParams(vmem_limit_bytes=12 * 2**20),
+    )(mine, *args)
 
 
 def fetch(spot, sources, buffer, sem, start):
@@ -426,7 +430,7 @@
                     outs[i][pl.ds(start + row, ROWS), :] = product.astype(outs[i].dtype)
 
 
-def in_kernel(count, where_ref, hidden_ref, *refs):
+def in_kernel(count, place, where_ref, hidden_ref, *refs):
     sources, (out_ref, buffers, total, sems) = refs[:7], refs[7:]
     rows = out_ref.shape[0]
     fetch(where_ref[1], sources, buffers.at[0], sems.at[0], True)
@@ -435,7 +439,7 @@
             slot = (i + 1) % 2
             fetch(where_ref[i + 2], sources, buffers.at[slot], sems.at[slot], True)
         fetch(where_ref[i + 1], sources, buffers.at[i % 2], sems.at[i % 2], False)
-        depth, wide = hidden_ref.shape[2], buffers.shape[2]
+        depth, wide = hidden_ref.shape[2], buffers.shape[2] // 2
         packed = buffers[i % 2, depth:, :]
         below = jnp.concatenate([packed[:, :depth], packed[:, depth:]], axis=0)
 
@@ -444,14 +448,14 @@
             here = pl.ds(pl.multiple_of(row, HALO), rows // 3)
             there = pl.ds(pl.multiple_of(where_ref[0] + row, HALO), rows // 3)
             hidden = hidden_ref[i, there, :]
-            large = jnp.dot(hidden, buffers[i % 2, :depth, :], preferred_element_type=F32)
-            small = lax.dot_general(
-                hidden, below, (((1,), (1,)), ((), ())), preferred_element_type=F32
-            )[:, : out_ref.shape[1] - wide]
-            for part, columns in (
-                (large, slice(0, wide)),
-                (small, slice(wide, out_ref.shape[1])),
-            ):
+            weight = buffers[i % 2, :depth, place * wide : (place + 1) * wide]
+            products = [(jnp.dot(hidden, weight, preferred_element_type=F32), slice(0, wide))]
+            if out_ref.shape[1] > wide:
+                small = lax.dot_general(
+                    hidden, below, (((1,), (1,)), ((), ())), preferred_element_type=F32
+                )[:, : out_ref.shape[1] - wide]
+                products.append((small, slice(wide, out_ref.shape[1])))
+            for part, columns in products:
                 if i == 0:
                     total[here, columns] = part
                 elif i + 1 < count:
@@ -475,15 +479,15 @@
             bytes_accessed=4 * own.size + 2 * count * sources[0].size,
             transcendentals=0,
         ),
-        compiler_params=pltpu.CompilerParams(vmem_limit_bytes=32 * 2**20),
+        compiler_params=pltpu.CompilerParams(vmem_limit_bytes=60 * 2**20),
     )(where, own, far, *sources)
 
 
-def in_call(where, hidden, sources, rows, columns, kind):
+def in_call(place, where, hidden, sources, rows, columns, kind):
     count, _, depth = hidden.shape
     block = sources[0].shape
     return pl.pallas_call(
-        functools.partial(in_kernel, count),
+        functools.partial(in_kernel, count, place),
         out_shape=shape((rows, columns), kind),
         in_specs=[SMEM_SPEC, VMEM_SPEC] + [HBM_SPEC] * len(sources),
         out_specs=VMEM_SPEC,
@@ -497,7 +501,7 @@
             bytes_accessed=2 * hidden.size + 2 * count * sources[0].size,
             transcendentals=0,
         ),
-        compiler_params=pltpu.CompilerParams(vmem_limit_bytes=40 * 2**20),
+        compiler_params=pltpu.CompilerParams(vmem_limit_bytes=60 * 2**20),
     )(where, hidden, *sources)
 
 
@@ -682,57 +686,76 @@
     reach = tokens + HALO
     keep_start = jnp.where(first, 0, tokens)
     send_start = tokens - keep_start
+    columns = (half + small, half)
     if line:
         spots = [z - (head ^ k) for k in range(4)]
         where = lambda start: jnp.stack([start] + spots).astype(jnp.int32)
-        columns = width + small
-        theirs = in_call(where(send_start), all_hidden, in_blocks, reach, columns, BF16)
-        mine = in_call(where(keep_start), all_hidden, in_blocks, reach, columns, F32)
+        project = lambda place, start, kind: in_call(
+            place, where(start), all_hidden, in_blocks, reach, columns[place], kind
+        )
+        theirs = [project(0, send_start, BF16), project(1, send_start, BF16)]
+        mine = [project(0, keep_start, F32), project(1, keep_start, F32)]
     else:
         wide = jnp.concatenate([pick(all_hidden, head ^ i) for i in range(head_size)], axis=1)
         total = jnp.dot(
             wide, in_blocks.reshape(z_size * block, w_in.shape[1]), preferred_element_type=F32
         )
-        mine = lax.dynamic_slice_in_dim(total, keep_start, reach, 0)
-        theirs = lax.dynamic_slice_in_dim(total, send_start, reach, 0).astype(BF16)
-    scale_mine = lax.dynamic_slice_in_dim(scale_two, keep_start, reach, 0)
-    taps = jnp.concatenate(
-        [conv_x, lax.dynamic_slice_in_dim(conv_bc, head * share, share, 1)], axis=1
-    ).astype(F32)
-    x_two, bc_share, step_two = conv_call(
-        mine,
-        y_swap(theirs),
-        scale_mine[:, None],
+        total = [jnp.concatenate([total[:, :half], total[:, width:]], axis=1), total[:, half:width]]
+        mine = [lax.dynamic_slice_in_dim(t, keep_start, reach, 0) for t in total]
+        theirs = [lax.dynamic_slice_in_dim(t, send_start, reach, 0).astype(BF16) for t in total]
+    scale_mine = lax.dynamic_slice_in_dim(scale_two, keep_start, reach, 0)[:, None]
+    bc_taps = lax.dynamic_slice_in_dim(conv_bc, head * share, share, 1)
+    taps = jnp.concatenate([conv_x[:, :half], bc_taps], axis=1).astype(F32)
+    head_half = decay_code.shape[2] // 2
+    far_a = y_swap(theirs[0])
+    x_a, bc_share, step_a, step_b = conv_call(
+        [
+            shape((tokens, half), BF16),
+            shape((tokens, share), BF16),
+            shape((tokens, head_half), F32),
+            shape((tokens, head_half), F32),
+        ],
+        mine[0],
+        far_a,
+        scale_mine,
         taps,
         step_time_bias[None, :],
-        tokens,
-        width,
-        share,
+    )
+    (x_b,) = conv_call(
+        [shape((tokens, half), BF16)],
+        mine[1],
+        y_swap(theirs[1]),
+        scale_mine,
+        conv_x[:, half:].astype(F32),
     )
     bc_pair = jnp.stack([bc_share, x_swap(bc_share)])
     bc_other = c_swap(bc_pair)
     bc_stack = jnp.stack([bc_pair[0], bc_other[0], bc_pair[1], bc_other[1]])
     bc_two = jnp.concatenate([pick(bc_stack, head ^ i) for i in range(head_size)], axis=1)
 
-    code_two, rate_two = decay_code[1], decay_rate[1][None, :]
-    first_two, end_two, payload_two = chunk_states(
-        x_two, bc_two[:, :state_width], step_two, code_two, rate_two
-    )
-    within_two = within_blocks(x_two, bc_two, step_two, code_two, rate_two, skip_gain[1][None, :])
-    carried_two = exchange_states(end_two, payload_two, y)
-    mixed_two, square_last = whole_call(
-        last_kernel,
-        [shape((tokens, width), F32), shape((1, tokens), F32)],
-        4 * x_in.size * state_width,
-        *carried_two,
-        first_two,
-        within_two,
-        bc_two[:, state_width:],
-        code_two,
-        rate_two,
-    )
-    square_last = lax.psum(square_last[0], "head")
-    mixer_out = (mixed_two * lax.rsqrt(square_last / inner_count + 1e-05)[:, None]).astype(BF16)
+    mixed, squares = [], []
+    for x, step, picked in (
+        (x_a, step_a, slice(0, head_half)), (x_b, step_b, slice(head_half, None))
+    ):
+        code, rate = decay_code[1][:, picked], decay_rate[1][None, picked]
+        first_two, end, payload = chunk_states(x, bc_two[:, :state_width], step, code, rate)
+        within = within_blocks(x, bc_two, step, code, rate, skip_gain[1][None, picked])
+        part, square = whole_call(
+            last_kernel,
+            [shape((tokens, half), F32), shape((1, tokens), F32)],
+            4 * x.size * state_width,
+            *exchange_states(end, payload, y),
+            first_two,
+            within,
+            bc_two[:, state_width:],
+            code,
+            rate,
+        )
+        mixed.append(part)
+        squares.append(square[0])
+    square_last = lax.psum(squares[0] + squares[1], "head")
+    scale_last = lax.rsqrt(square_last / inner_count + 1e-05)[:, None]
+    mixer_out = jnp.concatenate([(part * scale_last).astype(BF16) for part in mixed], axis=1)
     return (resid_out, mixer_out)
 
 

time: 376 us -> 357 us (0.949)
  waiting for transfers between devices: 222 us -> 166 us
  starting transfers between devices: 47.6 us -> 66.2 us
  Pallas kernels: 65 us -> 81 us
  other arithmetic: 18.2 us -> 22.2 us
    ppermute x18 -> x20, waiting for transfers between devices: 115 us -> 67.2 us  [flip(): return lax.ppermute(value, axis, [(i, i ^ bit) for i in range(n)])]
    pallas_call x3 -> x6, Pallas kernels: 22.2 us -> 36.2 us  [the longest x4 33.4 us: in_call(): pl.pallas_call(functools.partial(in_kernel, count, place), out_shape=shap...]
    ppermute x18 -> x20, starting transfers between devices: 37.9 us -> 51.5 us  [z_shift(): return lax.ppermute(value, 'seq', pairs)]
    ppermute x18 -> x20, waiting for transfers between devices: 108 us -> 98.7 us  [z_shift(): return lax.ppermute(value, 'seq', pairs)]
    ppermute x18 -> x20, starting transfers between devices: 9.73 us -> 14.7 us  [flip(): return lax.ppermute(value, axis, [(i, i ^ bit) for i in range(n)])]
    unnamed x64 -> x60, local copies, waits for them, and re-layouts: 8.16 us -> 5.26 us
    pallas_call x2 -> x3, Pallas kernels: 6.78 us -> 8.36 us  [within_blocks(): pl.pallas_call(within_kernel, name='within', grid=(tokens // GROUP,), out...]
    pallas_call x8 -> x12, Pallas kernels: 22 us -> 20.9 us  [whole_call(): pl.pallas_call(kernel, out_shape=outs, in_specs=[SMEM_SPEC if a.shape ==...]
  transfers between devices with their start and end apart: 36 -> 40, of which waited for: 22 -> 20; matrix products, arithmetic and copies ran while one was open for 6% -> 7% of each run, Pallas kernels for 10% -> 20%
where the time goes in v2:
time: 357 us; the launch traced here: 355 us
  waiting for transfers between devices  166 us (46%)
  Pallas kernels  81 us (23%)
  starting transfers between devices  66.2 us (19%)
  other arithmetic  22.2 us (6%)
  local copies, waits for them, and re-layouts  12.6 us (4%)
  blocking collectives  5.65 us (2%)
    ppermute x20, waiting for transfers between devices, z_shift(): return lax.ppermute(value, 'seq', pairs)  98.7 us
    ppermute x20, waiting for transfers between devices, flip(): return lax.ppermute(value, axis, [(i, i ^ bit) for i in range(n)])  67.2 us
    ppermute x20, starting transfers between devices, z_shift(): return lax.ppermute(value, 'seq', pairs)  51.5 us
    pallas_call x4, Pallas kernels, in_call(): pl.pallas_call(functools.partial(in_kernel, count, place), out_shape=shap...  33.4 us
    pallas_call x12, Pallas kernels, whole_call(): pl.pallas_call(kernel, out_shape=outs, in_specs=[SMEM_SPEC if a.shape ==...  20.9 us
    pallas_call x2, Pallas kernels, out_call(): pl.pallas_call(functools.partial(out_kernel, count), out_shape=outs, in_s...  15.5 us
    ppermute x20, starting transfers between devices, flip(): return lax.ppermute(value, axis, [(i, i ^ bit) for i in range(n)])  14.7 us
    pallas_call x3, Pallas kernels, within_blocks(): pl.pallas_call(within_kernel, name='within', grid=(tokens // GROUP,), out...  8.36 us
  transfers between devices with their start and end apart: 40, of which 20 were waited for; matrix products, arithmetic and copies ran while one was open for 7% of the time, Pallas kernels for 20%

profile of v2, /device:TPU:28, one launch (start us, length us, event | category | flops | bytes accessed | tf_op | source)
XLA Modules:
  0.0 354.9 jit_solution(12148481305269197845)
XLA Ops:
  2.1 5.5 %collective-permute-start.5 = (bf16[1024,512]{1,0:T(8,128)(2,1)}, bf16[1024,512]{1,0:T(8,128)(2,1)}, u32[]{:S(2)}, u32[]{:S(2)}) collective-permute-start(bf16[1024,512]{1,0:T(8,128)(2,1)} %refs_3_.3), channel_id=1, source_target_pairs={{8,0},{12,4},{16,8},{20,12},{24,16},{28,20},{9,1},{13,5},{17,9},{2... | collective-permute-start | bytes 3145736 | tf_op jit(solution)/shard_map/ppermute | solution.py:20
  8.6 19.3 %collective-permute-done.8.refs_4_ = bf16[1024,512]{1,0:T(8,128)(2,1)} collective-permute-done((bf16[1024,512]{1,0:T(8,128)(2,1)}, bf16[1024,512]{1,0:T(8,128)(2,1)}, u32[]{:S(2)}, u32[]{:S(2)}) %collective-permute-start.8) | collective-permute-done | bytes 1048608 | tf_op jit(solution)/shard_map/ppermute | solution.py:20
  29.2 5.5 %collective-permute-start.6 = (bf16[1024,512]{1,0:T(8,128)(2,1)}, bf16[1024,512]{1,0:T(8,128)(2,1)}, u32[]{:S(2)}, u32[]{:S(2)}) collective-permute-start(bf16[1024,512]{1,0:T(8,128)(2,1)} %collective-permute-done.5.refs_2_), channel_id=1, source_target_pairs={{8,0},{12,4},{16,8},{20,12},{24,16},{28,20},{9,1},{13,5},{17,9},{2... | collective-permute-start | bytes 3145736 | tf_op jit(solution)/shard_map/ppermute | solution.py:20
  42.9 6.9 %collective-permute-done.1.far_ref = bf16[144,1024]{1,0:T(8,128)(2,1)} collective-permute-done((bf16[144,1024]{1,0:T(8,128)(2,1)S(1)}, bf16[144,1024]{1,0:T(8,128)(2,1)}, u32[]{:S(2)}, u32[]{:S(2)}) %collective-permute-start.1) | collective-permute-done | bytes 294944 | tf_op jit(solution)/shard_map/ppermute | solution.py:25
  52.2 8.1 %collective-permute-done.2.far_ref = bf16[144,1024]{1,0:T(8,128)(2,1)S(1)} collective-permute-done((bf16[144,1024]{1,0:T(8,128)(2,1)S(1)}, bf16[144,1024]{1,0:T(8,128)(2,1)S(1)}, u32[]{:S(2)}, u32[]{:S(2)}) %collective-permute-start.2) | collective-permute-done | bytes 294944 | tf_op jit(solution)/shard_map/ppermute | solution.py:20
  66.0 11.0 %collective-permute-done.3.far_ref = bf16[144,1024]{1,0:T(8,128)(2,1)S(1)} collective-permute-done((bf16[144,1024]{1,0:T(8,128)(2,1)S(1)}, bf16[144,1024]{1,0:T(8,128)(2,1)S(1)}, u32[]{:S(2)}, u32[]{:S(2)}) %collective-permute-start.3) | collective-permute-done | bytes 294944 | tf_op jit(solution)/shard_map/ppermute | solution.py:20
  82.2 5.5 %collective-permute-start.7 = (bf16[1024,512]{1,0:T(8,128)(2,1)}, bf16[1024,512]{1,0:T(8,128)(2,1)}, u32[]{:S(2)}, u32[]{:S(2)}) collective-permute-start(bf16[1024,512]{1,0:T(8,128)(2,1)} %collective-permute-done.6.refs_1_), channel_id=1, source_target_pairs={{8,0},{12,4},{16,8},{20,12},{24,16},{28,20},{9,1},{13,5},{17,9},{2... | collective-permute-start | bytes 3145736 | tf_op jit(solution)/shard_map/ppermute | solution.py:20
  88.3 16.9 %collective-permute-done.4.far_ref = bf16[512,1024]{1,0:T(8,128)(2,1)S(1)} collective-permute-done((bf16[512,1024]{1,0:T(8,128)(2,1)S(1)}, bf16[512,1024]{1,0:T(8,128)(2,1)S(1)}, u32[]{:S(2)}, u32[]{:S(2)}) %collective-permute-start.4) | collective-permute-done | bytes 1048608 | tf_op jit(solution)/shard_map/ppermute | solution.py:25
  108.8 7.6 %shard_map.181 = bf16[2,1024,512]{2,1,0:T(8,128)(2,1)} custom-call(s32[3]{0:T(128)} %pad_add_fusion.1.where_ref, bf16[512,1024]{1,0:T(8,128)(2,1)} %copy-done.4, bf16[512,1024]{1,0:T(8,128)(2,1)} %copy-done.20, bf16[1024,512]{1,0:T(8,128)(2,1)} %collective-permute-done.7.refs_0_, bf16[1024,512]{1,0:T(8,128)(2,1)} %collective-permute-done.6.refs_1_, ...), custom_call_target="tpu_custom_call" | custom-call | flops 2147483648 | bytes 4194304 | tf_op jit(solution)/shard_map/pallas_call | solution.py:471
  119.8 7.9 %shard_map.180 = (f32[1024,512]{1,0:T(8,128)}, f32[1024,512]{1,0:T(8,128)}) custom-call(s32[3]{0:T(128)} %pad_add_fusion.where_ref, bf16[512,1024]{1,0:T(8,128)(2,1)} %copy-done.4, bf16[512,1024]{1,0:T(8,128)(2,1)} %copy-done.20, bf16[1024,512]{1,0:T(8,128)(2,1)} %collective-permute-done.7.refs_0_, bf16[1024,512]{1,0:T(8,128)(2,1)} %collective-permute-done.6.refs_1_, ...), custom_call_target="tpu_custom_call" | custom-call | flops 2147483648 | bytes 4194304 | tf_op jit(solution)/shard_map/pallas_call | solution.py:471
  134.2 22.4 %collective-permute-done.14 = f32[1,512]{1,0:T(1,128)S(1)} collective-permute-done((f32[1,512]{1,0:T(1,128)S(1)}, f32[1,512]{1,0:T(1,128)S(1)}, u32[]{:S(2)}, u32[]{:S(2)}) %collective-permute-start.14) | collective-permute-done | bytes 2080 | tf_op jit(solution)/shard_map/ppermute | solution.py:25
  167.6 5.4 %collective-permute-start.20 = (bf16[560,1024]{1,0:T(8,128)(2,1)S(1)}, bf16[560,1024]{1,0:T(8,128)(2,1)}, u32[]{:S(2)}, u32[]{:S(2)}) collective-permute-start(bf16[560,1024]{1,0:T(8,128)(2,1)S(1)} %maximum_maximum_fusion.1.refs_3_), channel_id=1, source_target_pairs={{8,0},{12,4},{16,8},{20,12},{24,16},{28,20},{9,1},{13,5},{17,9},{2... | collective-permute-start | bytes 3440648 | tf_op jit(solution)/shard_map/ppermute | solution.py:20
  174.5 13.6 %collective-permute-done.17 = bf16[1024,512]{1,0:T(8,128)(2,1)} collective-permute-done((bf16[1024,512]{1,0:T(8,128)(2,1)}, bf16[1024,512]{1,0:T(8,128)(2,1)}, u32[]{:S(2)}, u32[]{:S(2)}) %collective-permute-start.17) | collective-permute-done | bytes 1048608 | tf_op jit(solution)/shard_map/ppermute | solution.py:25
  194.6 5.5 %collective-permute-start.21 = (bf16[560,1024]{1,0:T(8,128)(2,1)}, bf16[560,1024]{1,0:T(8,128)(2,1)}, u32[]{:S(2)}, u32[]{:S(2)}) collective-permute-start(bf16[560,1024]{1,0:T(8,128)(2,1)} %collective-permute-done.20.refs_2_), channel_id=1, source_target_pairs={{8,0},{12,4},{16,8},{20,12},{24,16},{28,20},{9,1},{13,5},{17,9},{2... | collective-permute-start | bytes 3440648 | tf_op jit(solution)/shard_map/ppermute | solution.py:20
  202.4 18.7 %collective-permute-done.21.refs_1_ = bf16[560,1024]{1,0:T(8,128)(2,1)} collective-permute-done((bf16[560,1024]{1,0:T(8,128)(2,1)}, bf16[560,1024]{1,0:T(8,128)(2,1)}, u32[]{:S(2)}, u32[]{:S(2)}) %collective-permute-start.21) | collective-permute-done | bytes 1146912 | tf_op jit(solution)/shard_map/ppermute | solution.py:20
  221.1 5.4 %collective-permute-start.22 = (bf16[560,1024]{1,0:T(8,128)(2,1)}, bf16[560,1024]{1,0:T(8,128)(2,1)}, u32[]{:S(2)}, u32[]{:S(2)}) collective-permute-start(bf16[560,1024]{1,0:T(8,128)(2,1)} %collective-permute-done.21.refs_1_), channel_id=1, source_target_pairs={{8,0},{12,4},{16,8},{20,12},{24,16},{28,20},{9,1},{13,5},{17,9},{2... | collective-permute-start | bytes 3440648 | tf_op jit(solution)/shard_map/ppermute | solution.py:20
  233.2 19.7 %collective-permute-done.19 = bf16[4,16,512]{2,1,0:T(8,128)(2,1)S(1)} collective-permute-done((bf16[4,16,512]{2,1,0:T(8,128)(2,1)S(1)}, bf16[4,16,512]{2,1,0:T(8,128)(2,1)S(1)}, u32[]{:S(2)}, u32[]{:S(2)}) %collective-permute-start.19) | collective-permute-done | bytes 65568 | tf_op jit(solution)/shard_map/ppermute | solution.py:20
  256.7 8.5 %shard_map.183 = bf16[528,592]{1,0:T(8,128)(2,1)} custom-call(s32[5]{0:T(128)} %stack.104.where_ref, bf16[4,1040,512]{2,1,0:T(8,128)(2,1)} %maximum_maximum_fusion.hidden_ref, bf16[560,1024]{1,0:T(8,128)(2,1)} %collective-permute-done.22.refs_0_, bf16[560,1024]{1,0:T(8,128)(2,1)} %collective-permute-done.21.refs_1_, ...), custom_call_target="tpu_custom_call" | custom-call | flops 2214592512 | bytes 8847360 | tf_op jit(solution)/shard_map/pallas_call | solution.py:489
  268.0 3.9 %collective-permute-done.30 = f32[16]{0:T(128)S(1)} collective-permute-done((f32[16]{0:T(128)S(1)}, f32[16]{0:T(128)S(1)}, u32[]{:S(2)}, u32[]{:S(2)}) %collective-permute-start.30) | collective-permute-done | bytes 96 | tf_op jit(solution)/shard_map/ppermute | solution.py:20
  272.2 8.0 %shard_map.190 = bf16[528,512]{1,0:T(8,128)(2,1)} custom-call(s32[5]{0:T(128)} %stack.104.where_ref, bf16[4,1040,512]{2,1,0:T(8,128)(2,1)} %maximum_maximum_fusion.hidden_ref, bf16[560,1024]{1,0:T(8,128)(2,1)} %collective-permute-done.22.refs_0_, bf16[560,1024]{1,0:T(8,128)(2,1)} %collective-permute-done.21.refs_1_, ...), custom_call_target="tpu_custom_call" | custom-call | flops 2214592512 | bytes 8847360 | tf_op jit(solution)/shard_map/pallas_call | solution.py:489
  281.8 8.7 %shard_map.182.mine_ref = f32[528,592]{1,0:T(8,128)} custom-call(s32[5]{0:T(128)} %stack.98.where_ref, bf16[4,1040,512]{2,1,0:T(8,128)(2,1)} %maximum_maximum_fusion.hidden_ref, bf16[560,1024]{1,0:T(8,128)(2,1)} %collective-permute-done.22.refs_0_, bf16[560,1024]{1,0:T(8,128)(2,1)} %collective-permute-done.21.refs_1_, ...), custom_call_target="tpu_custom_call" | custom-call | flops 2214592512 | bytes 8847360 | tf_op jit(solution)/shard_map/pallas_call | solution.py:489
  298.7 8.2 %shard_map.189.mine_ref = f32[528,512]{1,0:T(8,128)} custom-call(s32[5]{0:T(128)} %stack.98.where_ref, bf16[4,1040,512]{2,1,0:T(8,128)(2,1)} %maximum_maximum_fusion.hidden_ref, bf16[560,1024]{1,0:T(8,128)(2,1)} %collective-permute-done.22.refs_0_, bf16[560,1024]{1,0:T(8,128)(2,1)} %collective-permute-done.21.refs_1_, ...), custom_call_target="tpu_custom_call" | custom-call | flops 2214592512 | bytes 8847360 | tf_op jit(solution)/shard_map/pallas_call | solution.py:489
  335.8 7.8 %collective-permute-done.39.far_ref = bf16[144,512]{1,0:T(8,128)(2,1)S(1)} collective-permute-done((bf16[144,512]{1,0:T(8,128)(2,1)S(1)}, bf16[144,512]{1,0:T(8,128)(2,1)S(1)}, u32[]{:S(2)}, u32[]{:S(2)}) %collective-permute-start.39) | collective-permute-done | bytes 147488 | tf_op jit(solution)/shard_map/ppermute | solution.py:20
  348.0 5.7 %psum.7 = f32[512]{0:T(512)S(1)} all-reduce(f32[512]{0:T(512)S(1)} %bitcast.57), channel_id=1, replica_groups=mesh['seq'=8,'head'=4] {'head'}, use_global_device_ids=true, to_apply=%region_1.2 | all-reduce | flops 512 | bytes 4096 | tf_op jit(solution)/shard_map/psum | solution.py:756
  (194 shorter events, 117.5 us)
Async XLA Ops:
  0.6 27.2 %collective-permute-start.8 = (bf16[1024,512]{1,0:T(8,128)(2,1)}, bf16[1024,512]{1,0:T(8,128)(2,1)}, u32[]{:S(2)}, u32[]{:S(2)}) collective-permute-start(bf16[1024,512]{1,0:T(8,128)(2,1)} %refs_3_.3), channel_id=1, source_target_pairs={{0,8},{4,12},{8,16},{12,20},{16,24},{20,28},{1,9},{5,13},{9,17},{1... | collective-permute-start | bytes 3145736 | tf_op jit(solution)/shard_map/ppermute | solution.py:20
  2.1 27.1 %collective-permute-start.5 = (bf16[1024,512]{1,0:T(8,128)(2,1)}, bf16[1024,512]{1,0:T(8,128)(2,1)}, u32[]{:S(2)}, u32[]{:S(2)}) collective-permute-start(bf16[1024,512]{1,0:T(8,128)(2,1)} %refs_3_.3), channel_id=1, source_target_pairs={{8,0},{12,4},{16,8},{20,12},{24,16},{28,20},{9,1},{13,5},{17,9},{2... | collective-permute-start | bytes 3145736 | tf_op jit(solution)/shard_map/ppermute | solution.py:20
  27.9 53.0 %collective-permute-start.9 = (bf16[1024,512]{1,0:T(8,128)(2,1)}, bf16[1024,512]{1,0:T(8,128)(2,1)}, u32[]{:S(2)}, u32[]{:S(2)}) collective-permute-start(bf16[1024,512]{1,0:T(8,128)(2,1)} %collective-permute-done.8.refs_4_), channel_id=1, source_target_pairs={{0,8},{4,12},{8,16},{12,20},{16,24},{20,28},{1,9},{5,13},{9,17},{1... | collective-permute-start | bytes 3145736 | tf_op jit(solution)/shard_map/ppermute | solution.py:20
  29.2 53.0 %collective-permute-start.6 = (bf16[1024,512]{1,0:T(8,128)(2,1)}, bf16[1024,512]{1,0:T(8,128)(2,1)}, u32[]{:S(2)}, u32[]{:S(2)}) collective-permute-start(bf16[1024,512]{1,0:T(8,128)(2,1)} %collective-permute-done.5.refs_2_), channel_id=1, source_target_pairs={{8,0},{12,4},{16,8},{20,12},{24,16},{28,20},{9,1},{13,5},{17,9},{2... | collective-permute-start | bytes 3145736 | tf_op jit(solution)/shard_map/ppermute | solution.py:20
  80.3 24.9 %collective-permute-start.4 = (bf16[512,1024]{1,0:T(8,128)(2,1)S(1)}, bf16[512,1024]{1,0:T(8,128)(2,1)S(1)}, u32[]{:S(2)}, u32[]{:S(2)}) collective-permute-start(bf16[512,1024]{1,0:T(8,128)(2,1)S(1)} %get-tuple-element.54.own_ref), channel_id=1, source_target_pairs={{0,4},{4,0},{8,12},{12,8},{16,20},{20,16},{24,28},{28,24},{1,5},{5... | collective-permute-start | bytes 3145736 | tf_op jit(solution)/shard_map/ppermute | solution.py:25
  80.9 26.8 %collective-permute-start.10 = (bf16[1024,512]{1,0:T(8,128)(2,1)}, bf16[1024,512]{1,0:T(8,128)(2,1)}, u32[]{:S(2)}, u32[]{:S(2)}) collective-permute-start(bf16[1024,512]{1,0:T(8,128)(2,1)} %collective-permute-done.9.refs_5_), channel_id=1, source_target_pairs={{0,8},{4,12},{8,16},{12,20},{16,24},{20,28},{1,9},{5,13},{9,17},{1... | collective-permute-start | bytes 3145736 | tf_op jit(solution)/shard_map/ppermute | solution.py:20
  82.2 26.7 %collective-permute-start.7 = (bf16[1024,512]{1,0:T(8,128)(2,1)}, bf16[1024,512]{1,0:T(8,128)(2,1)}, u32[]{:S(2)}, u32[]{:S(2)}) collective-permute-start(bf16[1024,512]{1,0:T(8,128)(2,1)} %collective-permute-done.6.refs_1_), channel_id=1, source_target_pairs={{8,0},{12,4},{16,8},{20,12},{24,16},{28,20},{9,1},{13,5},{17,9},{2... | collective-permute-start | bytes 3145736 | tf_op jit(solution)/shard_map/ppermute | solution.py:20
  117.6 39.5 %collective-permute-start = (bf16[512,512]{1,0:T(8,128)(2,1)S(1)}, bf16[512,512]{1,0:T(8,128)(2,1)S(1)}, u32[]{:S(2)}, u32[]{:S(2)}) collective-permute-start(bf16[512,512]{1,0:T(8,128)(2,1)S(1)} %constant_dynamic-slice_fusion.4), channel_id=1, source_target_pairs={{0,4},{4,0},{8,12},{12,8},{16,20},{20,16},{24,28},{28,24},{1,5},{5... | collective-permute-start | bytes 1572872 | tf_op jit(solution)/shard_map/ppermute | solution.py:25
  131.0 29.2 %collective-permute-start.12 = (bf16[1024,512]{1,0:T(8,128)(2,1)}, bf16[1024,512]{1,0:T(8,128)(2,1)}, u32[]{:S(2)}, u32[]{:S(2)}) collective-permute-start(bf16[1024,512]{1,0:T(8,128)(2,1)} %fusion.2), channel_id=1, source_target_pairs={{0,2},{1,3},{2,0},{3,1},{4,6},{5,7},{6,4},{7,5},{8,10},{9,11},{10,... | collective-permute-start | bytes 3145736 | tf_op jit(solution)/shard_map/ppermute | solution.py:25
  133.7 22.9 %collective-permute-start.14 = (f32[1,512]{1,0:T(1,128)S(1)}, f32[1,512]{1,0:T(1,128)S(1)}, u32[]{:S(2)}, u32[]{:S(2)}) collective-permute-start(f32[1,512]{1,0:T(1,128)S(1)} %add.126), channel_id=1, source_target_pairs={{0,2},{1,3},{2,0},{3,1},{4,6},{5,7},{6,4},{7,5},{8,10},{9,11},{10,... | collective-permute-start | bytes 6152 | tf_op jit(solution)/shard_map/ppermute | solution.py:25
  164.5 23.6 %collective-permute-start.17 = (bf16[1024,512]{1,0:T(8,128)(2,1)}, bf16[1024,512]{1,0:T(8,128)(2,1)}, u32[]{:S(2)}, u32[]{:S(2)}) collective-permute-start(bf16[1024,512]{1,0:T(8,128)(2,1)} %fusion), channel_id=1, source_target_pairs={{0,2},{1,3},{2,0},{3,1},{4,6},{5,7},{6,4},{7,5},{8,10},{9,11},{10,... | collective-permute-start | bytes 3145736 | tf_op jit(solution)/shard_map/ppermute | solution.py:25
  167.6 27.0 %collective-permute-start.20 = (bf16[560,1024]{1,0:T(8,128)(2,1)S(1)}, bf16[560,1024]{1,0:T(8,128)(2,1)}, u32[]{:S(2)}, u32[]{:S(2)}) collective-permute-start(bf16[560,1024]{1,0:T(8,128)(2,1)S(1)} %maximum_maximum_fusion.1.refs_3_), channel_id=1, source_target_pairs={{8,0},{12,4},{16,8},{20,12},{24,16},{28,20},{9,1},{13,5},{17,9},{2... | collective-permute-start | bytes 3440648 | tf_op jit(solution)/shard_map/ppermute | solution.py:20
  173.0 27.1 %collective-permute-start.23 = (bf16[560,1024]{1,0:T(8,128)(2,1)S(1)}, bf16[560,1024]{1,0:T(8,128)(2,1)}, u32[]{:S(2)}, u32[]{:S(2)}) collective-permute-start(bf16[560,1024]{1,0:T(8,128)(2,1)S(1)} %maximum_maximum_fusion.1.refs_3_), channel_id=1, source_target_pairs={{0,8},{4,12},{8,16},{12,20},{16,24},{20,28},{1,9},{5,13},{9,17},{1... | collective-permute-start | bytes 3440648 | tf_op jit(solution)/shard_map/ppermute | solution.py:20
  190.9 37.1 %collective-permute-start.18 = (bf16[2,1024,512]{2,1,0:T(8,128)(2,1)}, bf16[2,1024,512]{2,1,0:T(8,128)(2,1)}, u32[]{:S(2)}, u32[]{:S(2)}) collective-permute-start(bf16[2,1024,512]{2,1,0:T(8,128)(2,1)} %pad_maximum_fusion), channel_id=1, source_target_pairs={{0,1},{1,0},{2,3},{3,2},{4,5},{5,4},{6,7},{7,6},{8,9},{9,8},{10,11... | collective-permute-start | bytes 6291464 | tf_op jit(solution)/shard_map/ppermute | solution.py:25
  194.6 26.6 %collective-permute-start.21 = (bf16[560,1024]{1,0:T(8,128)(2,1)}, bf16[560,1024]{1,0:T(8,128)(2,1)}, u32[]{:S(2)}, u32[]{:S(2)}) collective-permute-start(bf16[560,1024]{1,0:T(8,128)(2,1)} %collective-permute-done.20.refs_2_), channel_id=1, source_target_pairs={{8,0},{12,4},{16,8},{20,12},{24,16},{28,20},{9,1},{13,5},{17,9},{2... | collective-permute-start | bytes 3440648 | tf_op jit(solution)/shard_map/ppermute | solution.py:20
  200.1 26.4 %collective-permute-start.24 = (bf16[560,1024]{1,0:T(8,128)(2,1)}, bf16[560,1024]{1,0:T(8,128)(2,1)S(1)}, u32[]{:S(2)}, u32[]{:S(2)}) collective-permute-start(bf16[560,1024]{1,0:T(8,128)(2,1)} %collective-permute-done.23.refs_4_), channel_id=1, source_target_pairs={{0,8},{4,12},{8,16},{12,20},{16,24},{20,28},{1,9},{5,13},{9,17},{1... | collective-permute-start | bytes 3440648 | tf_op jit(solution)/shard_map/ppermute | solution.py:20
  201.8 26.1 %collective-permute-start.27 = (f32[1024]{0:T(1024)S(1)}, f32[1024]{0:T(1024)S(1)}, u32[]{:S(2)}, u32[]{:S(2)}) collective-permute-start(f32[1024]{0:T(1024)S(1)} %get-tuple-element.86), channel_id=1, source_target_pairs={{0,2},{1,3},{2,0},{3,1},{4,6},{5,7},{6,4},{7,5},{8,10},{9,11},{10,... | collective-permute-start | bytes 12296 | tf_op jit(solution)/shard_map/ppermute | solution.py:25
  221.1 35.5 %collective-permute-start.22 = (bf16[560,1024]{1,0:T(8,128)(2,1)}, bf16[560,1024]{1,0:T(8,128)(2,1)}, u32[]{:S(2)}, u32[]{:S(2)}) collective-permute-start(bf16[560,1024]{1,0:T(8,128)(2,1)} %collective-permute-done.21.refs_1_), channel_id=1, source_target_pairs={{8,0},{12,4},{16,8},{20,12},{24,16},{28,20},{9,1},{13,5},{17,9},{2... | collective-permute-start | bytes 3440648 | tf_op jit(solution)/shard_map/ppermute | solution.py:20
  226.6 30.1 %collective-permute-start.25 = (bf16[560,1024]{1,0:T(8,128)(2,1)S(1)}, bf16[560,1024]{1,0:T(8,128)(2,1)}, u32[]{:S(2)}, u32[]{:S(2)}) collective-permute-start(bf16[560,1024]{1,0:T(8,128)(2,1)S(1)} %collective-permute-done.24.refs_5_), channel_id=1, source_target_pairs={{0,8},{4,12},{8,16},{12,20},{16,24},{20,28},{1,9},{5,13},{9,17},{1... | collective-permute-start | bytes 3440648 | tf_op jit(solution)/shard_map/ppermute | solution.py:20
  230.7 22.2 %collective-permute-start.19 = (bf16[4,16,512]{2,1,0:T(8,128)(2,1)S(1)}, bf16[4,16,512]{2,1,0:T(8,128)(2,1)S(1)}, u32[]{:S(2)}, u32[]{:S(2)}) collective-permute-start(bf16[4,16,512]{2,1,0:T(8,128)(2,1)S(1)} %pad_maximum_fusion.8), channel_id=1, source_target_pairs={{0,8},{4,12},{8,16},{12,20},{16,24},{20,28},{1,9},{5,13},{9,17},{1... | collective-permute-start | bytes 196616 | tf_op jit(solution)/shard_map/ppermute | solution.py:20
  232.7 33.7 %collective-permute-start.29 = (f32[1024]{0:T(1024)S(1)}, f32[1024]{0:T(1024)S(1)}, u32[]{:S(2)}, u32[]{:S(2)}) collective-permute-start(f32[1024]{0:T(1024)S(1)} %add.135), channel_id=1, source_target_pairs={{0,4},{4,0},{8,12},{12,8},{16,20},{20,16},{24,28},{28,24},{1,5},{5... | collective-permute-start | bytes 12296 | tf_op jit(solution)/shard_map/ppermute | solution.py:25
  265.2 25.3 %collective-permute-start.26 = (bf16[528,592]{1,0:T(8,128)(2,1)}, bf16[528,592]{1,0:T(8,128)(2,1)S(1)}, u32[]{:S(2)}, u32[]{:S(2)}) collective-permute-start(bf16[528,592]{1,0:T(8,128)(2,1)} %shard_map.183), channel_id=1, source_target_pairs={{0,4},{4,0},{8,12},{12,8},{16,20},{20,16},{24,28},{28,24},{1,5},{5... | collective-permute-start | bytes 1875464 | tf_op jit(solution)/shard_map/ppermute | solution.py:25
  280.2 26.7 %collective-permute-start.36 = (bf16[528,512]{1,0:T(8,128)(2,1)}, bf16[528,512]{1,0:T(8,128)(2,1)S(1)}, u32[]{:S(2)}, u32[]{:S(2)}) collective-permute-start(bf16[528,512]{1,0:T(8,128)(2,1)} %shard_map.190), channel_id=1, source_target_pairs={{0,4},{4,0},{8,12},{12,8},{16,20},{20,16},{24,28},{28,24},{1,5},{5... | collective-permute-start | bytes 1622024 | tf_op jit(solution)/shard_map/ppermute | solution.py:25
  295.4 22.3 %collective-permute-start.16 = (bf16[512,512]{1,0:T(8,128)(2,1)S(1)}, bf16[512,512]{1,0:T(8,128)(2,1)}, u32[]{:S(2)}, u32[]{:S(2)}) collective-permute-start(bf16[512,512]{1,0:T(8,128)(2,1)S(1)} %constant_dynamic-slice_fusion.3), channel_id=1, source_target_pairs={{0,4},{4,0},{8,12},{12,8},{16,20},{20,16},{24,28},{28,24},{1,5},{5... | collective-permute-start | bytes 1572872 | tf_op jit(solution)/shard_map/ppermute | solution.py:25
  (44 other events, 591.9 us)

commit v3 on v2

--- a/solution.py
+++ b/solution.py
@@ -37,12 +37,25 @@
     return flip(value, "head", 1)
 
 
-def z_line(value):
+def z_line(value, place):
     ups, downs = [value], [value]
     for _ in range(1, 4):
         ups.append(z_shift(ups[-1], 1))
         downs.append(z_shift(downs[-1], -1))
-    return downs[:0:-1] + ups
+    early, low, high = place >= 1, place == 0, place == 3
+    blocks = [
+        value,
+        jnp.where(early, ups[1], downs[1]),
+        jnp.where(place >= 2, ups[2], downs[2]),
+        jnp.where(low, downs[3], jnp.where(high, ups[3], downs[1])),
+    ]
+    places = [
+        place,
+        jnp.where(early, place - 1, 1),
+        (place + 2) % 4,
+        jnp.where(low, 3, jnp.where(high, 0, place + 1)),
+    ]
+    return blocks, places
 
 
 def z_whole(value):
@@ -282,7 +295,6 @@
 
 VMEM_SPEC = pl.BlockSpec(memory_space=pltpu.VMEM)
 SMEM_SPEC = pl.BlockSpec(memory_space=pltpu.SMEM)
-HBM_SPEC = pl.BlockSpec(memory_space=pltpu.HBM)
 
 
 def whole_call(kernel, outs, flops, *args):
@@ -392,117 +404,100 @@
     )(mine, *args)
 
 
-def fetch(spot, sources, buffer, sem, start):
-    reach = len(sources) // 2
-    for k in range(len(sources)):
-
-        @pl.when(spot == k - reach)
-        def _():
-            copy = pltpu.make_async_copy(sources[k], buffer, sem)
-            if start:
-                copy.start()
-            else:
-                copy.wait()
-
-
-def out_kernel(count, where_ref, own_ref, far_ref, *refs):
-    sources, outs, (buffers, sems) = refs[:7], refs[7:-2], refs[-2:]
+def out_kernel(where_ref, own_ref, far_ref, *refs):
+    blocks, (send_ref, keep_ref) = refs[:4], refs[4:]
     tokens = own_ref.shape[0]
     own_start = pl.multiple_of(where_ref[0] * tokens, tokens)
     far_start = pl.multiple_of((1 - where_ref[0]) * tokens, tokens)
-    fetch(where_ref[1], sources, buffers.at[0], sems.at[0], True)
-    for i in range(count):
-        if i + 1 < count:
-            slot = (i + 1) % 2
-            fetch(where_ref[i + 2], sources, buffers.at[slot], sems.at[slot], True)
-        fetch(where_ref[i + 1], sources, buffers.at[i % 2], sems.at[i % 2], False)
+    for i, block_ref in enumerate(blocks):
+        kept, spot = where_ref[2 * i + 1], where_ref[2 * i + 2]
         for ref, start in ((own_ref, own_start), (far_ref, far_start)):
 
             @pl.loop(0, tokens, step=ROWS)
             def _(row):
                 row = pl.multiple_of(row, ROWS)
                 product = jnp.dot(
-                    ref[pl.ds(row, ROWS), :], buffers[i % 2], preferred_element_type=F32
+                    ref[pl.ds(row, ROWS), :], block_ref[...], preferred_element_type=F32
                 )
-                if len(outs) == 1:
-                    outs[0][i, pl.ds(start + row, ROWS), :] = product.astype(outs[0].dtype)
-                else:
-                    outs[i][pl.ds(start + row, ROWS), :] = product.astype(outs[i].dtype)
-
-
-def in_kernel(count, place, where_ref, hidden_ref, *refs):
-    sources, (out_ref, buffers, total, sems) = refs[:7], refs[7:]
-    rows = out_ref.shape[0]
-    fetch(where_ref[1], sources, buffers.at[0], sems.at[0], True)
-    for i in range(count):
-        if i + 1 < count:
-            slot = (i + 1) % 2
-            fetch(where_ref[i + 2], sources, buffers.at[slot], sems.at[slot], True)
-        fetch(where_ref[i + 1], sources, buffers.at[i % 2], sems.at[i % 2], False)
-        depth, wide = hidden_ref.shape[2], buffers.shape[2] // 2
-        packed = buffers[i % 2, depth:, :]
-        below = jnp.concatenate([packed[:, :depth], packed[:, depth:]], axis=0)
-
-        @pl.loop(0, rows, step=rows // 3)
-        def _(row):
-            here = pl.ds(pl.multiple_of(row, HALO), rows // 3)
-            there = pl.ds(pl.multiple_of(where_ref[0] + row, HALO), rows // 3)
-            hidden = hidden_ref[i, there, :]
-            weight = buffers[i % 2, :depth, place * wide : (place + 1) * wide]
-            products = [(jnp.dot(hidden, weight, preferred_element_type=F32), slice(0, wide))]
-            if out_ref.shape[1] > wide:
-                small = lax.dot_general(
-                    hidden, below, (((1,), (1,)), ((), ())), preferred_element_type=F32
-                )[:, : out_ref.shape[1] - wide]
-                products.append((small, slice(wide, out_ref.shape[1])))
-            for part, columns in products:
-                if i == 0:
-                    total[here, columns] = part
-                elif i + 1 < count:
-                    total[here, columns] += part
-                else:
-                    out_ref[here, columns] = (total[here, columns] + part).astype(out_ref.dtype)
-
-
-def out_call(where, own, far, sources, outs):
-    count = where.shape[0] - 1
+
+                @pl.when(kept == 1)
+                def _():
+                    keep_ref[spot, pl.ds(start + row, ROWS), :] = product
+
+                @pl.when(kept == 0)
+                def _():
+                    send_ref[spot, pl.ds(start + row, ROWS), :] = product.astype(BF16)
+
+
+def in_kernel(place, where_ref, hidden_ref, *refs):
+    blocks, out_ref = refs[:4], refs[4]
+    rows, columns = out_ref.shape
+    depth = hidden_ref.shape[2]
+    wide = blocks[0].shape[1] // 2
+
+    @pl.loop(0, rows, step=rows // 3)
+    def _(row):
+        here = pl.ds(pl.multiple_of(row, HALO), rows // 3)
+        there = pl.ds(pl.multiple_of(where_ref[0] + row, HALO), rows // 3)
+        large, small = None, None
+        for i, block_ref in enumerate(blocks):
+            hidden = hidden_ref[where_ref[i + 1], there, :]
+            weight = block_ref[:depth, place * wide : (place + 1) * wide]
+            part = jnp.dot(hidden, weight, preferred_element_type=F32)
+            large = part if large is None else large + part
+            if columns > wide:
+                packed = block_ref[depth:, :]
+                part = lax.dot_general(
+                    hidden,
+                    jnp.concatenate([packed[:, :depth], packed[:, depth:]], axis=0),
+                    (((1,), (1,)), ((), ())),
+                    preferred_element_type=F32,
+                )
+                small = part if small is None else small + part
+        out_ref[here, :wide] = large.astype(out_ref.dtype)
+        if columns > wide:
+            out_ref[here, wide:] = small[:, : columns - wide].astype(out_ref.dtype)
+
+
+def out_call(where, own, far, blocks):
     tokens, depth = own.shape
-    block = sources[0].shape
+    width = blocks[0].shape[1]
     return pl.pallas_call(
-        functools.partial(out_kernel, count),
-        out_shape=outs,
-        in_specs=[SMEM_SPEC, VMEM_SPEC, VMEM_SPEC] + [HBM_SPEC] * len(sources),
-        out_specs=[VMEM_SPEC] * len(outs),
-        scratch_shapes=[pltpu.VMEM((2,) + block, BF16), pltpu.SemaphoreType.DMA((2,))],
+        out_kernel,
+        name="out",
+        out_shape=[shape((2, 2 * tokens, width), BF16), shape((2, 2 * tokens, width), F32)],
+        in_specs=[SMEM_SPEC] + [VMEM_SPEC] * (2 + len(blocks)),
+        out_specs=[VMEM_SPEC] * 2,
         cost_estimate=pl.CostEstimate(
-            flops=4 * count * tokens * depth * block[1],
-            bytes_accessed=4 * own.size + 2 * count * sources[0].size,
+            flops=16 * tokens * depth * width,
+            bytes_accessed=4 * own.size + 8 * blocks[0].size,
             transcendentals=0,
         ),
-        compiler_params=pltpu.CompilerParams(vmem_limit_bytes=60 * 2**20),
-    )(where, own, far, *sources)
-
-
-def in_call(place, where, hidden, sources, rows, columns, kind):
+        compiler_params=pltpu.CompilerParams(vmem_limit_bytes=16 * 2**20),
+    )(where, own, far, *blocks)
+
+
+def in_call(place, where, hidden, blocks, rows, columns, kind):
     count, _, depth = hidden.shape
-    block = sources[0].shape
     return pl.pallas_call(
-        functools.partial(in_kernel, count, place),
+        functools.partial(in_kernel, place),
         out_shape=shape((rows, columns), kind),
-        in_specs=[SMEM_SPEC, VMEM_SPEC] + [HBM_SPEC] * len(sources),
+        in_specs=[SMEM_SPEC] + [VMEM_SPEC] * (1 + len(blocks)),
         out_specs=VMEM_SPEC,
-        scratch_shapes=[
-            pltpu.VMEM((2,) + block, BF16),
-            pltpu.VMEM((rows, columns), F32),
-            pltpu.SemaphoreType.DMA((2,)),
-        ],
         cost_estimate=pl.CostEstimate(
-            flops=2 * count * rows * depth * block[1],
-            bytes_accessed=2 * hidden.size + 2 * count * sources[0].size,
+            flops=2 * count * rows * depth * columns,
+            bytes_accessed=2 * (hidden.size + count * depth * columns),
             transcendentals=0,
         ),
-        compiler_params=pltpu.CompilerParams(vmem_limit_bytes=60 * 2**20),
-    )(where, hidden, *sources)
+        compiler_params=pltpu.CompilerParams(vmem_limit_bytes=16 * 2**20),
+    )(where, hidden, *blocks)
+
+
+def join_kernel(y_ref, mine_ref, back_ref, out_ref):
+    first = y_ref[0] == 0
+    half = mine_ref.shape[1]
+    out_ref[:, :half] = jnp.where(first, mine_ref[...], back_ref[...])
+    out_ref[:, half:] = jnp.where(first, back_ref[...], mine_ref[...])
 
 
 def pick(stack, index):
@@ -577,8 +572,8 @@
         below = jnp.concatenate([below, jnp.zeros((-small % 32, block), BF16)], axis=0)
         below = below.reshape(2, below.shape[0] // 2, block)
         below = jnp.concatenate([below[0], below[1]], axis=1)
-        out_blocks = z_line(w_out)
-        in_blocks = z_line(jnp.concatenate([w_in_x, below], axis=0))
+        out_blocks, out_places = z_line(w_out, z)
+        in_blocks, in_places = z_line(jnp.concatenate([w_in_x, below], axis=0), z)
     else:
         w_in = jnp.concatenate([w_in_x, bc_weight, w_in_dt], axis=1)
         out_blocks, in_blocks = z_whole(w_out), z_whole(w_in)
@@ -625,21 +620,10 @@
     keep_heads = [2 * (x_bit ^ i) + c_bit for i in range(2)]
     send_heads = [2 * (x_bit ^ i) + (1 - c_bit) for i in range(2)]
     if line:
-        where = lambda heads: jnp.stack([y] + [z - h for h in heads]).astype(jnp.int32)
-        (sends,) = out_call(
-            where(send_heads),
-            scaled,
-            scaled_far,
-            out_blocks,
-            [shape((2, pair_tokens, block), BF16)],
-        )
-        keeps = out_call(
-            where(keep_heads),
-            scaled,
-            scaled_far,
-            out_blocks,
-            [shape((pair_tokens, block), F32)] * 2,
-        )
+        where = [y]
+        for place in out_places:
+            where += [(place % 2 == c_bit).astype(jnp.int32), (place // 2) ^ x_bit]
+        sends, keeps = out_call(jnp.stack(where).astype(jnp.int32), scaled, scaled_far, out_blocks)
     else:
         both = jnp.concatenate(
             [jnp.where(first, scaled, scaled_far), jnp.where(first, scaled_far, scaled)], axis=0
@@ -658,10 +642,17 @@
 
     resid_back = y_swap(lax.dynamic_slice_in_dim(resid_new, (1 - y) * tokens, tokens, 0))
     resid_mine = lax.dynamic_slice_in_dim(resid_new, y * tokens, tokens, 0)
-    both = [jnp.where(first, resid_mine, resid_back), jnp.where(first, resid_back, resid_mine)]
     if per_head == 1:
-        resid_out = jnp.concatenate(both, axis=1)
+        (resid_out,) = whole_call(
+            join_kernel,
+            [shape((tokens, width), BF16)],
+            resid_in.size,
+            y[None].astype(jnp.int32),
+            resid_mine,
+            resid_back,
+        )
     else:
+        both = [jnp.where(first, resid_mine, resid_back), jnp.where(first, resid_back, resid_mine)]
         both = [a.reshape(tokens, per_head, block) for a in both]
         resid_out = jnp.stack(both, axis=2).reshape(tokens, width)
 
@@ -688,7 +679,7 @@
     send_start = tokens - keep_start
     columns = (half + small, half)
     if line:
-        spots = [z - (head ^ k) for k in range(4)]
+        spots = [place ^ head for place in in_places]
         where = lambda start: jnp.stack([start] + spots).astype(jnp.int32)
         project = lambda place, start, kind: in_call(
             place, where(start), all_hidden, in_blocks, reach, columns[place], kind

time: 357 us -> 366 us (1.025)
  waiting for transfers between devices: 166 us -> 193 us
  Pallas kernels: 81 us -> 55.3 us
  local copies, waits for them, and re-layouts: 12.6 us -> 27.7 us
  starting transfers between devices: 66.2 us -> 60.3 us
    pallas_call x6 -> x5, Pallas kernels: 48.9 us -> 19.6 us  [the longest x4 11.7 us: in_call(): pl.pallas_call(functools.partial(in_kernel, place), out_shape=shape((rows...]
    ppermute x20, waiting for transfers between devices: 67.2 us -> 88.5 us  [flip(): return lax.ppermute(value, axis, [(i, i ^ bit) for i in range(n)])]
    unnamed x60 -> x98, local copies, waits for them, and re-layouts: 5.26 us -> 16.7 us
    ppermute x20, starting transfers between devices: 51.5 us -> 45.7 us  [z_shift(): return lax.ppermute(value, 'seq', pairs)]
    ppermute x20, waiting for transfers between devices: 98.7 us -> 104 us  [z_shift(): return lax.ppermute(value, 'seq', pairs)]
    select_n x1 -> x4, other arithmetic: 1.23 us -> 6.37 us  [the longest x2 3.65 us: z_line(): jnp.where(low, downs[3], jnp.where(high, ups[3], downs[1]))]
    pallas_call x12 -> x13, Pallas kernels: 20.9 us -> 22 us  [whole_call(): pl.pallas_call(kernel, out_shape=outs, in_specs=[SMEM_SPEC if a.shape ==...]
  transfers between devices with their start and end apart: 40 -> 40, of which waited for: 20 -> 23; matrix products, arithmetic and copies ran while one was open for 7% -> 8% of each run, Pallas kernels for 20% -> 12%
where the time goes in v3:
time: 366 us; the launch traced here: 363 us
  waiting for transfers between devices  193 us (53%)
  starting transfers between devices  60.3 us (16%)
  Pallas kernels  55.3 us (15%)
  local copies, waits for them, and re-layouts  27.7 us (8%)
  other arithmetic  20.1 us (5%)
  blocking collectives  5.75 us (2%)
    ppermute x20, waiting for transfers between devices, z_shift(): return lax.ppermute(value, 'seq', pairs)  104 us
    ppermute x20, waiting for transfers between devices, flip(): return lax.ppermute(value, axis, [(i, i ^ bit) for i in range(n)])  88.5 us
    ppermute x20, starting transfers between devices, z_shift(): return lax.ppermute(value, 'seq', pairs)  45.7 us
    pallas_call x13, Pallas kernels, whole_call(): pl.pallas_call(kernel, out_shape=outs, in_specs=[SMEM_SPEC if a.shape ==...  22 us
    unnamed x98, local copies, waits for them, and re-layouts  16.7 us
    ppermute x20, starting transfers between devices, flip(): return lax.ppermute(value, axis, [(i, i ^ bit) for i in range(n)])  14.6 us
    pallas_call x4, Pallas kernels, in_call(): pl.pallas_call(functools.partial(in_kernel, place), out_shape=shape((rows...  11.7 us
    pallas_call x3, Pallas kernels, within_blocks(): pl.pallas_call(within_kernel, name='within', grid=(tokens // GROUP,), out...  8.36 us
  transfers between devices with their start and end apart: 40, of which 23 were waited for; matrix products, arithmetic and copies ran while one was open for 8% of the time, Pallas kernels for 12%

profile of v3, /device:TPU:28, one launch (start us, length us, event | category | flops | bytes accessed | tf_op | source)
XLA Modules:
  0.0 363.3 jit_solution(3327110178699763385)
XLA Ops:
  0.6 3.5 collective-permute-start.6
  5.4 20.4 %collective-permute-done.6 = bf16[1024,512]{1,0:T(8,128)(2,1)} collective-permute-done((bf16[1024,512]{1,0:T(8,128)(2,1)}, bf16[1024,512]{1,0:T(8,128)(2,1)}, u32[]{:S(2)}, u32[]{:S(2)}) %collective-permute-start.6) | collective-permute-done | bytes 1048608 | tf_op jit(solution)/shard_map/ppermute | solution.py:20
  25.9 5.4 %collective-permute-start.8 = (bf16[1024,512]{1,0:T(8,128)(2,1)}, bf16[1024,512]{1,0:T(8,128)(2,1)}, u32[]{:S(2)}, u32[]{:S(2)}) collective-permute-start(bf16[1024,512]{1,0:T(8,128)(2,1)} %collective-permute-done.6), channel_id=1, source_target_pairs={{8,0},{12,4},{16,8},{20,12},{24,16},{28,20},{9,1},{13,5},{17,9},{2... | collective-permute-start | bytes 3145736 | tf_op jit(solution)/shard_map/ppermute | solution.py:20
  37.8 3.8 %shard_map.176 = (f32[128,1024]{1,0:T(8,128)S(1)}, f32[128,1024]{1,0:T(8,128)S(1)}, bf16[144,1024]{1,0:T(8,128)(2,1)S(1)}) custom-call(bf16[512,1024]{1,0:T(8,128)(2,1)S(1)} %copy-done.15, bf16[512,128]{1,0:T(8,128)(2,1)S(1)} %get-tuple-element.107.b_ref, f32[512,16]{1,0:T(8,128)S(1)} %copy.25.step_ref, s32[512,16]{1,0:T(8,128)S(1)} %bitcast.48, ...), custom_call_target="tpu_custom_call" | custom-call | flops 268435456 | bytes 2588736 | tf_op jit(solution)/shard_map/pallas_call | solution.py:303
  42.2 7.2 %collective-permute-done.1.far_ref = bf16[144,1024]{1,0:T(8,128)(2,1)} collective-permute-done((bf16[144,1024]{1,0:T(8,128)(2,1)S(1)}, bf16[144,1024]{1,0:T(8,128)(2,1)}, u32[]{:S(2)}, u32[]{:S(2)}) %collective-permute-start.1) | collective-permute-done | bytes 294944 | tf_op jit(solution)/shard_map/ppermute | solution.py:25
  52.1 5.7 %collective-permute-start.9 = (bf16[1024,512]{1,0:T(8,128)(2,1)}, bf16[1024,512]{1,0:T(8,128)(2,1)}, u32[]{:S(2)}, u32[]{:S(2)}) collective-permute-start(bf16[1024,512]{1,0:T(8,128)(2,1)} %collective-permute-done.8), channel_id=1, source_target_pairs={{8,0},{12,4},{16,8},{20,12},{24,16},{28,20},{9,1},{13,5},{17,9},{2... | collective-permute-start | bytes 3145736 | tf_op jit(solution)/shard_map/ppermute | solution.py:20
  60.7 4.9 %collective-permute-done.2.far_ref = bf16[144,1024]{1,0:T(8,128)(2,1)S(1)} collective-permute-done((bf16[144,1024]{1,0:T(8,128)(2,1)S(1)}, bf16[144,1024]{1,0:T(8,128)(2,1)S(1)}, u32[]{:S(2)}, u32[]{:S(2)}) %collective-permute-start.2) | collective-permute-done | bytes 294944 | tf_op jit(solution)/shard_map/ppermute | solution.py:20
  68.1 3.4 within.3.within_ref
  71.5 26.0 %collective-permute-done.3.far_ref = bf16[144,1024]{1,0:T(8,128)(2,1)S(1)} collective-permute-done((bf16[144,1024]{1,0:T(8,128)(2,1)S(1)}, bf16[144,1024]{1,0:T(8,128)(2,1)S(1)}, u32[]{:S(2)}, u32[]{:S(2)}) %collective-permute-start.3) | collective-permute-done | bytes 294944 | tf_op jit(solution)/shard_map/ppermute | solution.py:20
  104.9 19.2 %collective-permute-done.4.far_ref = bf16[512,1024]{1,0:T(8,128)(2,1)S(1)} collective-permute-done((bf16[512,1024]{1,0:T(8,128)(2,1)S(1)}, bf16[512,1024]{1,0:T(8,128)(2,1)S(1)}, u32[]{:S(2)}, u32[]{:S(2)}) %collective-permute-start.4) | collective-permute-done | bytes 1048608 | tf_op jit(solution)/shard_map/ppermute | solution.py:25
  127.6 7.9 %out.1 = (bf16[2,1024,512]{2,1,0:T(8,128)(2,1)S(1)}, f32[2,1024,512]{2,1,0:T(8,128)S(1)}) custom-call(s32[9]{0:T(128)S(1)} %stack.116.where_ref, bf16[512,1024]{1,0:T(8,128)(2,1)S(1)} %copy-done.28, bf16[512,1024]{1,0:T(8,128)(2,1)S(1)} %copy-done.30, bf16[1024,512]{1,0:T(8,128)(2,1)S(1)} %copy-done.26, bf16[1024,512]{1,0:T(8,128)(2,1)S(1)} %get-tuple-element.97.refs_1_, ...), custom_call_target="tpu_custom_call" | custom-call | flops 4294967296 | bytes 6291456 | tf_op jit(solution)/shard_map/out/pallas_call | solution.py:465
  149.0 21.6 %collective-permute-done.14 = f32[1,512]{1,0:T(1,128)S(1)} collective-permute-done((f32[1,512]{1,0:T(1,128)S(1)}, f32[1,512]{1,0:T(1,128)S(1)}, u32[]{:S(2)}, u32[]{:S(2)}) %collective-permute-start.14) | collective-permute-done | bytes 2080 | tf_op jit(solution)/shard_map/ppermute | solution.py:25
  181.7 18.7 %collective-permute-done.17 = bf16[1024,512]{1,0:T(8,128)(2,1)S(1)} collective-permute-done((bf16[1024,512]{1,0:T(8,128)(2,1)S(1)}, bf16[1024,512]{1,0:T(8,128)(2,1)S(1)}, u32[]{:S(2)}, u32[]{:S(2)}) %collective-permute-start.17) | collective-permute-done | bytes 1048608 | tf_op jit(solution)/shard_map/ppermute | solution.py:25
  203.0 5.4 %collective-permute-start.23 = (bf16[560,1024]{1,0:T(8,128)(2,1)S(1)}, bf16[560,1024]{1,0:T(8,128)(2,1)}, u32[]{:S(2)}, u32[]{:S(2)}) collective-permute-start(bf16[560,1024]{1,0:T(8,128)(2,1)S(1)} %collective-permute-done.21), channel_id=1, source_target_pairs={{8,0},{12,4},{16,8},{20,12},{24,16},{28,20},{9,1},{13,5},{17,9},{2... | collective-permute-start | bytes 3440648 | tf_op jit(solution)/shard_map/ppermute | solution.py:20
  209.7 19.7 %collective-permute-done.23 = bf16[560,1024]{1,0:T(8,128)(2,1)} collective-permute-done((bf16[560,1024]{1,0:T(8,128)(2,1)S(1)}, bf16[560,1024]{1,0:T(8,128)(2,1)}, u32[]{:S(2)}, u32[]{:S(2)}) %collective-permute-start.23) | collective-permute-done | bytes 1146912 | tf_op jit(solution)/shard_map/ppermute | solution.py:20
  229.4 5.5 %collective-permute-start.24 = (bf16[560,1024]{1,0:T(8,128)(2,1)}, bf16[560,1024]{1,0:T(8,128)(2,1)}, u32[]{:S(2)}, u32[]{:S(2)}) collective-permute-start(bf16[560,1024]{1,0:T(8,128)(2,1)} %collective-permute-done.23), channel_id=1, source_target_pairs={{8,0},{12,4},{16,8},{20,12},{24,16},{28,20},{9,1},{13,5},{17,9},{2... | collective-permute-start | bytes 3440648 | tf_op jit(solution)/shard_map/ppermute | solution.py:20
  244.4 11.0 %collective-permute-done.24 = bf16[560,1024]{1,0:T(8,128)(2,1)} collective-permute-done((bf16[560,1024]{1,0:T(8,128)(2,1)}, bf16[560,1024]{1,0:T(8,128)(2,1)}, u32[]{:S(2)}, u32[]{:S(2)}) %collective-permute-start.24) | collective-permute-done | bytes 1146912 | tf_op jit(solution)/shard_map/ppermute | solution.py:20
  255.4 5.8 %collective-permute-done.25 = bf16[560,1024]{1,0:T(8,128)(2,1)} collective-permute-done((bf16[560,1024]{1,0:T(8,128)(2,1)}, bf16[560,1024]{1,0:T(8,128)(2,1)}, u32[]{:S(2)}, u32[]{:S(2)}) %collective-permute-start.25) | collective-permute-done | bytes 1146912 | tf_op jit(solution)/shard_map/ppermute | solution.py:20
  265.1 3.6 shard_map.182
  272.0 8.7 %collective-permute-done.29 = f32[1024]{0:T(1024)S(1)} collective-permute-done((f32[1024]{0:T(1024)S(1)}, f32[1024]{0:T(1024)S(1)}, u32[]{:S(2)}, u32[]{:S(2)}) %collective-permute-start.29) | collective-permute-done | bytes 4128 | tf_op jit(solution)/shard_map/ppermute | solution.py:25
  282.2 4.1 %collective-permute-done.30 = f32[16]{0:T(128)S(1)} collective-permute-done((f32[16]{0:T(128)S(1)}, f32[16]{0:T(128)S(1)}, u32[]{:S(2)}, u32[]{:S(2)}) %collective-permute-start.30) | collective-permute-done | bytes 96 | tf_op jit(solution)/shard_map/ppermute | solution.py:20
  302.2 4.9 %collective-permute-done.31 = bf16[512,64]{1,0:T(8,128)(2,1)} collective-permute-done((bf16[512,64]{1,0:T(8,128)(2,1)}, bf16[512,64]{1,0:T(8,128)(2,1)}, u32[]{:S(2)}, u32[]{:S(2)}) %collective-permute-start.31) | collective-permute-done | bytes 65568 | tf_op jit(solution)/shard_map/ppermute | solution.py:25
  343.8 8.1 %collective-permute-done.35.far_ref = bf16[144,512]{1,0:T(8,128)(2,1)S(1)} collective-permute-done((bf16[144,512]{1,0:T(8,128)(2,1)S(1)}, bf16[144,512]{1,0:T(8,128)(2,1)S(1)}, u32[]{:S(2)}, u32[]{:S(2)}) %collective-permute-start.35) | collective-permute-done | bytes 147488 | tf_op jit(solution)/shard_map/ppermute | solution.py:20
  356.2 5.7 %psum.7 = f32[512]{0:T(512)S(1)} all-reduce(f32[512]{0:T(512)S(1)} %bitcast.60), channel_id=1, replica_groups=mesh['seq'=8,'head'=4] {'head'}, use_global_device_ids=true, to_apply=%region_1.2 | all-reduce | flops 512 | bytes 4096 | tf_op jit(solution)/shard_map/psum | solution.py:747
  (233 shorter events, 131.6 us)
Async XLA Ops:
  0.6 25.2 %collective-permute-start.6 = (bf16[1024,512]{1,0:T(8,128)(2,1)}, bf16[1024,512]{1,0:T(8,128)(2,1)}, u32[]{:S(2)}, u32[]{:S(2)}) collective-permute-start(bf16[1024,512]{1,0:T(8,128)(2,1)} %refs_0_.1), channel_id=1, source_target_pairs={{8,0},{12,4},{16,8},{20,12},{24,16},{28,20},{9,1},{13,5},{17,9},{2... | collective-permute-start | bytes 3145736 | tf_op jit(solution)/shard_map/ppermute | solution.py:20
  4.1 27.1 %collective-permute-start.5 = (bf16[1024,512]{1,0:T(8,128)(2,1)}, bf16[1024,512]{1,0:T(8,128)(2,1)}, u32[]{:S(2)}, u32[]{:S(2)}) collective-permute-start(bf16[1024,512]{1,0:T(8,128)(2,1)} %refs_0_.1), channel_id=1, source_target_pairs={{0,8},{4,12},{8,16},{12,20},{16,24},{20,28},{1,9},{5,13},{9,17},{1... | collective-permute-start | bytes 3145736 | tf_op jit(solution)/shard_map/ppermute | solution.py:20
  25.9 26.2 %collective-permute-start.8 = (bf16[1024,512]{1,0:T(8,128)(2,1)}, bf16[1024,512]{1,0:T(8,128)(2,1)}, u32[]{:S(2)}, u32[]{:S(2)}) collective-permute-start(bf16[1024,512]{1,0:T(8,128)(2,1)} %collective-permute-done.6), channel_id=1, source_target_pairs={{8,0},{12,4},{16,8},{20,12},{24,16},{28,20},{9,1},{13,5},{17,9},{2... | collective-permute-start | bytes 3145736 | tf_op jit(solution)/shard_map/ppermute | solution.py:20
  31.2 28.2 %collective-permute-start.7 = (bf16[1024,512]{1,0:T(8,128)(2,1)}, bf16[1024,512]{1,0:T(8,128)(2,1)}, u32[]{:S(2)}, u32[]{:S(2)}) collective-permute-start(bf16[1024,512]{1,0:T(8,128)(2,1)} %collective-permute-done.5), channel_id=1, source_target_pairs={{0,8},{4,12},{8,16},{12,20},{16,24},{20,28},{1,9},{5,13},{9,17},{1... | collective-permute-start | bytes 3145736 | tf_op jit(solution)/shard_map/ppermute | solution.py:20
  50.5 15.1 %collective-permute-start.2 = (bf16[144,1024]{1,0:T(8,128)(2,1)S(1)}, bf16[144,1024]{1,0:T(8,128)(2,1)S(1)}, u32[]{:S(2)}, u32[]{:S(2)}) collective-permute-start(bf16[144,1024]{1,0:T(8,128)(2,1)S(1)} %get-tuple-element.49.own_ref), channel_id=1, source_target_pairs={{0,8},{4,12},{8,16},{12,20},{16,24},{20,28},{1,9},{5,13},{9,17},{1... | collective-permute-start | bytes 884744 | tf_op jit(solution)/shard_map/ppermute | solution.py:20
  52.1 50.6 %collective-permute-start.9 = (bf16[1024,512]{1,0:T(8,128)(2,1)}, bf16[1024,512]{1,0:T(8,128)(2,1)}, u32[]{:S(2)}, u32[]{:S(2)}) collective-permute-start(bf16[1024,512]{1,0:T(8,128)(2,1)} %collective-permute-done.8), channel_id=1, source_target_pairs={{8,0},{12,4},{16,8},{20,12},{24,16},{28,20},{9,1},{13,5},{17,9},{2... | collective-permute-start | bytes 3145736 | tf_op jit(solution)/shard_map/ppermute | solution.py:20
  59.5 43.3 %collective-permute-start.10 = (bf16[1024,512]{1,0:T(8,128)(2,1)}, bf16[1024,512]{1,0:T(8,128)(2,1)}, u32[]{:S(2)}, u32[]{:S(2)}) collective-permute-start(bf16[1024,512]{1,0:T(8,128)(2,1)} %collective-permute-done.7), channel_id=1, source_target_pairs={{0,8},{4,12},{8,16},{12,20},{16,24},{20,28},{1,9},{5,13},{9,17},{1... | collective-permute-start | bytes 3145736 | tf_op jit(solution)/shard_map/ppermute | solution.py:20
  66.6 30.9 %collective-permute-start.3 = (bf16[144,1024]{1,0:T(8,128)(2,1)S(1)}, bf16[144,1024]{1,0:T(8,128)(2,1)S(1)}, u32[]{:S(2)}, u32[]{:S(2)}) collective-permute-start(bf16[144,1024]{1,0:T(8,128)(2,1)S(1)} %get-tuple-element.52), channel_id=1, source_target_pairs={{0,16},{4,20},{8,24},{12,28},{1,17},{5,21},{9,25},{13,29},{2,18},{... | collective-permute-start | bytes 884744 | tf_op jit(solution)/shard_map/ppermute | solution.py:20
  100.7 23.4 %collective-permute-start.4 = (bf16[512,1024]{1,0:T(8,128)(2,1)S(1)}, bf16[512,1024]{1,0:T(8,128)(2,1)S(1)}, u32[]{:S(2)}, u32[]{:S(2)}) collective-permute-start(bf16[512,1024]{1,0:T(8,128)(2,1)S(1)} %get-tuple-element.54.own_ref), channel_id=1, source_target_pairs={{0,4},{4,0},{8,12},{12,8},{16,20},{20,16},{24,28},{28,24},{1,5},{5... | collective-permute-start | bytes 3145736 | tf_op jit(solution)/shard_map/ppermute | solution.py:25
  138.6 32.4 %collective-permute-start = (bf16[512,512]{1,0:T(8,128)(2,1)S(1)}, bf16[512,512]{1,0:T(8,128)(2,1)S(1)}, u32[]{:S(2)}, u32[]{:S(2)}) collective-permute-start(bf16[512,512]{1,0:T(8,128)(2,1)S(1)} %constant_dynamic-slice_fusion.5), channel_id=1, source_target_pairs={{0,4},{4,0},{8,12},{12,8},{16,20},{20,16},{24,28},{28,24},{1,5},{5... | collective-permute-start | bytes 1572872 | tf_op jit(solution)/shard_map/ppermute | solution.py:25
  145.1 29.1 %collective-permute-start.12 = (bf16[1024,512]{1,0:T(8,128)(2,1)}, bf16[1024,512]{1,0:T(8,128)(2,1)S(1)}, u32[]{:S(2)}, u32[]{:S(2)}) collective-permute-start(bf16[1024,512]{1,0:T(8,128)(2,1)} %fusion.5), channel_id=1, source_target_pairs={{0,2},{1,3},{2,0},{3,1},{4,6},{5,7},{6,4},{7,5},{8,10},{9,11},{10,... | collective-permute-start | bytes 3145736 | tf_op jit(solution)/shard_map/ppermute | solution.py:25
  148.4 22.2 %collective-permute-start.14 = (f32[1,512]{1,0:T(1,128)S(1)}, f32[1,512]{1,0:T(1,128)S(1)}, u32[]{:S(2)}, u32[]{:S(2)}) collective-permute-start(f32[1,512]{1,0:T(1,128)S(1)} %add.151), channel_id=1, source_target_pairs={{0,2},{1,3},{2,0},{3,1},{4,6},{5,7},{6,4},{7,5},{8,10},{9,11},{10,... | collective-permute-start | bytes 6152 | tf_op jit(solution)/shard_map/ppermute | solution.py:25
  177.1 23.3 %collective-permute-start.17 = (bf16[1024,512]{1,0:T(8,128)(2,1)S(1)}, bf16[1024,512]{1,0:T(8,128)(2,1)S(1)}, u32[]{:S(2)}, u32[]{:S(2)}) collective-permute-start(bf16[1024,512]{1,0:T(8,128)(2,1)S(1)} %fusion), channel_id=1, source_target_pairs={{0,2},{1,3},{2,0},{3,1},{4,6},{5,7},{6,4},{7,5},{8,10},{9,11},{10,... | collective-permute-start | bytes 3145736 | tf_op jit(solution)/shard_map/ppermute | solution.py:25
  178.8 24.2 %collective-permute-start.21 = (bf16[560,1024]{1,0:T(8,128)(2,1)S(1)}, bf16[560,1024]{1,0:T(8,128)(2,1)S(1)}, u32[]{:S(2)}, u32[]{:S(2)}) collective-permute-start(bf16[560,1024]{1,0:T(8,128)(2,1)S(1)} %maximum_maximum_fusion.1.refs_0_), channel_id=1, source_target_pairs={{8,0},{12,4},{16,8},{20,12},{24,16},{28,20},{9,1},{13,5},{17,9},{2... | collective-permute-start | bytes 3440648 | tf_op jit(solution)/shard_map/ppermute | solution.py:20
  180.1 28.2 %collective-permute-start.20 = (bf16[560,1024]{1,0:T(8,128)(2,1)S(1)}, bf16[560,1024]{1,0:T(8,128)(2,1)S(1)}, u32[]{:S(2)}, u32[]{:S(2)}) collective-permute-start(bf16[560,1024]{1,0:T(8,128)(2,1)S(1)} %maximum_maximum_fusion.1.refs_0_), channel_id=1, source_target_pairs={{0,8},{4,12},{8,16},{12,20},{16,24},{20,28},{1,9},{5,13},{9,17},{1... | collective-permute-start | bytes 3440648 | tf_op jit(solution)/shard_map/ppermute | solution.py:20
  202.1 38.4 %collective-permute-start.18 = (bf16[2,1024,512]{2,1,0:T(8,128)(2,1)}, bf16[2,1024,512]{2,1,0:T(8,128)(2,1)}, u32[]{:S(2)}, u32[]{:S(2)}) collective-permute-start(bf16[2,1024,512]{2,1,0:T(8,128)(2,1)} %pad_maximum_fusion), channel_id=1, source_target_pairs={{0,1},{1,0},{2,3},{3,2},{4,5},{5,4},{6,7},{7,6},{8,9},{9,8},{10,11... | collective-permute-start | bytes 6291464 | tf_op jit(solution)/shard_map/ppermute | solution.py:25
  203.0 26.4 %collective-permute-start.23 = (bf16[560,1024]{1,0:T(8,128)(2,1)S(1)}, bf16[560,1024]{1,0:T(8,128)(2,1)}, u32[]{:S(2)}, u32[]{:S(2)}) collective-permute-start(bf16[560,1024]{1,0:T(8,128)(2,1)S(1)} %collective-permute-done.21), channel_id=1, source_target_pairs={{8,0},{12,4},{16,8},{20,12},{24,16},{28,20},{9,1},{13,5},{17,9},{2... | collective-permute-start | bytes 3440648 | tf_op jit(solution)/shard_map/ppermute | solution.py:20
  208.4 26.5 %collective-permute-start.22 = (bf16[560,1024]{1,0:T(8,128)(2,1)S(1)}, bf16[560,1024]{1,0:T(8,128)(2,1)}, u32[]{:S(2)}, u32[]{:S(2)}) collective-permute-start(bf16[560,1024]{1,0:T(8,128)(2,1)S(1)} %collective-permute-done.20), channel_id=1, source_target_pairs={{0,8},{4,12},{8,16},{12,20},{16,24},{20,28},{1,9},{5,13},{9,17},{1... | collective-permute-start | bytes 3440648 | tf_op jit(solution)/shard_map/ppermute | solution.py:20
  229.4 26.0 %collective-permute-start.24 = (bf16[560,1024]{1,0:T(8,128)(2,1)}, bf16[560,1024]{1,0:T(8,128)(2,1)}, u32[]{:S(2)}, u32[]{:S(2)}) collective-permute-start(bf16[560,1024]{1,0:T(8,128)(2,1)} %collective-permute-done.23), channel_id=1, source_target_pairs={{8,0},{12,4},{16,8},{20,12},{24,16},{28,20},{9,1},{13,5},{17,9},{2... | collective-permute-start | bytes 3440648 | tf_op jit(solution)/shard_map/ppermute | solution.py:20
  234.9 26.3 %collective-permute-start.25 = (bf16[560,1024]{1,0:T(8,128)(2,1)}, bf16[560,1024]{1,0:T(8,128)(2,1)}, u32[]{:S(2)}, u32[]{:S(2)}) collective-permute-start(bf16[560,1024]{1,0:T(8,128)(2,1)} %collective-permute-done.22), channel_id=1, source_target_pairs={{0,8},{4,12},{8,16},{12,20},{16,24},{20,28},{1,9},{5,13},{9,17},{1... | collective-permute-start | bytes 3440648 | tf_op jit(solution)/shard_map/ppermute | solution.py:20
  242.6 22.0 %collective-permute-start.19 = (bf16[4,16,512]{2,1,0:T(8,128)(2,1)S(1)}, bf16[4,16,512]{2,1,0:T(8,128)(2,1)S(1)}, u32[]{:S(2)}, u32[]{:S(2)}) collective-permute-start(bf16[4,16,512]{2,1,0:T(8,128)(2,1)S(1)} %pad_maximum_fusion.7), channel_id=1, source_target_pairs={{0,8},{4,12},{8,16},{12,20},{16,24},{20,28},{1,9},{5,13},{9,17},{1... | collective-permute-start | bytes 196616 | tf_op jit(solution)/shard_map/ppermute | solution.py:20
  268.8 27.6 %collective-permute-start.26 = (bf16[528,592]{1,0:T(8,128)(2,1)}, bf16[528,592]{1,0:T(8,128)(2,1)}, u32[]{:S(2)}, u32[]{:S(2)}) collective-permute-start(bf16[528,592]{1,0:T(8,128)(2,1)} %shard_map.182), channel_id=1, source_target_pairs={{0,4},{4,0},{8,12},{12,8},{16,20},{20,16},{24,28},{28,24},{1,5},{5... | collective-permute-start | bytes 1875464 | tf_op jit(solution)/shard_map/ppermute | solution.py:25
  293.1 22.4 %collective-permute-start.36 = (bf16[528,512]{1,0:T(8,128)(2,1)}, bf16[528,512]{1,0:T(8,128)(2,1)}, u32[]{:S(2)}, u32[]{:S(2)}) collective-permute-start(bf16[528,512]{1,0:T(8,128)(2,1)} %shard_map.189), channel_id=1, source_target_pairs={{0,4},{4,0},{8,12},{12,8},{16,20},{20,16},{24,28},{28,24},{1,5},{5... | collective-permute-start | bytes 1622024 | tf_op jit(solution)/shard_map/ppermute | solution.py:25
  309.5 17.8 %collective-permute-start.16 = (bf16[512,512]{1,0:T(8,128)(2,1)S(1)}, bf16[512,512]{1,0:T(8,128)(2,1)S(1)}, u32[]{:S(2)}, u32[]{:S(2)}) collective-permute-start(bf16[512,512]{1,0:T(8,128)(2,1)S(1)} %get-tuple-element.94), channel_id=1, source_target_pairs={{0,4},{4,0},{8,12},{12,8},{16,20},{20,16},{24,28},{28,24},{1,5},{5... | collective-permute-start | bytes 1572872 | tf_op jit(solution)/shard_map/ppermute | solution.py:25
  (63 other events, 838.4 us)

commit v4 on v3

--- a/solution.py
+++ b/solution.py
@@ -14,9 +14,13 @@
 BF16 = jnp.bfloat16
 
 
-def z_shift(value, by):
+def z_shift(value, by, hops=1):
     n = lax.axis_size("seq")
-    pairs = [(i, i + 2 * by) for i in range(n) if 0 <= i + 2 * by < n]
+    pairs = [
+        (i, i + 2 * by)
+        for i in range(n)
+        if 0 <= i + 2 * by < n and 0 <= i - 2 * by * (hops - 1) < n
+    ]
     return lax.ppermute(value, "seq", pairs)
 
 
@@ -39,9 +43,9 @@
 
 def z_line(value, place):
     ups, downs = [value], [value]
-    for _ in range(1, 4):
-        ups.append(z_shift(ups[-1], 1))
-        downs.append(z_shift(downs[-1], -1))
+    for step in range(1, 4):
+        ups.append(z_shift(ups[-1], 1, step))
+        downs.append(z_shift(downs[-1], -1, step))
     early, low, high = place >= 1, place == 0, place == 3
     blocks = [
         value,
@@ -145,8 +149,13 @@
     early, early_decay = jnp.where(first, own, far), jnp.where(first, own_decay, far_decay)
     late, late_decay = jnp.where(first, far, own), jnp.where(first, far_decay, own_decay)
     window = jnp.exp(late_decay) * early + late
+    decay = early_decay + late_decay
+    half = window_ref.shape[1]
+    if half < window.shape[1]:
+        window = jnp.where(first, window[:, :half], window[:, half:])
+        decay = jnp.where(first, decay[:, :half], decay[:, half:])
     window_ref[...] = window
-    put_payload(payload_ref, window, early_decay + late_decay)
+    put_payload(payload_ref, window, decay)
     early_ref[...] = early
     early_decay_ref[...] = early_decay
 
@@ -173,6 +182,21 @@
     put_payload(payload_ref, window, own_decay + far_decay)
     before_out[...] = far
     decay_out[...] = far_decay
+
+
+def close_kernel(before_ref, decay_ref, far_ref, out_ref):
+    far, _ = get_payload(far_ref)
+    out_ref[...] = (before_ref[...] + jnp.exp(decay_ref[...]) * far).astype(BF16)
+
+
+def entering_halves(y_ref, early_ref, early_decay_ref, own_ref, other_ref):
+    first = y_ref[0] == 0
+    own, other = own_ref[...].astype(F32), other_ref[...].astype(F32)
+    before = jnp.concatenate(
+        [jnp.where(first, own, other), jnp.where(first, other, own)], axis=1
+    )
+    late = jnp.exp(early_decay_ref[...]) * before + early_ref[...]
+    return jnp.where(first, before, late)
 
 
 def entering(y_ref, early_ref, early_decay_ref, before_ref, decay_ref, far_ref):
@@ -243,9 +267,8 @@
     y_ref,
     early_ref,
     early_decay_ref,
-    before_ref,
-    decay_ref,
-    far_ref,
+    own_ref,
+    other_ref,
     first_ref,
     within_ref,
     c_ref,
@@ -258,7 +281,7 @@
 ):
     tokens, channels = within_ref.shape
     table = spread(channels // HEAD_CHANNELS)
-    state = entering(y_ref, early_ref, early_decay_ref, before_ref, decay_ref, far_ref)
+    state = entering_halves(y_ref, early_ref, early_decay_ref, own_ref, other_ref)
     for start in range(0, tokens, GROUP):
         mixed, decay = finish_group(start, state, within_ref, c_ref, code_ref, rate_ref, table)
         state = state * decay + first_ref[...]
@@ -504,13 +527,15 @@
     return lax.dynamic_index_in_dim(stack, index, 0, False)
 
 
-def exchange_states(end, payload, y):
-    full, packed = shape(end.shape, F32), shape(payload.shape, BF16)
-    row = shape((1, end.shape[1]), F32)
+def exchange_states(end, payload, y, split):
+    part = end.shape[1] // 2 if split else end.shape[1]
+    full, row = shape(end.shape, F32), shape((1, end.shape[1]), F32)
+    piece, packed = shape((end.shape[0], part), F32), shape((payload.shape[0], part), BF16)
+    piece_row = shape((1, part), F32)
     flag = y[None].astype(jnp.int32)
     far = y_swap(payload)
     window, payload, early, early_decay = whole_call(
-        pair_kernel, [full, packed, full, row], end.size, flag, end, payload, far
+        pair_kernel, [piece, packed, full, row], end.size, flag, end, payload, far
     )
     parts = ()
     reach, size = 1, lax.axis_size("seq") // 2
@@ -518,7 +543,7 @@
         far = z_shift(payload, reach)
         window, payload, *parts = whole_call(
             step_kernel if parts else start_kernel,
-            [full, packed, full, row],
+            [piece, packed, piece, piece_row],
             end.size,
             window,
             payload,
@@ -527,6 +552,9 @@
         )
         reach *= 2
     far = z_shift(payload, reach)
+    if split:
+        (own,) = whole_call(close_kernel, [shape(piece.shape, BF16)], end.size, *parts, far)
+        return (flag, early, early_decay, own, y_swap(own))
     return (flag, early, early_decay, *parts, far)
 
 
@@ -592,7 +620,7 @@
         x_in, bc_in[:, :state_width], step_in, code_one, rate_one
     )
     within_one = within_blocks(x_in, bc_in, step_in, code_one, rate_one, skip_gain[0][None, :])
-    carried_one = exchange_states(end_one, payload_one, y)
+    carried_one = exchange_states(end_one, payload_one, y, True)
     scaled, square_own = whole_call(
         gated_kernel,
         [shape((tokens, width), BF16), shape((1, tokens), F32)],
@@ -735,7 +763,7 @@
             last_kernel,
             [shape((tokens, half), F32), shape((1, tokens), F32)],
             4 * x.size * state_width,
-            *exchange_states(end, payload, y),
+            *exchange_states(end, payload, y, False),
             first_two,
             within,
             bc_two[:, state_width:],

time: 366 us -> 340 us (0.929)
  starting transfers between devices: 60.3 us -> 46.4 us
  waiting for transfers between devices: 193 us -> 182 us
    ppermute x20, starting transfers between devices: 45.7 us -> 30.8 us  [z_shift(): return lax.ppermute(value, 'seq', pairs)]
    ppermute x20 -> x21, waiting for transfers between devices: 88.5 us -> 82 us  [flip(): return lax.ppermute(value, axis, [(i, i ^ bit) for i in range(n)])]
    ppermute x20, waiting for transfers between devices: 104 us -> 100 us  [z_shift(): return lax.ppermute(value, 'seq', pairs)]
    ppermute x20 -> x21, starting transfers between devices: 14.6 us -> 15.6 us  [flip(): return lax.ppermute(value, axis, [(i, i ^ bit) for i in range(n)])]
    unnamed x98 -> x100, local copies, waits for them, and re-layouts: 16.7 us -> 16.7 us
    pallas_call x13 -> x14, Pallas kernels: 22 us -> 22 us  [whole_call(): pl.pallas_call(kernel, out_shape=outs, in_specs=[SMEM_SPEC if a.shape ==...]
  transfers between devices with their start and end apart: 40 -> 41, of which waited for: 23 -> 25; matrix products, arithmetic and copies ran while one was open for 8% -> 8% of each run, Pallas kernels for 12% -> 13%
where the time goes in v4:
time: 340 us; the launch traced here: 338 us
  waiting for transfers between devices  182 us (54%)
  Pallas kernels  55.2 us (16%)
  starting transfers between devices  46.4 us (14%)
  local copies, waits for them, and re-layouts  26.4 us (8%)
  other arithmetic  20.3 us (6%)
  blocking collectives  5.75 us (2%)
    ppermute x20, waiting for transfers between devices, z_shift(): return lax.ppermute(value, 'seq', pairs)  100 us
    ppermute x21, waiting for transfers between devices, flip(): return lax.ppermute(value, axis, [(i, i ^ bit) for i in range(n)])  82 us
    ppermute x20, starting transfers between devices, z_shift(): return lax.ppermute(value, 'seq', pairs)  30.8 us
    pallas_call x14, Pallas kernels, whole_call(): pl.pallas_call(kernel, out_shape=outs, in_specs=[SMEM_SPEC if a.shape ==...  22 us
    unnamed x100, local copies, waits for them, and re-layouts  16.7 us
    ppermute x21, starting transfers between devices, flip(): return lax.ppermute(value, axis, [(i, i ^ bit) for i in range(n)])  15.6 us
    pallas_call x4, Pallas kernels, in_call(): pl.pallas_call(functools.partial(in_kernel, place), out_shape=shape((rows...  11.6 us
    pallas_call x3, Pallas kernels, within_blocks(): pl.pallas_call(within_kernel, name='within', grid=(tokens // GROUP,), out...  8.34 us
  transfers between devices with their start and end apart: 41, of which 25 were waited for; matrix products, arithmetic and copies ran while one was open for 8% of the time, Pallas kernels for 13%

profile of v4, /device:TPU:28, one launch (start us, length us, event | category | flops | bytes accessed | tf_op | source)
XLA Modules:
  0.0 337.5 jit_solution(1614973061543456044)
XLA Ops:
  0.6 3.5 %collective-permute-start.7 = (bf16[1024,512]{1,0:T(8,128)(2,1)}, bf16[1024,512]{1,0:T(8,128)(2,1)}, u32[]{:S(2)}, u32[]{:S(2)}) collective-permute-start(bf16[1024,512]{1,0:T(8,128)(2,1)} %refs_0_.1), channel_id=1, source_target_pairs={{8,0},{12,4},{16,8},{20,12},{24,16},{28,20},{9,1},{13,5},{17,9},{2... | collective-permute-start | bytes 3145736 | tf_op jit(solution)/shard_map/ppermute | solution.py:24
  5.4 20.4 %collective-permute-done.7 = bf16[1024,512]{1,0:T(8,128)(2,1)} collective-permute-done((bf16[1024,512]{1,0:T(8,128)(2,1)}, bf16[1024,512]{1,0:T(8,128)(2,1)}, u32[]{:S(2)}, u32[]{:S(2)}) %collective-permute-start.7) | collective-permute-done | bytes 1048608 | tf_op jit(solution)/shard_map/ppermute | solution.py:24
  27.5 3.5 %collective-permute-done.6 = bf16[1024,512]{1,0:T(8,128)(2,1)} collective-permute-done((bf16[1024,512]{1,0:T(8,128)(2,1)}, bf16[1024,512]{1,0:T(8,128)(2,1)}, u32[]{:S(2)}, u32[]{:S(2)}) %collective-permute-start.6) | collective-permute-done | bytes 1048608 | tf_op jit(solution)/shard_map/ppermute | solution.py:24
  36.9 3.8 %shard_map.176 = (f32[128,1024]{1,0:T(8,128)S(1)}, f32[128,1024]{1,0:T(8,128)S(1)}, bf16[144,1024]{1,0:T(8,128)(2,1)S(1)}) custom-call(bf16[512,1024]{1,0:T(8,128)(2,1)S(1)} %copy-done.14, bf16[512,128]{1,0:T(8,128)(2,1)S(1)} %get-tuple-element.107.b_ref, f32[512,16]{1,0:T(8,128)S(1)} %copy.25.step_ref, s32[512,16]{1,0:T(8,128)S(1)} %bitcast.48, ...), custom_call_target="tpu_custom_call" | custom-call | flops 268435456 | bytes 2588736 | tf_op jit(solution)/shard_map/pallas_call | solution.py:326
  41.3 7.2 %collective-permute-done.1.far_ref = bf16[144,1024]{1,0:T(8,128)(2,1)} collective-permute-done((bf16[144,1024]{1,0:T(8,128)(2,1)S(1)}, bf16[144,1024]{1,0:T(8,128)(2,1)}, u32[]{:S(2)}, u32[]{:S(2)}) %collective-permute-start.1) | collective-permute-done | bytes 294944 | tf_op jit(solution)/shard_map/ppermute | solution.py:29
  52.6 5.9 %collective-permute-done.8 = bf16[1024,512]{1,0:T(8,128)(2,1)} collective-permute-done((bf16[1024,512]{1,0:T(8,128)(2,1)}, bf16[1024,512]{1,0:T(8,128)(2,1)}, u32[]{:S(2)}, u32[]{:S(2)}) %collective-permute-start.8) | collective-permute-done | bytes 1048608 | tf_op jit(solution)/shard_map/ppermute | solution.py:24
  62.7 6.4 %collective-permute-done.3.far_ref = bf16[144,512]{1,0:T(8,128)(2,1)S(1)} collective-permute-done((bf16[144,512]{1,0:T(8,128)(2,1)S(1)}, bf16[144,512]{1,0:T(8,128)(2,1)S(1)}, u32[]{:S(2)}, u32[]{:S(2)}) %collective-permute-start.3) | collective-permute-done | bytes 147488 | tf_op jit(solution)/shard_map/ppermute | solution.py:24
  69.8 3.4 within.3.within_ref
  74.3 3.4 %shard_map.180 = (bf16[512,1024]{1,0:T(8,128)(2,1)S(1)}, f32[1,512]{1,0:T(1,128)S(1)}) custom-call(s32[1]{0:T(128)} %bitcast.y_ref, f32[128,1024]{1,0:T(8,128)S(1)} %get-tuple-element.46.early_ref, f32[1,1024]{1,0:T(1,128)S(1)} %get-tuple-element.47.early_decay_ref, bf16[128,512]{1,0:T(8,128)(2,1)S(1)} %shard_map.179.own_ref, ...), custom_call_target="tpu_custom_call" | custom-call | flops 268435456 | bytes 5679172 | tf_op jit(solution)/shard_map/pallas_call | solution.py:326
  79.7 6.0 %collective-permute-done.11 = bf16[1024,512]{1,0:T(8,128)(2,1)} collective-permute-done((bf16[1024,512]{1,0:T(8,128)(2,1)}, bf16[1024,512]{1,0:T(8,128)(2,1)}, u32[]{:S(2)}, u32[]{:S(2)}) %collective-permute-start.11) | collective-permute-done | bytes 1048608 | tf_op jit(solution)/shard_map/ppermute | solution.py:24
  87.8 12.2 %collective-permute-done.5.far_ref = bf16[512,1024]{1,0:T(8,128)(2,1)S(1)} collective-permute-done((bf16[512,1024]{1,0:T(8,128)(2,1)S(1)}, bf16[512,1024]{1,0:T(8,128)(2,1)S(1)}, u32[]{:S(2)}, u32[]{:S(2)}) %collective-permute-start.5) | collective-permute-done | bytes 1048608 | tf_op jit(solution)/shard_map/ppermute | solution.py:29
  103.4 7.9 %out.1 = (bf16[2,1024,512]{2,1,0:T(8,128)(2,1)S(1)}, f32[2,1024,512]{2,1,0:T(8,128)S(1)}) custom-call(s32[9]{0:T(128)S(1)} %stack.116.where_ref, bf16[512,1024]{1,0:T(8,128)(2,1)S(1)} %copy-done.28, bf16[512,1024]{1,0:T(8,128)(2,1)S(1)} %copy-done.30, bf16[1024,512]{1,0:T(8,128)(2,1)S(1)} %copy-done.26, bf16[1024,512]{1,0:T(8,128)(2,1)S(1)} %get-tuple-element.97.refs_1_, ...), custom_call_target="tpu_custom_call" | custom-call | flops 4294967296 | bytes 6291456 | tf_op jit(solution)/shard_map/out/pallas_call | solution.py:488
  117.6 3.3 fusion.5
  124.4 22.0 %collective-permute-done.15 = f32[1,512]{1,0:T(1,128)S(1)} collective-permute-done((f32[1,512]{1,0:T(1,128)S(1)}, f32[1,512]{1,0:T(1,128)S(1)}, u32[]{:S(2)}, u32[]{:S(2)}) %collective-permute-start.15) | collective-permute-done | bytes 2080 | tf_op jit(solution)/shard_map/ppermute | solution.py:29
  157.9 18.3 %collective-permute-done.18 = bf16[1024,512]{1,0:T(8,128)(2,1)S(1)} collective-permute-done((bf16[1024,512]{1,0:T(8,128)(2,1)S(1)}, bf16[1024,512]{1,0:T(8,128)(2,1)S(1)}, u32[]{:S(2)}, u32[]{:S(2)}) %collective-permute-start.18) | collective-permute-done | bytes 1048608 | tf_op jit(solution)/shard_map/ppermute | solution.py:29
  186.1 23.2 %collective-permute-done.23 = bf16[560,1024]{1,0:T(8,128)(2,1)} collective-permute-done((bf16[560,1024]{1,0:T(8,128)(2,1)S(1)}, bf16[560,1024]{1,0:T(8,128)(2,1)}, u32[]{:S(2)}, u32[]{:S(2)}) %collective-permute-start.23) | collective-permute-done | bytes 1146912 | tf_op jit(solution)/shard_map/ppermute | solution.py:24
  218.8 16.7 %collective-permute-done.26 = bf16[560,1024]{1,0:T(8,128)(2,1)} collective-permute-done((bf16[560,1024]{1,0:T(8,128)(2,1)}, bf16[560,1024]{1,0:T(8,128)(2,1)}, u32[]{:S(2)}, u32[]{:S(2)}) %collective-permute-start.26) | collective-permute-done | bytes 1146912 | tf_op jit(solution)/shard_map/ppermute | solution.py:24
  239.1 3.6 %shard_map.183 = bf16[528,592]{1,0:T(8,128)(2,1)} custom-call(s32[5]{0:T(128)S(1)} %stack.128.where_ref, bf16[4,1040,512]{2,1,0:T(8,128)(2,1)S(1)} %maximum_maximum_fusion.hidden_ref, bf16[560,1024]{1,0:T(8,128)(2,1)S(1)} %maximum_maximum_fusion.1.refs_0_, bf16[560,1024]{1,0:T(8,128)(2,1)S(1)} %get-tuple-element.93.refs_1_, ...), custom_call_target="tpu_custom_call" | custom-call | flops 1280311296 | bytes 6684672 | tf_op jit(solution)/shard_map/pallas_call | solution.py:505
  246.0 8.4 %collective-permute-done.30 = f32[1024]{0:T(1024)S(1)} collective-permute-done((f32[1024]{0:T(1024)S(1)}, f32[1024]{0:T(1024)S(1)}, u32[]{:S(2)}, u32[]{:S(2)}) %collective-permute-start.30) | collective-permute-done | bytes 4128 | tf_op jit(solution)/shard_map/ppermute | solution.py:29
  255.9 4.1 %collective-permute-done.31 = f32[16]{0:T(128)S(1)} collective-permute-done((f32[16]{0:T(128)S(1)}, f32[16]{0:T(128)S(1)}, u32[]{:S(2)}, u32[]{:S(2)}) %collective-permute-start.31) | collective-permute-done | bytes 96 | tf_op jit(solution)/shard_map/ppermute | solution.py:24
  270.6 3.2 shard_map.184
  276.3 4.9 %collective-permute-done.32 = bf16[512,64]{1,0:T(8,128)(2,1)} collective-permute-done((bf16[512,64]{1,0:T(8,128)(2,1)}, bf16[512,64]{1,0:T(8,128)(2,1)}, u32[]{:S(2)}, u32[]{:S(2)}) %collective-permute-start.32) | collective-permute-done | bytes 65568 | tf_op jit(solution)/shard_map/ppermute | solution.py:29
  317.5 8.5 %collective-permute-done.36.far_ref = bf16[144,512]{1,0:T(8,128)(2,1)S(1)} collective-permute-done((bf16[144,512]{1,0:T(8,128)(2,1)S(1)}, bf16[144,512]{1,0:T(8,128)(2,1)S(1)}, u32[]{:S(2)}, u32[]{:S(2)}) %collective-permute-start.36) | collective-permute-done | bytes 147488 | tf_op jit(solution)/shard_map/ppermute | solution.py:24
  330.5 5.7 %psum.7 = f32[512]{0:T(512)S(1)} all-reduce(f32[512]{0:T(512)S(1)} %bitcast.60), channel_id=1, replica_groups=mesh['seq'=8,'head'=4] {'head'}, use_global_device_ids=true, to_apply=%region_1.2 | all-reduce | flops 512 | bytes 4096 | tf_op jit(solution)/shard_map/psum | solution.py:775
  (238 shorter events, 130.4 us)
Async XLA Ops:
  0.6 25.2 %collective-permute-start.7 = (bf16[1024,512]{1,0:T(8,128)(2,1)}, bf16[1024,512]{1,0:T(8,128)(2,1)}, u32[]{:S(2)}, u32[]{:S(2)}) collective-permute-start(bf16[1024,512]{1,0:T(8,128)(2,1)} %refs_0_.1), channel_id=1, source_target_pairs={{8,0},{12,4},{16,8},{20,12},{24,16},{28,20},{9,1},{13,5},{17,9},{2... | collective-permute-start | bytes 3145736 | tf_op jit(solution)/shard_map/ppermute | solution.py:24
  4.1 26.8 %collective-permute-start.6 = (bf16[1024,512]{1,0:T(8,128)(2,1)}, bf16[1024,512]{1,0:T(8,128)(2,1)}, u32[]{:S(2)}, u32[]{:S(2)}) collective-permute-start(bf16[1024,512]{1,0:T(8,128)(2,1)} %refs_0_.1), channel_id=1, source_target_pairs={{0,8},{4,12},{8,16},{12,20},{16,24},{20,28},{1,9},{5,13},{9,17},{1... | collective-permute-start | bytes 3145736 | tf_op jit(solution)/shard_map/ppermute | solution.py:24
  25.9 25.1 %collective-permute-start.9 = (bf16[1024,512]{1,0:T(8,128)(2,1)}, bf16[1024,512]{1,0:T(8,128)(2,1)}, u32[]{:S(2)}, u32[]{:S(2)}) collective-permute-start(bf16[1024,512]{1,0:T(8,128)(2,1)} %collective-permute-done.7), channel_id=1, source_target_pairs={{8,0},{12,4},{16,8},{20,12},{9,1},{13,5},{17,9},{21,13},{10,2},{14... | collective-permute-start | bytes 3145736 | tf_op jit(solution)/shard_map/ppermute | solution.py:24
  31.0 27.5 %collective-permute-start.8 = (bf16[1024,512]{1,0:T(8,128)(2,1)}, bf16[1024,512]{1,0:T(8,128)(2,1)}, u32[]{:S(2)}, u32[]{:S(2)}) collective-permute-start(bf16[1024,512]{1,0:T(8,128)(2,1)} %collective-permute-done.6), channel_id=1, source_target_pairs={{8,16},{12,20},{16,24},{20,28},{9,17},{13,21},{17,25},{21,29},{10,... | collective-permute-start | bytes 3145736 | tf_op jit(solution)/shard_map/ppermute | solution.py:24
  49.6 10.8 %collective-permute-start.2 = (bf16[144,512]{1,0:T(8,128)(2,1)S(1)}, bf16[144,512]{1,0:T(8,128)(2,1)S(1)}, u32[]{:S(2)}, u32[]{:S(2)}) collective-permute-start(bf16[144,512]{1,0:T(8,128)(2,1)S(1)} %get-tuple-element.49.own_ref), channel_id=1, source_target_pairs={{0,8},{4,12},{8,16},{12,20},{16,24},{20,28},{1,9},{5,13},{9,17},{1... | collective-permute-start | bytes 442376 | tf_op jit(solution)/shard_map/ppermute | solution.py:24
  51.0 28.7 %collective-permute-start.10 = (bf16[1024,512]{1,0:T(8,128)(2,1)}, bf16[1024,512]{1,0:T(8,128)(2,1)}, u32[]{:S(2)}, u32[]{:S(2)}) collective-permute-start(bf16[1024,512]{1,0:T(8,128)(2,1)} %collective-permute-done.9), channel_id=1, source_target_pairs={{8,0},{12,4},{9,1},{13,5},{10,2},{14,6},{11,3},{15,7}} | collective-permute-start | bytes 3145736 | tf_op jit(solution)/shard_map/ppermute | solution.py:24
  58.5 27.2 %collective-permute-start.11 = (bf16[1024,512]{1,0:T(8,128)(2,1)}, bf16[1024,512]{1,0:T(8,128)(2,1)}, u32[]{:S(2)}, u32[]{:S(2)}) collective-permute-start(bf16[1024,512]{1,0:T(8,128)(2,1)} %collective-permute-done.8), channel_id=1, source_target_pairs={{16,24},{20,28},{17,25},{21,29},{18,26},{22,30},{19,27},{23,31}} | collective-permute-start | bytes 3145736 | tf_op jit(solution)/shard_map/ppermute | solution.py:24
  77.7 22.3 %collective-permute-start.5 = (bf16[512,1024]{1,0:T(8,128)(2,1)S(1)}, bf16[512,1024]{1,0:T(8,128)(2,1)S(1)}, u32[]{:S(2)}, u32[]{:S(2)}) collective-permute-start(bf16[512,1024]{1,0:T(8,128)(2,1)S(1)} %get-tuple-element.54.own_ref), channel_id=1, source_target_pairs={{0,4},{4,0},{8,12},{12,8},{16,20},{20,16},{24,28},{28,24},{1,5},{5... | collective-permute-start | bytes 3145736 | tf_op jit(solution)/shard_map/ppermute | solution.py:29
  114.4 32.9 %collective-permute-start = (bf16[512,512]{1,0:T(8,128)(2,1)S(1)}, bf16[512,512]{1,0:T(8,128)(2,1)}, u32[]{:S(2)}, u32[]{:S(2)}) collective-permute-start(bf16[512,512]{1,0:T(8,128)(2,1)S(1)} %constant_dynamic-slice_fusion.5), channel_id=1, source_target_pairs={{0,4},{4,0},{8,12},{12,8},{16,20},{20,16},{24,28},{28,24},{1,5},{5... | collective-permute-start | bytes 1572872 | tf_op jit(solution)/shard_map/ppermute | solution.py:29
  120.9 29.1 %collective-permute-start.13 = (bf16[1024,512]{1,0:T(8,128)(2,1)}, bf16[1024,512]{1,0:T(8,128)(2,1)S(1)}, u32[]{:S(2)}, u32[]{:S(2)}) collective-permute-start(bf16[1024,512]{1,0:T(8,128)(2,1)} %fusion.5), channel_id=1, source_target_pairs={{0,2},{1,3},{2,0},{3,1},{4,6},{5,7},{6,4},{7,5},{8,10},{9,11},{10,... | collective-permute-start | bytes 3145736 | tf_op jit(solution)/shard_map/ppermute | solution.py:29
  123.9 22.5 %collective-permute-start.15 = (f32[1,512]{1,0:T(1,128)S(1)}, f32[1,512]{1,0:T(1,128)S(1)}, u32[]{:S(2)}, u32[]{:S(2)}) collective-permute-start(f32[1,512]{1,0:T(1,128)S(1)} %add.151), channel_id=1, source_target_pairs={{0,2},{1,3},{2,0},{3,1},{4,6},{5,7},{6,4},{7,5},{8,10},{9,11},{10,... | collective-permute-start | bytes 6152 | tf_op jit(solution)/shard_map/ppermute | solution.py:29
  153.0 23.3 %collective-permute-start.18 = (bf16[1024,512]{1,0:T(8,128)(2,1)S(1)}, bf16[1024,512]{1,0:T(8,128)(2,1)S(1)}, u32[]{:S(2)}, u32[]{:S(2)}) collective-permute-start(bf16[1024,512]{1,0:T(8,128)(2,1)S(1)} %fusion), channel_id=1, source_target_pairs={{0,2},{1,3},{2,0},{3,1},{4,6},{5,7},{6,4},{7,5},{8,10},{9,11},{10,... | collective-permute-start | bytes 3145736 | tf_op jit(solution)/shard_map/ppermute | solution.py:29
  154.6 24.3 %collective-permute-start.22 = (bf16[560,1024]{1,0:T(8,128)(2,1)S(1)}, bf16[560,1024]{1,0:T(8,128)(2,1)S(1)}, u32[]{:S(2)}, u32[]{:S(2)}) collective-permute-start(bf16[560,1024]{1,0:T(8,128)(2,1)S(1)} %maximum_maximum_fusion.1.refs_0_), channel_id=1, source_target_pairs={{8,0},{12,4},{16,8},{20,12},{24,16},{28,20},{9,1},{13,5},{17,9},{2... | collective-permute-start | bytes 3440648 | tf_op jit(solution)/shard_map/ppermute | solution.py:24
  156.4 26.7 %collective-permute-start.21 = (bf16[560,1024]{1,0:T(8,128)(2,1)S(1)}, bf16[560,1024]{1,0:T(8,128)(2,1)S(1)}, u32[]{:S(2)}, u32[]{:S(2)}) collective-permute-start(bf16[560,1024]{1,0:T(8,128)(2,1)S(1)} %maximum_maximum_fusion.1.refs_0_), channel_id=1, source_target_pairs={{0,8},{4,12},{8,16},{12,20},{16,24},{20,28},{1,9},{5,13},{9,17},{1... | collective-permute-start | bytes 3440648 | tf_op jit(solution)/shard_map/ppermute | solution.py:24
  178.0 36.9 %collective-permute-start.19 = (bf16[2,1024,512]{2,1,0:T(8,128)(2,1)}, bf16[2,1024,512]{2,1,0:T(8,128)(2,1)}, u32[]{:S(2)}, u32[]{:S(2)}) collective-permute-start(bf16[2,1024,512]{2,1,0:T(8,128)(2,1)} %pad_maximum_fusion), channel_id=1, source_target_pairs={{0,1},{1,0},{2,3},{3,2},{4,5},{5,4},{6,7},{7,6},{8,9},{9,8},{10,11... | collective-permute-start | bytes 6291464 | tf_op jit(solution)/shard_map/ppermute | solution.py:29
  183.1 26.2 %collective-permute-start.23 = (bf16[560,1024]{1,0:T(8,128)(2,1)S(1)}, bf16[560,1024]{1,0:T(8,128)(2,1)}, u32[]{:S(2)}, u32[]{:S(2)}) collective-permute-start(bf16[560,1024]{1,0:T(8,128)(2,1)S(1)} %collective-permute-done.21), channel_id=1, source_target_pairs={{8,16},{12,20},{16,24},{20,28},{9,17},{13,21},{17,25},{21,29},{10,... | collective-permute-start | bytes 3440648 | tf_op jit(solution)/shard_map/ppermute | solution.py:24
  184.5 34.3 %collective-permute-start.25 = (bf16[560,1024]{1,0:T(8,128)(2,1)}, bf16[560,1024]{1,0:T(8,128)(2,1)}, u32[]{:S(2)}, u32[]{:S(2)}) collective-permute-start(bf16[560,1024]{1,0:T(8,128)(2,1)} %collective-permute-done.24), channel_id=1, source_target_pairs={{8,0},{12,4},{9,1},{13,5},{10,2},{14,6},{11,3},{15,7}} | collective-permute-start | bytes 3440648 | tf_op jit(solution)/shard_map/ppermute | solution.py:24
  209.3 26.2 %collective-permute-start.26 = (bf16[560,1024]{1,0:T(8,128)(2,1)}, bf16[560,1024]{1,0:T(8,128)(2,1)}, u32[]{:S(2)}, u32[]{:S(2)}) collective-permute-start(bf16[560,1024]{1,0:T(8,128)(2,1)} %collective-permute-done.23), channel_id=1, source_target_pairs={{16,24},{20,28},{17,25},{21,29},{18,26},{22,30},{19,27},{23,31}} | collective-permute-start | bytes 3440648 | tf_op jit(solution)/shard_map/ppermute | solution.py:24
  217.0 21.6 %collective-permute-start.20 = (bf16[4,16,512]{2,1,0:T(8,128)(2,1)S(1)}, bf16[4,16,512]{2,1,0:T(8,128)(2,1)S(1)}, u32[]{:S(2)}, u32[]{:S(2)}) collective-permute-start(bf16[4,16,512]{2,1,0:T(8,128)(2,1)S(1)} %pad_maximum_fusion.7), channel_id=1, source_target_pairs={{0,8},{4,12},{8,16},{12,20},{16,24},{20,28},{1,9},{5,13},{9,17},{1... | collective-permute-start | bytes 196616 | tf_op jit(solution)/shard_map/ppermute | solution.py:24
  242.7 27.9 %collective-permute-start.27 = (bf16[528,592]{1,0:T(8,128)(2,1)}, bf16[528,592]{1,0:T(8,128)(2,1)}, u32[]{:S(2)}, u32[]{:S(2)}) collective-permute-start(bf16[528,592]{1,0:T(8,128)(2,1)} %shard_map.183), channel_id=1, source_target_pairs={{0,4},{4,0},{8,12},{12,8},{16,20},{20,16},{24,28},{28,24},{1,5},{5... | collective-permute-start | bytes 1875464 | tf_op jit(solution)/shard_map/ppermute | solution.py:29
  266.7 22.4 %collective-permute-start.37 = (bf16[528,512]{1,0:T(8,128)(2,1)}, bf16[528,512]{1,0:T(8,128)(2,1)}, u32[]{:S(2)}, u32[]{:S(2)}) collective-permute-start(bf16[528,512]{1,0:T(8,128)(2,1)} %shard_map.190), channel_id=1, source_target_pairs={{0,4},{4,0},{8,12},{12,8},{16,20},{20,16},{24,28},{28,24},{1,5},{5... | collective-permute-start | bytes 1622024 | tf_op jit(solution)/shard_map/ppermute | solution.py:29
  283.6 17.2 %collective-permute-start.17 = (bf16[512,512]{1,0:T(8,128)(2,1)S(1)}, bf16[512,512]{1,0:T(8,128)(2,1)S(1)}, u32[]{:S(2)}, u32[]{:S(2)}) collective-permute-start(bf16[512,512]{1,0:T(8,128)(2,1)S(1)} %get-tuple-element.94), channel_id=1, source_target_pairs={{0,4},{4,0},{8,12},{12,8},{16,20},{20,16},{24,28},{28,24},{1,5},{5... | collective-permute-start | bytes 1572872 | tf_op jit(solution)/shard_map/ppermute | solution.py:29
  310.4 15.7 %collective-permute-start.36 = (bf16[144,512]{1,0:T(8,128)(2,1)S(1)}, bf16[144,512]{1,0:T(8,128)(2,1)S(1)}, u32[]{:S(2)}, u32[]{:S(2)}) collective-permute-start(bf16[144,512]{1,0:T(8,128)(2,1)S(1)} %get-tuple-element.69), channel_id=1, source_target_pairs={{0,16},{4,20},{8,24},{12,28},{1,17},{5,21},{9,25},{13,29},{2,18},{... | collective-permute-start | bytes 442376 | tf_op jit(solution)/shard_map/ppermute | solution.py:24
  313.4 14.9 %collective-permute-start.40 = (bf16[144,512]{1,0:T(8,128)(2,1)S(1)}, bf16[144,512]{1,0:T(8,128)(2,1)S(1)}, u32[]{:S(2)}, u32[]{:S(2)}) collective-permute-start(bf16[144,512]{1,0:T(8,128)(2,1)S(1)} %get-tuple-element.82), channel_id=1, source_target_pairs={{0,16},{4,20},{8,24},{12,28},{1,17},{5,21},{9,25},{13,29},{2,18},{... | collective-permute-start | bytes 442376 | tf_op jit(solution)/shard_map/ppermute | solution.py:24
  (65 other events, 711.2 us)

commit v5 on v4

--- a/solution.py
+++ b/solution.py
@@ -697,7 +697,10 @@
     square_two = square_two + c_swap(square_two)
     square_two = square_two + y_swap(square_two)
     all_hidden = jnp.stack([pair[0], other[0], pair[1], other[1]])
-    halo_hidden = z_shift(all_hidden[:, pair_tokens - HALO :], 1)
+    halo = z_shift(hidden[pair_tokens - HALO :], 1)
+    halo_pair = jnp.stack([halo, x_swap(halo)])
+    halo_other = c_swap(halo_pair)
+    halo_hidden = jnp.stack([halo_pair[0], halo_other[0], halo_pair[1], halo_other[1]])
     halo_square = z_shift(square_two[pair_tokens - HALO :], 1)
     all_hidden = jnp.concatenate([halo_hidden, all_hidden], axis=1)
     scale_two = lax.rsqrt(jnp.concatenate([halo_square, square_two]) / inner_count + 1e-05)

time: 340 us -> 327 us (0.962)
  waiting for transfers between devices: 182 us -> 167 us
    ppermute x20, waiting for transfers between devices: 100 us -> 82.5 us  [z_shift(): return lax.ppermute(value, 'seq', pairs)]
    ppermute x21 -> x23, waiting for transfers between devices: 82 us -> 84.9 us  [flip(): return lax.ppermute(value, axis, [(i, i ^ bit) for i in range(n)])]
    ppermute x21 -> x23, starting transfers between devices: 15.6 us -> 17 us  [flip(): return lax.ppermute(value, axis, [(i, i ^ bit) for i in range(n)])]
    unnamed x100 -> x96, local copies, waits for them, and re-layouts: 16.7 us -> 16.2 us
  transfers between devices with their start and end apart: 41 -> 43, of which waited for: 25 -> 24; matrix products, arithmetic and copies ran while one was open for 8% -> 10% of each run, Pallas kernels for 13% -> 14%
where the time goes in v5:
time: 327 us; the launch traced here: 325 us
  waiting for transfers between devices  167 us (51%)
  Pallas kernels  55.2 us (17%)
  starting transfers between devices  47.5 us (15%)
  local copies, waits for them, and re-layouts  26.1 us (8%)
  other arithmetic  21.7 us (7%)
  blocking collectives  5.65 us (2%)
    ppermute x23, waiting for transfers between devices, flip(): return lax.ppermute(value, axis, [(i, i ^ bit) for i in range(n)])  84.9 us
    ppermute x20, waiting for transfers between devices, z_shift(): return lax.ppermute(value, 'seq', pairs)  82.5 us
    ppermute x20, starting transfers between devices, z_shift(): return lax.ppermute(value, 'seq', pairs)  30.5 us
    pallas_call x14, Pallas kernels, whole_call(): pl.pallas_call(kernel, out_shape=outs, in_specs=[SMEM_SPEC if a.shape ==...  22 us
    ppermute x23, starting transfers between devices, flip(): return lax.ppermute(value, axis, [(i, i ^ bit) for i in range(n)])  17 us
    unnamed x96, local copies, waits for them, and re-layouts  16.2 us
    pallas_call x4, Pallas kernels, in_call(): pl.pallas_call(functools.partial(in_kernel, place), out_shape=shape((rows...  11.7 us
    pallas_call x3, Pallas kernels, within_blocks(): pl.pallas_call(within_kernel, name='within', grid=(tokens // GROUP,), out...  8.34 us
  transfers between devices with their start and end apart: 43, of which 24 were waited for; matrix products, arithmetic and copies ran while one was open for 10% of the time, Pallas kernels for 14%

profile of v5, /device:TPU:28, one launch (start us, length us, event | category | flops | bytes accessed | tf_op | source)
XLA Modules:
  0.0 325.2 jit_solution(17813298786834420833)
XLA Ops:
  0.6 3.5 %collective-permute-start.7 = (bf16[1024,512]{1,0:T(8,128)(2,1)}, bf16[1024,512]{1,0:T(8,128)(2,1)}, u32[]{:S(2)}, u32[]{:S(2)}) collective-permute-start(bf16[1024,512]{1,0:T(8,128)(2,1)} %refs_0_.1), channel_id=1, source_target_pairs={{8,0},{12,4},{16,8},{20,12},{24,16},{28,20},{9,1},{13,5},{17,9},{2... | collective-permute-start | bytes 3145736 | tf_op jit(solution)/shard_map/ppermute | solution.py:24
  5.4 20.4 %collective-permute-done.7 = bf16[1024,512]{1,0:T(8,128)(2,1)} collective-permute-done((bf16[1024,512]{1,0:T(8,128)(2,1)}, bf16[1024,512]{1,0:T(8,128)(2,1)}, u32[]{:S(2)}, u32[]{:S(2)}) %collective-permute-start.7) | collective-permute-done | bytes 1048608 | tf_op jit(solution)/shard_map/ppermute | solution.py:24
  27.5 3.5 %collective-permute-done.6 = bf16[1024,512]{1,0:T(8,128)(2,1)} collective-permute-done((bf16[1024,512]{1,0:T(8,128)(2,1)}, bf16[1024,512]{1,0:T(8,128)(2,1)}, u32[]{:S(2)}, u32[]{:S(2)}) %collective-permute-start.6) | collective-permute-done | bytes 1048608 | tf_op jit(solution)/shard_map/ppermute | solution.py:24
  36.9 3.8 %shard_map.176 = (f32[128,1024]{1,0:T(8,128)S(1)}, f32[128,1024]{1,0:T(8,128)S(1)}, bf16[144,1024]{1,0:T(8,128)(2,1)S(1)}) custom-call(bf16[512,1024]{1,0:T(8,128)(2,1)S(1)} %copy-done.14, bf16[512,128]{1,0:T(8,128)(2,1)S(1)} %get-tuple-element.107.b_ref, f32[512,16]{1,0:T(8,128)S(1)} %copy.25.step_ref, s32[512,16]{1,0:T(8,128)S(1)} %bitcast.50, ...), custom_call_target="tpu_custom_call" | custom-call | flops 268435456 | bytes 2588736 | tf_op jit(solution)/shard_map/pallas_call | solution.py:326
  41.3 7.2 %collective-permute-done.1.far_ref = bf16[144,1024]{1,0:T(8,128)(2,1)} collective-permute-done((bf16[144,1024]{1,0:T(8,128)(2,1)S(1)}, bf16[144,1024]{1,0:T(8,128)(2,1)}, u32[]{:S(2)}, u32[]{:S(2)}) %collective-permute-start.1) | collective-permute-done | bytes 294944 | tf_op jit(solution)/shard_map/ppermute | solution.py:29
  52.6 5.9 %collective-permute-done.8 = bf16[1024,512]{1,0:T(8,128)(2,1)} collective-permute-done((bf16[1024,512]{1,0:T(8,128)(2,1)}, bf16[1024,512]{1,0:T(8,128)(2,1)}, u32[]{:S(2)}, u32[]{:S(2)}) %collective-permute-start.8) | collective-permute-done | bytes 1048608 | tf_op jit(solution)/shard_map/ppermute | solution.py:24
  62.7 6.4 %collective-permute-done.3.far_ref = bf16[144,512]{1,0:T(8,128)(2,1)S(1)} collective-permute-done((bf16[144,512]{1,0:T(8,128)(2,1)S(1)}, bf16[144,512]{1,0:T(8,128)(2,1)S(1)}, u32[]{:S(2)}, u32[]{:S(2)}) %collective-permute-start.3) | collective-permute-done | bytes 147488 | tf_op jit(solution)/shard_map/ppermute | solution.py:24
  69.8 3.4 %within.3.within_ref = f32[512,1024]{1,0:T(8,128)S(1)} custom-call(bf16[512,1024]{1,0:T(8,128)(2,1)S(1)} %copy-done.15, bf16[512,256]{1,0:T(8,128)(2,1)S(1)} %copy-done.19, f32[512,16]{1,0:T(8,128)S(1)} %copy.25.step_ref, s32[512,16]{1,0:T(8,128)S(1)} %bitcast.51, f32[1,16]{1,0:T(1,128)S(1)} %slice.108.rate_ref, f32[1,16]{1,0:T(1,128)S(1)} %slice.109.skip_ref), custom_call_target="tpu_custom_call" | custom-call | flops 2147483648 | bytes 4194304 | tf_op jit(solution)/shard_map/within/pallas_call | solution.py:363
  74.3 3.4 %shard_map.180 = (bf16[512,1024]{1,0:T(8,128)(2,1)S(1)}, f32[1,512]{1,0:T(1,128)S(1)}) custom-call(s32[1]{0:T(128)} %bitcast.y_ref, f32[128,1024]{1,0:T(8,128)S(1)} %get-tuple-element.46.early_ref, f32[1,1024]{1,0:T(1,128)S(1)} %get-tuple-element.47.early_decay_ref, bf16[128,512]{1,0:T(8,128)(2,1)S(1)} %shard_map.179.own_ref, ...), custom_call_target="tpu_custom_call" | custom-call | flops 268435456 | bytes 5679172 | tf_op jit(solution)/shard_map/pallas_call | solution.py:326
  79.7 6.0 %collective-permute-done.11 = bf16[1024,512]{1,0:T(8,128)(2,1)} collective-permute-done((bf16[1024,512]{1,0:T(8,128)(2,1)}, bf16[1024,512]{1,0:T(8,128)(2,1)}, u32[]{:S(2)}, u32[]{:S(2)}) %collective-permute-start.11) | collective-permute-done | bytes 1048608 | tf_op jit(solution)/shard_map/ppermute | solution.py:24
  87.8 12.2 %collective-permute-done.5.far_ref = bf16[512,1024]{1,0:T(8,128)(2,1)S(1)} collective-permute-done((bf16[512,1024]{1,0:T(8,128)(2,1)S(1)}, bf16[512,1024]{1,0:T(8,128)(2,1)S(1)}, u32[]{:S(2)}, u32[]{:S(2)}) %collective-permute-start.5) | collective-permute-done | bytes 1048608 | tf_op jit(solution)/shard_map/ppermute | solution.py:29
  103.4 7.9 %out.1 = (bf16[2,1024,512]{2,1,0:T(8,128)(2,1)S(1)}, f32[2,1024,512]{2,1,0:T(8,128)S(1)}) custom-call(s32[9]{0:T(128)S(1)} %stack.128.where_ref, bf16[512,1024]{1,0:T(8,128)(2,1)S(1)} %copy-done.28, bf16[512,1024]{1,0:T(8,128)(2,1)S(1)} %copy-done.30, bf16[1024,512]{1,0:T(8,128)(2,1)S(1)} %copy-done.26, bf16[1024,512]{1,0:T(8,128)(2,1)S(1)} %get-tuple-element.97.refs_1_, ...), custom_call_target="tpu_custom_call" | custom-call | flops 4294967296 | bytes 6291456 | tf_op jit(solution)/shard_map/out/pallas_call | solution.py:488
  117.6 3.3 %fusion.5 = bf16[1024,512]{1,0:T(8,128)(2,1)} fusion(f32[2,1024,512]{2,1,0:T(8,128)} %copy-done.9, bf16[2,1024,512]{2,1,0:T(8,128)(2,1)} %collective-permute-done.12), kind=kLoop, calls=%fused_computation.15 | loop fusion | flops 1572864 | bytes 4194304 | tf_op jit(solution)/shard_map/convert_element_type | solution.py:665
  126.3 20.1 %collective-permute-done.15 = f32[1,512]{1,0:T(1,128)S(1)} collective-permute-done((f32[1,512]{1,0:T(1,128)S(1)}, f32[1,512]{1,0:T(1,128)S(1)}, u32[]{:S(2)}, u32[]{:S(2)}) %collective-permute-start.15) | collective-permute-done | bytes 2080 | tf_op jit(solution)/shard_map/ppermute | solution.py:29
  158.1 18.8 %collective-permute-done.21 = bf16[1024,512]{1,0:T(8,128)(2,1)S(1)} collective-permute-done((bf16[1024,512]{1,0:T(8,128)(2,1)S(1)}, bf16[1024,512]{1,0:T(8,128)(2,1)S(1)}, u32[]{:S(2)}, u32[]{:S(2)}) %collective-permute-start.21) | collective-permute-done | bytes 1048608 | tf_op jit(solution)/shard_map/ppermute | solution.py:29
  180.3 3.6 %collective-permute-done.25 = bf16[560,1024]{1,0:T(8,128)(2,1)} collective-permute-done((bf16[560,1024]{1,0:T(8,128)(2,1)S(1)}, bf16[560,1024]{1,0:T(8,128)(2,1)}, u32[]{:S(2)}, u32[]{:S(2)}) %collective-permute-start.25) | collective-permute-done | bytes 1146912 | tf_op jit(solution)/shard_map/ppermute | solution.py:24
  188.5 22.3 %collective-permute-done.18 = bf16[16,512]{1,0:T(8,128)(2,1)S(1)} collective-permute-done((bf16[16,512]{1,0:T(8,128)(2,1)S(1)}, bf16[16,512]{1,0:T(8,128)(2,1)S(1)}, u32[]{:S(2)}, u32[]{:S(2)}) %collective-permute-start.18) | collective-permute-done | bytes 16416 | tf_op jit(solution)/shard_map/ppermute | solution.py:24
  221.0 3.6 %shard_map.183 = bf16[528,592]{1,0:T(8,128)(2,1)} custom-call(s32[5]{0:T(128)S(1)} %stack.144.where_ref, bf16[4,1040,512]{2,1,0:T(8,128)(2,1)S(1)} %maximum_maximum_fusion.hidden_ref, bf16[560,1024]{1,0:T(8,128)(2,1)S(1)} %maximum_maximum_fusion.1.refs_0_, bf16[560,1024]{1,0:T(8,128)(2,1)S(1)} %get-tuple-element.93.refs_1_, ...), custom_call_target="tpu_custom_call" | custom-call | flops 1280311296 | bytes 6684672 | tf_op jit(solution)/shard_map/pallas_call | solution.py:505
  227.9 14.3 %collective-permute-done.32 = f32[1024]{0:T(1024)S(1)} collective-permute-done((f32[1024]{0:T(1024)S(1)}, f32[1024]{0:T(1024)S(1)}, u32[]{:S(2)}, u32[]{:S(2)}) %collective-permute-start.32) | collective-permute-done | bytes 4128 | tf_op jit(solution)/shard_map/ppermute | solution.py:29
  243.7 4.1 %collective-permute-done.33 = f32[16]{0:T(128)S(1)} collective-permute-done((f32[16]{0:T(128)S(1)}, f32[16]{0:T(128)S(1)}, u32[]{:S(2)}, u32[]{:S(2)}) %collective-permute-start.33) | collective-permute-done | bytes 96 | tf_op jit(solution)/shard_map/ppermute | solution.py:24
  258.3 3.2 shard_map.184
  264.7 4.3 %collective-permute-done.34 = bf16[512,64]{1,0:T(8,128)(2,1)} collective-permute-done((bf16[512,64]{1,0:T(8,128)(2,1)}, bf16[512,64]{1,0:T(8,128)(2,1)}, u32[]{:S(2)}, u32[]{:S(2)}) %collective-permute-start.34) | collective-permute-done | bytes 65568 | tf_op jit(solution)/shard_map/ppermute | solution.py:29
  305.3 8.5 %collective-permute-done.38.far_ref = bf16[144,512]{1,0:T(8,128)(2,1)S(1)} collective-permute-done((bf16[144,512]{1,0:T(8,128)(2,1)S(1)}, bf16[144,512]{1,0:T(8,128)(2,1)S(1)}, u32[]{:S(2)}, u32[]{:S(2)}) %collective-permute-start.38) | collective-permute-done | bytes 147488 | tf_op jit(solution)/shard_map/ppermute | solution.py:24
  318.2 5.7 %psum.7 = f32[512]{0:T(512)S(1)} all-reduce(f32[512]{0:T(512)S(1)} %bitcast.65), channel_id=1, replica_groups=mesh['seq'=8,'head'=4] {'head'}, use_global_device_ids=true, to_apply=%region_1.2 | all-reduce | flops 512 | bytes 4096 | tf_op jit(solution)/shard_map/psum | solution.py:778
  (240 shorter events, 128.3 us)
Async XLA Ops:
  0.6 25.2 %collective-permute-start.7 = (bf16[1024,512]{1,0:T(8,128)(2,1)}, bf16[1024,512]{1,0:T(8,128)(2,1)}, u32[]{:S(2)}, u32[]{:S(2)}) collective-permute-start(bf16[1024,512]{1,0:T(8,128)(2,1)} %refs_0_.1), channel_id=1, source_target_pairs={{8,0},{12,4},{16,8},{20,12},{24,16},{28,20},{9,1},{13,5},{17,9},{2... | collective-permute-start | bytes 3145736 | tf_op jit(solution)/shard_map/ppermute | solution.py:24
  4.1 26.8 %collective-permute-start.6 = (bf16[1024,512]{1,0:T(8,128)(2,1)}, bf16[1024,512]{1,0:T(8,128)(2,1)}, u32[]{:S(2)}, u32[]{:S(2)}) collective-permute-start(bf16[1024,512]{1,0:T(8,128)(2,1)} %refs_0_.1), channel_id=1, source_target_pairs={{0,8},{4,12},{8,16},{12,20},{16,24},{20,28},{1,9},{5,13},{9,17},{1... | collective-permute-start | bytes 3145736 | tf_op jit(solution)/shard_map/ppermute | solution.py:24
  25.9 25.1 %collective-permute-start.9 = (bf16[1024,512]{1,0:T(8,128)(2,1)}, bf16[1024,512]{1,0:T(8,128)(2,1)}, u32[]{:S(2)}, u32[]{:S(2)}) collective-permute-start(bf16[1024,512]{1,0:T(8,128)(2,1)} %collective-permute-done.7), channel_id=1, source_target_pairs={{8,0},{12,4},{16,8},{20,12},{9,1},{13,5},{17,9},{21,13},{10,2},{14... | collective-permute-start | bytes 3145736 | tf_op jit(solution)/shard_map/ppermute | solution.py:24
  30.9 27.5 %collective-permute-start.8 = (bf16[1024,512]{1,0:T(8,128)(2,1)}, bf16[1024,512]{1,0:T(8,128)(2,1)}, u32[]{:S(2)}, u32[]{:S(2)}) collective-permute-start(bf16[1024,512]{1,0:T(8,128)(2,1)} %collective-permute-done.6), channel_id=1, source_target_pairs={{8,16},{12,20},{16,24},{20,28},{9,17},{13,21},{17,25},{21,29},{10,... | collective-permute-start | bytes 3145736 | tf_op jit(solution)/shard_map/ppermute | solution.py:24
  51.0 28.7 %collective-permute-start.10 = (bf16[1024,512]{1,0:T(8,128)(2,1)}, bf16[1024,512]{1,0:T(8,128)(2,1)}, u32[]{:S(2)}, u32[]{:S(2)}) collective-permute-start(bf16[1024,512]{1,0:T(8,128)(2,1)} %collective-permute-done.9), channel_id=1, source_target_pairs={{8,0},{12,4},{9,1},{13,5},{10,2},{14,6},{11,3},{15,7}} | collective-permute-start | bytes 3145736 | tf_op jit(solution)/shard_map/ppermute | solution.py:24
  58.5 27.2 %collective-permute-start.11 = (bf16[1024,512]{1,0:T(8,128)(2,1)}, bf16[1024,512]{1,0:T(8,128)(2,1)}, u32[]{:S(2)}, u32[]{:S(2)}) collective-permute-start(bf16[1024,512]{1,0:T(8,128)(2,1)} %collective-permute-done.8), channel_id=1, source_target_pairs={{16,24},{20,28},{17,25},{21,29},{18,26},{22,30},{19,27},{23,31}} | collective-permute-start | bytes 3145736 | tf_op jit(solution)/shard_map/ppermute | solution.py:24
  77.7 22.3 %collective-permute-start.5 = (bf16[512,1024]{1,0:T(8,128)(2,1)S(1)}, bf16[512,1024]{1,0:T(8,128)(2,1)S(1)}, u32[]{:S(2)}, u32[]{:S(2)}) collective-permute-start(bf16[512,1024]{1,0:T(8,128)(2,1)S(1)} %get-tuple-element.54.own_ref), channel_id=1, source_target_pairs={{0,4},{4,0},{8,12},{12,8},{16,20},{20,16},{24,28},{28,24},{1,5},{5... | collective-permute-start | bytes 3145736 | tf_op jit(solution)/shard_map/ppermute | solution.py:29
  115.2 32.2 %collective-permute-start = (bf16[512,512]{1,0:T(8,128)(2,1)}, bf16[512,512]{1,0:T(8,128)(2,1)}, u32[]{:S(2)}, u32[]{:S(2)}) collective-permute-start(bf16[512,512]{1,0:T(8,128)(2,1)} %constant_dynamic-slice_fusion.5), channel_id=1, source_target_pairs={{0,4},{4,0},{8,12},{12,8},{16,20},{20,16},{24,28},{28,24},{1,5},{5... | collective-permute-start | bytes 1572872 | tf_op jit(solution)/shard_map/ppermute | solution.py:29
  120.9 29.2 %collective-permute-start.13 = (bf16[1024,512]{1,0:T(8,128)(2,1)}, bf16[1024,512]{1,0:T(8,128)(2,1)}, u32[]{:S(2)}, u32[]{:S(2)}) collective-permute-start(bf16[1024,512]{1,0:T(8,128)(2,1)} %fusion.5), channel_id=1, source_target_pairs={{0,2},{1,3},{2,0},{3,1},{4,6},{5,7},{6,4},{7,5},{8,10},{9,11},{10,... | collective-permute-start | bytes 3145736 | tf_op jit(solution)/shard_map/ppermute | solution.py:29
  122.6 32.3 %collective-permute-start.24 = (bf16[560,1024]{1,0:T(8,128)(2,1)S(1)}, bf16[560,1024]{1,0:T(8,128)(2,1)S(1)}, u32[]{:S(2)}, u32[]{:S(2)}) collective-permute-start(bf16[560,1024]{1,0:T(8,128)(2,1)S(1)} %maximum_maximum_fusion.1.refs_0_), channel_id=1, source_target_pairs={{8,0},{12,4},{16,8},{20,12},{24,16},{28,20},{9,1},{13,5},{17,9},{2... | collective-permute-start | bytes 3440648 | tf_op jit(solution)/shard_map/ppermute | solution.py:24
  124.3 32.2 %collective-permute-start.23 = (bf16[560,1024]{1,0:T(8,128)(2,1)S(1)}, bf16[560,1024]{1,0:T(8,128)(2,1)S(1)}, u32[]{:S(2)}, u32[]{:S(2)}) collective-permute-start(bf16[560,1024]{1,0:T(8,128)(2,1)S(1)} %maximum_maximum_fusion.1.refs_0_), channel_id=1, source_target_pairs={{0,8},{4,12},{8,16},{12,20},{16,24},{20,28},{1,9},{5,13},{9,17},{1... | collective-permute-start | bytes 3440648 | tf_op jit(solution)/shard_map/ppermute | solution.py:24
  125.7 20.7 %collective-permute-start.15 = (f32[1,512]{1,0:T(1,128)S(1)}, f32[1,512]{1,0:T(1,128)S(1)}, u32[]{:S(2)}, u32[]{:S(2)}) collective-permute-start(f32[1,512]{1,0:T(1,128)S(1)} %add.151), channel_id=1, source_target_pairs={{0,2},{1,3},{2,0},{3,1},{4,6},{5,7},{6,4},{7,5},{8,10},{9,11},{10,... | collective-permute-start | bytes 6152 | tf_op jit(solution)/shard_map/ppermute | solution.py:29
  153.3 23.6 %collective-permute-start.21 = (bf16[1024,512]{1,0:T(8,128)(2,1)S(1)}, bf16[1024,512]{1,0:T(8,128)(2,1)S(1)}, u32[]{:S(2)}, u32[]{:S(2)}) collective-permute-start(bf16[1024,512]{1,0:T(8,128)(2,1)S(1)} %fusion), channel_id=1, source_target_pairs={{0,2},{1,3},{2,0},{3,1},{4,6},{5,7},{6,4},{7,5},{8,10},{9,11},{10,... | collective-permute-start | bytes 3145736 | tf_op jit(solution)/shard_map/ppermute | solution.py:29
  154.9 23.8 %collective-permute-start.26 = (bf16[560,1024]{1,0:T(8,128)(2,1)S(1)}, bf16[560,1024]{1,0:T(8,128)(2,1)}, u32[]{:S(2)}, u32[]{:S(2)}) collective-permute-start(bf16[560,1024]{1,0:T(8,128)(2,1)S(1)} %collective-permute-done.24), channel_id=1, source_target_pairs={{8,0},{12,4},{16,8},{20,12},{9,1},{13,5},{17,9},{21,13},{10,2},{14... | collective-permute-start | bytes 3440648 | tf_op jit(solution)/shard_map/ppermute | solution.py:24
  156.6 27.3 %collective-permute-start.25 = (bf16[560,1024]{1,0:T(8,128)(2,1)S(1)}, bf16[560,1024]{1,0:T(8,128)(2,1)}, u32[]{:S(2)}, u32[]{:S(2)}) collective-permute-start(bf16[560,1024]{1,0:T(8,128)(2,1)S(1)} %collective-permute-done.23), channel_id=1, source_target_pairs={{8,16},{12,20},{16,24},{20,28},{9,17},{13,21},{17,25},{21,29},{10,... | collective-permute-start | bytes 3440648 | tf_op jit(solution)/shard_map/ppermute | solution.py:24
  178.6 39.4 %collective-permute-start.22 = (bf16[2,1024,512]{2,1,0:T(8,128)(2,1)}, bf16[2,1024,512]{2,1,0:T(8,128)(2,1)}, u32[]{:S(2)}, u32[]{:S(2)}) collective-permute-start(bf16[2,1024,512]{2,1,0:T(8,128)(2,1)} %pad_maximum_fusion), channel_id=1, source_target_pairs={{0,1},{1,0},{2,3},{3,2},{4,5},{5,4},{6,7},{7,6},{8,9},{9,8},{10,11... | collective-permute-start | bytes 6291464 | tf_op jit(solution)/shard_map/ppermute | solution.py:29
  178.6 35.9 %collective-permute-start.27 = (bf16[560,1024]{1,0:T(8,128)(2,1)}, bf16[560,1024]{1,0:T(8,128)(2,1)}, u32[]{:S(2)}, u32[]{:S(2)}) collective-permute-start(bf16[560,1024]{1,0:T(8,128)(2,1)} %collective-permute-done.26), channel_id=1, source_target_pairs={{8,0},{12,4},{9,1},{13,5},{10,2},{14,6},{11,3},{15,7}} | collective-permute-start | bytes 3440648 | tf_op jit(solution)/shard_map/ppermute | solution.py:24
  183.9 30.7 %collective-permute-start.28 = (bf16[560,1024]{1,0:T(8,128)(2,1)}, bf16[560,1024]{1,0:T(8,128)(2,1)}, u32[]{:S(2)}, u32[]{:S(2)}) collective-permute-start(bf16[560,1024]{1,0:T(8,128)(2,1)} %collective-permute-done.25), channel_id=1, source_target_pairs={{16,24},{20,28},{17,25},{21,29},{18,26},{22,30},{19,27},{23,31}} | collective-permute-start | bytes 3440648 | tf_op jit(solution)/shard_map/ppermute | solution.py:24
  186.0 24.8 %collective-permute-start.18 = (bf16[16,512]{1,0:T(8,128)(2,1)S(1)}, bf16[16,512]{1,0:T(8,128)(2,1)S(1)}, u32[]{:S(2)}, u32[]{:S(2)}) collective-permute-start(bf16[16,512]{1,0:T(8,128)(2,1)S(1)} %slice.136), channel_id=1, source_target_pairs={{0,8},{4,12},{8,16},{12,20},{16,24},{20,28},{1,9},{5,13},{9,17},{1... | collective-permute-start | bytes 49160 | tf_op jit(solution)/shard_map/ppermute | solution.py:24
  224.6 33.7 %collective-permute-start.29 = (bf16[528,592]{1,0:T(8,128)(2,1)}, bf16[528,592]{1,0:T(8,128)(2,1)}, u32[]{:S(2)}, u32[]{:S(2)}) collective-permute-start(bf16[528,592]{1,0:T(8,128)(2,1)} %shard_map.183), channel_id=1, source_target_pairs={{0,4},{4,0},{8,12},{12,8},{16,20},{20,16},{24,28},{28,24},{1,5},{5... | collective-permute-start | bytes 1875464 | tf_op jit(solution)/shard_map/ppermute | solution.py:29
  226.9 15.4 %collective-permute-start.32 = (f32[1024]{0:T(1024)S(1)}, f32[1024]{0:T(1024)S(1)}, u32[]{:S(2)}, u32[]{:S(2)}) collective-permute-start(f32[1024]{0:T(1024)S(1)} %add.160), channel_id=1, source_target_pairs={{0,4},{4,0},{8,12},{12,8},{16,20},{20,16},{24,28},{28,24},{1,5},{5... | collective-permute-start | bytes 12296 | tf_op jit(solution)/shard_map/ppermute | solution.py:29
  254.5 22.4 %collective-permute-start.39 = (bf16[528,512]{1,0:T(8,128)(2,1)}, bf16[528,512]{1,0:T(8,128)(2,1)}, u32[]{:S(2)}, u32[]{:S(2)}) collective-permute-start(bf16[528,512]{1,0:T(8,128)(2,1)} %shard_map.190), channel_id=1, source_target_pairs={{0,4},{4,0},{8,12},{12,8},{16,20},{20,16},{24,28},{28,24},{1,5},{5... | collective-permute-start | bytes 1622024 | tf_op jit(solution)/shard_map/ppermute | solution.py:29
  271.4 17.4 %collective-permute-start.17 = (bf16[512,512]{1,0:T(8,128)(2,1)S(1)}, bf16[512,512]{1,0:T(8,128)(2,1)S(1)}, u32[]{:S(2)}, u32[]{:S(2)}) collective-permute-start(bf16[512,512]{1,0:T(8,128)(2,1)S(1)} %get-tuple-element.94), channel_id=1, source_target_pairs={{0,4},{4,0},{8,12},{12,8},{16,20},{20,16},{24,28},{28,24},{1,5},{5... | collective-permute-start | bytes 1572872 | tf_op jit(solution)/shard_map/ppermute | solution.py:29
  298.2 15.6 %collective-permute-start.38 = (bf16[144,512]{1,0:T(8,128)(2,1)S(1)}, bf16[144,512]{1,0:T(8,128)(2,1)S(1)}, u32[]{:S(2)}, u32[]{:S(2)}) collective-permute-start(bf16[144,512]{1,0:T(8,128)(2,1)S(1)} %get-tuple-element.69), channel_id=1, source_target_pairs={{0,16},{4,20},{8,24},{12,28},{1,17},{5,21},{9,25},{13,29},{2,18},{... | collective-permute-start | bytes 442376 | tf_op jit(solution)/shard_map/ppermute | solution.py:24
  (65 other events, 618.3 us)
